TPU v7x, 256 devices: a whole 4x4x8 slice. The times are simulated.
256 devices in a mesh: dp: 8 (over y, core), cls: 32 (over z, x).
Axes of the slice: x: 4, y: 4, z: 8, core: 2. Of those that a mesh axis runs over, the one named last changes fastest.
Arguments:
- embeddings: bfloat16 [262144, 512], P(('dp', 'cls'))
- proxies: bfloat16 [98304, 512], P('cls')
- hard_tiles: int32 [2048, 8], P(('dp', 'cls')), may hold values from 0 to 767, as said below
- tile_count: int32 [2048], P(('dp', 'cls')), may hold values from 5 to 8
- labels: int32 [262144], P(('dp', 'cls')), may hold values from 0 to 98303, as said below
Outputs:
- row_loss: float32 [262144], P(('dp', 'cls'))
- embed_grad: bfloat16 [262144, 512], P(('dp', 'cls'))
- proxy_grad: float32 [98304, 512], P('cls', 'dp')
Inputs may be any that keep to these rules, and one draw needn't show every extreme that they name: `hard_tiles`: tile t is stored on class shard t // 24. Among the 8 x 8 list entries of one device's blocks (all entries, used or not), every one of the class shards is named exactly 2 times; the entries of one block name different tiles. Only the first tile_count entries of a block's list are used. `labels`: A row's positive class lies in the first tile of its block's list.
All inputs are finite; a program needn't handle non-finite values.
Results may differ from a plain program's by a relative error of at most 0.0098.
Values may be sent and summed in bfloat16 or wider, within the bound.
A program may use at most 128 MiB of HBM per device.

v0:
```python
import jax
import jax.numpy as jnp
from jax import lax
from jax.sharding import PartitionSpec as P

D = 512
TILE = 128
BR = 128
K = 8


logit_scale = 4.0
epsilon = 1e-06


def per_device(embeddings, proxies, hard_tiles, tile_count, labels):
    blocks = hard_tiles.shape[0]
    pair_count = blocks * K
    groups = lax.axis_size("cls")
    capacity = pair_count // groups
    tile_dev = proxies.shape[0] // TILE
    flat_tiles = hard_tiles.reshape(pair_count)
    owners = flat_tiles // tile_dev
    local_ids = flat_tiles % tile_dev
    counter = jnp.arange(pair_count, dtype=jnp.int32)
    same_owner = owners[:, None] == owners[None, :]
    earlier = counter[None, :] < counter[:, None]
    rank_order = jnp.sum(jnp.where(same_owner & earlier, 1, 0), axis=1).astype(jnp.int32)
    slot_of = owners * capacity + rank_order
    holder = jnp.sum(jnp.where(slot_of[None, :] == counter[:, None], counter[None, :], 0), axis=1)
    request_ids = local_ids[holder].reshape(groups, capacity)
    emb_exact = embeddings.astype(jnp.float32)
    inverse_norm = lax.rsqrt(jnp.sum(emb_exact * emb_exact, axis=1, keepdims=True) + epsilon)
    unit_exact = emb_exact * inverse_norm
    unit_rows = unit_exact.astype(jnp.bfloat16)
    unit_blocks = unit_rows.reshape(blocks, BR, D)
    entries = jnp.arange(K, dtype=jnp.int32)
    columns = jnp.arange(TILE, dtype=jnp.int32)
    valid_entry = entries[None, :] < tile_count[:, None]
    pos_cols = labels.reshape(blocks, BR) - hard_tiles[:, 0:1] * TILE
    tile_table = proxies.reshape(tile_dev, TILE, D)
    wanted = lax.all_to_all(request_ids, "cls", split_axis=0, concat_axis=0, tiled=True)
    outgoing = tile_table[wanted]
    fetched = lax.all_to_all(outgoing, "cls", split_axis=0, concat_axis=0, tiled=True)
    candidates = fetched.reshape(pair_count, TILE, D)[slot_of].reshape(blocks, K, TILE, D)
    logits = logit_scale * jnp.einsum(
        "brd,bkcd->brkc", unit_blocks, candidates, preferred_element_type=jnp.float32
    )
    masked = jnp.where(valid_entry[:, None, :, None], logits, -1e30)
    peak_row = jnp.max(masked, axis=(2, 3))
    total_row = jnp.sum(jnp.exp(masked - peak_row[:, :, None, None]), axis=(2, 3))
    log_total = peak_row + jnp.log(total_row)
    positive_hit = (
        (entries == 0)[None, None, :, None]
        & (columns[None, None, None, :] == pos_cols[:, :, None, None])
    ).astype(jnp.float32)
    positive = jnp.sum(logits * positive_hit, axis=(2, 3))
    probabilities = jnp.exp(masked - log_total[:, :, None, None])
    dscore = (logit_scale * (probabilities - positive_hit)).astype(jnp.bfloat16)
    tile_terms = jnp.einsum(
        "brkc,bkcd->brkd", dscore, candidates, preferred_element_type=jnp.float32
    ).astype(jnp.bfloat16)
    tile_terms = lax.optimization_barrier(tile_terms)
    grad_unit = jnp.sum(tile_terms.astype(jnp.float32), axis=2)
    pair_grads = jnp.einsum(
        "brkc,brd->bkcd", dscore, unit_blocks, preferred_element_type=jnp.float32
    )
    pair_grads = pair_grads.reshape(pair_count, TILE, D)[holder].reshape(groups, capacity, TILE, D)
    returned = lax.all_to_all(pair_grads, "cls", split_axis=0, concat_axis=0, tiled=True)
    got_ids = wanted.reshape(pair_count)
    got_terms = returned.reshape(pair_count, TILE * D)
    row_loss = (log_total - positive).reshape(-1)
    grad_flat = grad_unit.reshape(-1, D)
    radial = jnp.sum(unit_exact * grad_flat, axis=1, keepdims=True)
    embed_grad = ((grad_flat - unit_exact * radial) * inverse_norm).astype(jnp.bfloat16)
    select_rows = (jnp.arange(tile_dev, dtype=jnp.int32)[:, None] == got_ids[None, :]).astype(
        jnp.float32
    )
    owned = jnp.dot(
        select_rows, got_terms, precision=lax.Precision.HIGHEST, preferred_element_type=jnp.float32
    )
    owned = owned.reshape(tile_dev * TILE, D)
    proxy_share = lax.psum_scatter(owned, "dp", scatter_dimension=1, tiled=True)
    return (row_loss, embed_grad, proxy_share)


def solution(mesh):
    placed = (
        P(("dp", "cls"), None),
        P("cls", None),
        P(("dp", "cls"), None),
        P(("dp", "cls")),
        P(("dp", "cls")),
    )
    return jax.shard_map(
        per_device,
        mesh=mesh,
        in_specs=placed,
        out_specs=(P(("dp", "cls")), P(("dp", "cls"), None), P("cls", "dp")),
        check_vma=False,
    )
```

profile of v0, /device:TPU:1, one launch (start us, length us, event | category | flops | bytes accessed | tf_op | source)
XLA Modules:
  0.0 764.0 jit_solution(4350352955673623369)
XLA Ops:
  7.2 0.9 compare_and_fusion
  8.0 0.8 broadcast_divide_fusion
  9.1 0.2 select_reduce_fusion.1
  9.4 0.8 gather_fusion
  10.3 20.2 %all_to_all.22 = s32[32,1,2]{2,1,0:T(1,128)S(1)} all-to-all(s32[32,1,2]{2,1,0:T(1,128)S(1)} %bitcast.52), channel_id=1, replica_groups=mesh['dp'=8,'cls'=32] {'cls'}, dimensions={0} | all-to-all | bytes 512 | tf_op jit(solution)/shard_map/all_to_all | solution.py:42
  30.9 5.5 gather_fusion.1
  36.4 5.3 all-to-all-start.1
  41.9 0.1 multiply_reduce_fusion
  42.0 0.3 fusion.12
  42.5 0.3 fusion.7
  42.8 187.7 %all-to-all-done.1 = bf16[32,2,128,512]{3,2,1,0:T(8,128)(2,1)} async-done(((bf16[32,2,128,512]{3,2,1,0:T(8,128)(2,1)}), bf16[32,2,128,512]{3,2,1,0:T(8,128)(2,1)}, u32[]{:S(2)}, u32[]{:S(2)}) %all-to-all-start.1) | async-done | bytes 8388640 | tf_op jit(solution)/shard_map/all_to_all | solution.py:44
  230.6 8.9 %gather_fusion.2 = bf16[64,128,512]{2,1,0:T(8,128)(2,1)} fusion(bf16[64,128,512]{2,1,0:T(8,128)(2,1)} %bitcast.9, s32[1024]{0:T(1024)S(1)} %pad_clamp_fusion), kind=kCustom, calls=%fused_computation.2 | custom fusion | bytes 16777472 | tf_op jit(solution)/shard_map/gather | solution.py:45
  239.4 5.7 fusion.4
  245.2 1.7 fusion
  246.9 0.6 subtract_bitcast_fusion
  247.5 8.1 %fusion.20 = f32[8,8,128,512]{3,2,1,0:T(8,128)} fusion(bf16[8,128,512,1]{2,1,3,0:T(8,128)(2,1)S(1)} %bitcast.51, f32[8,128,8,128]{1,3,2,0:T(8,128)S(1)} %get-tuple-element.14, f32[8,128]{1,0:T(8,128)S(1)} %get-tuple-element.6, pred[8,128,128]{1,2,0:T(8,128)(4,1)S(1)} %iota_compare_fusion, pred[8,8]{1,0:T(8,128)(4,1)S(1)} %iota_compare_fusion.5, ...), kind=kOutput, calls=%fused_computation.59 | convolution fusion | flops 1082130432 | bytes 22155336 | tf_op jit(solution)/shard_map/brkc,brd->bkcd/dot_general | solution.py:65
  255.6 14.6 %gather_fusion.3 = f32[64,128,512]{2,1,0:T(8,128)} fusion(f32[64,128,512]{2,1,0:T(8,128)} %bitcast.44, s32[1024]{0:T(1024)S(1)} %pad_clamp_fusion.2), kind=kCustom, calls=%fused_computation.3 | custom fusion | bytes 33554688 | tf_op jit(solution)/shard_map/gather | solution.py:68
  270.2 6.4 all-to-all-start.2
  276.7 0.3 reduce-scatter.2.cloned.1.call-start
  276.9 0.5 broadcast.256
  277.4 0.7 reduce.5
  278.2 385.9 %all-to-all-done.2 = f32[32,2,128,512]{3,2,1,0:T(8,128)} async-done(((f32[32,2,128,512]{3,2,1,0:T(8,128)}), f32[32,2,128,512]{3,2,1,0:T(8,128)}, u32[]{:S(2)}, u32[]{:S(2)}) %all-to-all-start.2) | async-done | bytes 16777248 | tf_op jit(solution)/shard_map/all_to_all | solution.py:69
  664.1 15.2 %copy.41 = f32[8,8,128,512]{3,1,2,0:T(8,128)S(1)} copy(f32[8,8,128,512]{3,2,1,0:T(8,128)} %bitcast.23) | data formatting | bytes 33554432
  679.3 7.7 %fusion.14 = f32[24,65536]{1,0:T(8,128)} fusion(f32[64,65536]{1,0:T(8,128)S(1)} %bitcast.46, s32[64]{0:T(128)S(1)} %eq.76), kind=kOutput, calls=%fused_computation.32 | convolution fusion | flops 1207961088 | bytes 23068928 | tf_op jit(solution)/shard_map/dot_general | solution.py:79
  687.0 6.8 reshape.281
  693.8 6.6 copy.37
  700.4 8.6 %convert_bitcast_fusion = bf16[8,128,8,512]{1,3,2,0:T(8,128)(2,1)S(1)} fusion(bf16[8,8,128,512]{3,2,1,0:T(8,128)(2,1)} %bitcast.48, f32[8,128,8,128]{1,3,2,0:T(8,128)} %copy-done.2, f32[8,128]{1,0:T(8,128)S(1)} %get-tuple-element.6, pred[8,128,128]{1,2,0:T(8,128)(4,1)S(1)} %iota_compare_fusion, pred[8,8]{1,0:T(8,128)(4,1)S(1)} %iota_compare_fusion.5, ...), kind=kOutput, calls=%fused_computation.5 | convolution fusion | flops 1086324736 | bytes 21106760 | tf_op jit(solution)/shard_map/brkc,bkcd->brkd/dot_general | solution.py:60
  709.0 2.7 convert_reduce_fusion
  711.8 3.1 copy.36
  714.9 2.5 fusion.8
  717.4 2.6 fusion.11
  720.1 37.0 %reduce-scatter.2.cloned.1.call-done = f32[3072,64]{0,1:T(8,128)} async-done(((f32[3072,512]{0,1:T(8,128)}), f32[3072,64]{0,1:T(8,128)}) %reduce-scatter.2.cloned.1.call-update) | async-done | bytes 786448 | tf_op jit(solution)/shard_map/reduce_scatter | solution.py:83
  (41 shorter events, 1.3 us)
Async XLA Ops:
  7.2 23.7 %copy-start = (bf16[3072,512]{1,0:T(8,128)(2,1)S(1)}, bf16[3072,512]{1,0:T(8,128)(2,1)}, u32[]{:S(2)}) copy-start(bf16[3072,512]{1,0:T(8,128)(2,1)} %param.6) | copy-start | bytes 9437188
  36.4 5.5 copy-start.5
  36.4 5.6 copy-start.4
  36.4 5.9 copy-start.7
  36.4 6.0 copy-start.6
  36.4 194.2 %all-to-all-start.1 = ((bf16[32,2,128,512]{3,2,1,0:T(8,128)(2,1)}), bf16[32,2,128,512]{3,2,1,0:T(8,128)(2,1)}, u32[]{:S(2)}, u32[]{:S(2)}) async-start(bf16[32,2,128,512]{3,2,1,0:T(8,128)(2,1)} %bitcast.49), calls=%async_computation.1 | async-start | bytes 16777216 | tf_op jit(solution)/shard_map/all_to_all | solution.py:44
  245.2 10.4 %copy-start.2 = (f32[8,128,8,128]{1,3,2,0:T(8,128)}, f32[8,128,8,128]{1,3,2,0:T(8,128)S(1)}, u32[]{:S(2)}) copy-start(f32[8,128,8,128]{1,3,2,0:T(8,128)S(1)} %get-tuple-element.14) | copy-start | bytes 12582916
  270.2 393.9 %all-to-all-start.2 = ((f32[32,2,128,512]{3,2,1,0:T(8,128)}), f32[32,2,128,512]{3,2,1,0:T(8,128)}, u32[]{:S(2)}, u32[]{:S(2)}) async-start(f32[32,2,128,512]{3,2,1,0:T(8,128)} %bitcast.45), calls=%async_computation.2 | async-start | bytes 33554432 | tf_op jit(solution)/shard_map/all_to_all | solution.py:69
  276.7 480.5 %reduce-scatter.2.cloned.1.call-start = ((), (), s32[]{:S(2)}) async-start(), calls=%async_computation.4 | async-start | bytes 7077888 | tf_op jit(solution)/shard_map/reduce_scatter | solution.py:83
  711.8 45.4 %copy-start.1 = (bf16[3072,512]{1,0:T(8,128)(2,1)S(1)}, bf16[3072,512]{1,0:T(8,128)(2,1)}, u32[]{:S(2)}) copy-start(bf16[3072,512]{1,0:T(8,128)(2,1)} %param.6) | copy-start | bytes 9437188
  714.9 2.5 copy-start.3
Sparse Core Ops, SparseCore 0:
  700.5 56.5 reduce-scatter.1
where the time goes:
time: 765 us; the launch traced here: 764 us
  waiting for transfers between devices  611 us (80%)
  local copies, waits for them, and re-layouts  62.9 us (8%)
  matrix products  30.1 us (4%)
  blocking collectives  20.2 us (3%)
  between operations  14.3 us (2%)
  other arithmetic  13.8 us (2%)
  starting transfers between devices  12 us (2%)
    all_to_all x1, waiting for transfers between devices, per_device(): lax.all_to_all(pair_grads, 'cls', split_axis=0, concat_axis=0, tiled=True)  386 us
    all_to_all x1, waiting for transfers between devices, per_device(): lax.all_to_all(outgoing, 'cls', split_axis=0, concat_axis=0, tiled=True)  188 us
    reduce_scatter x1, waiting for transfers between devices, per_device(): proxy_share = lax.psum_scatter(owned, 'dp', scatter_dimension=1, tiled=True)  37 us
    all_to_all x1, blocking collectives, per_device(): lax.all_to_all(request_ids, 'cls', split_axis=0, concat_axis=0, tiled=True)  20.2 us
  transfers between devices with their start and end apart: 3, of which 3 were waited for; matrix products, arithmetic and copies ran while one was open for 3% of the time, Pallas kernels for 0%

commit v1 on v0

--- a/solution.py
+++ b/solution.py
@@ -64,7 +64,7 @@
     grad_unit = jnp.sum(tile_terms.astype(jnp.float32), axis=2)
     pair_grads = jnp.einsum(
         "brkc,brd->bkcd", dscore, unit_blocks, preferred_element_type=jnp.float32
-    )
+    ).astype(jnp.bfloat16)
     pair_grads = pair_grads.reshape(pair_count, TILE, D)[holder].reshape(groups, capacity, TILE, D)
     returned = lax.all_to_all(pair_grads, "cls", split_axis=0, concat_axis=0, tiled=True)
     got_ids = wanted.reshape(pair_count)
@@ -74,11 +74,9 @@
     radial = jnp.sum(unit_exact * grad_flat, axis=1, keepdims=True)
     embed_grad = ((grad_flat - unit_exact * radial) * inverse_norm).astype(jnp.bfloat16)
     select_rows = (jnp.arange(tile_dev, dtype=jnp.int32)[:, None] == got_ids[None, :]).astype(
-        jnp.float32
+        jnp.bfloat16
     )
-    owned = jnp.dot(
-        select_rows, got_terms, precision=lax.Precision.HIGHEST, preferred_element_type=jnp.float32
-    )
+    owned = jnp.dot(select_rows, got_terms, preferred_element_type=jnp.float32)
     owned = owned.reshape(tile_dev * TILE, D)
     proxy_share = lax.psum_scatter(owned, "dp", scatter_dimension=1, tiled=True)
     return (row_loss, embed_grad, proxy_share)

time: 765 us -> 541 us (0.71)
  waiting for transfers between devices: 611 us -> 400 us
  local copies, waits for them, and re-layouts: 62.9 us -> 53.9 us
    all_to_all x1, waiting for transfers between devices: 386 us -> 188 us  [per_device(): lax.all_to_all(pair_grads, 'cls', split_axis=0, concat_axis=0, tiled=True)]
    reduce_scatter x1, waiting for transfers between devices: 37 us -> 23.2 us  [per_device(): proxy_share = lax.psum_scatter(owned, 'dp', scatter_dimension=1, tiled=True)]
  transfers between devices with their start and end apart: 3 -> 3, of which waited for: 3 -> 3; matrix products, arithmetic and copies ran while one was open for 3% -> 4% of each run, Pallas kernels for 0% -> 0%
where the time goes in v1:
time: 541 us; the launch traced here: 540 us
  waiting for transfers between devices  400 us (74%)
  local copies, waits for them, and re-layouts  53.9 us (10%)
  matrix products  26.2 us (5%)
  blocking collectives  20.2 us (4%)
  between operations  14.2 us (3%)
  other arithmetic  13.9 us (3%)
  starting transfers between devices  11.8 us (2%)
    all_to_all x1, waiting for transfers between devices, per_device(): lax.all_to_all(pair_grads, 'cls', split_axis=0, concat_axis=0, tiled=True)  188 us
    all_to_all x1, waiting for transfers between devices, per_device(): lax.all_to_all(outgoing, 'cls', split_axis=0, concat_axis=0, tiled=True)  188 us
    reduce_scatter x1, waiting for transfers between devices, per_device(): proxy_share = lax.psum_scatter(owned, 'dp', scatter_dimension=1, tiled=True)  23.2 us
    all_to_all x1, blocking collectives, per_device(): lax.all_to_all(request_ids, 'cls', split_axis=0, concat_axis=0, tiled=True)  20.2 us
    reshape x2, local copies, waits for them, and re-layouts, per_device(): owned = owned.reshape(tile_dev * TILE, D)  13.5 us
    unnamed x17, local copies, waits for them, and re-layouts  11.8 us
  transfers between devices with their start and end apart: 3, of which 3 were waited for; matrix products, arithmetic and copies ran while one was open for 4% of the time, Pallas kernels for 0%

profile of v1, /device:TPU:1, one launch (start us, length us, event | category | flops | bytes accessed | tf_op | source)
XLA Modules:
  0.0 539.9 jit_solution(1943303593541357191)
XLA Ops:
  7.2 0.9 compare_and_fusion
  8.0 0.8 broadcast_divide_fusion
  9.1 0.2 select_reduce_fusion.1
  9.4 0.8 gather_fusion
  10.3 20.2 %all_to_all.22 = s32[32,1,2]{2,1,0:T(1,128)S(1)} all-to-all(s32[32,1,2]{2,1,0:T(1,128)S(1)} %bitcast.52), channel_id=1, replica_groups=mesh['dp'=8,'cls'=32] {'cls'}, dimensions={0} | all-to-all | bytes 512 | tf_op jit(solution)/shard_map/all_to_all | solution.py:42
  30.9 5.5 %gather_fusion.1 = bf16[64,128,512]{2,1,0:T(8,128)(2,1)} fusion(bf16[24,128,512]{2,1,0:T(8,128)(2,1)S(1)} %bitcast.43, s32[1024]{0:T(1024)S(1)} %pad_clamp_fusion.1), kind=kCustom, calls=%fused_computation.1 | custom fusion | bytes 16777472 | tf_op jit(solution)/shard_map/gather | solution.py:43
  36.4 5.1 all-to-all-start.1
  41.7 0.1 multiply_reduce_fusion
  41.9 0.3 fusion.12
  42.4 0.3 fusion.7
  42.7 187.9 %all-to-all-done.1 = bf16[32,2,128,512]{3,2,1,0:T(8,128)(2,1)} async-done(((bf16[32,2,128,512]{3,2,1,0:T(8,128)(2,1)}), bf16[32,2,128,512]{3,2,1,0:T(8,128)(2,1)}, u32[]{:S(2)}, u32[]{:S(2)}) %all-to-all-start.1) | async-done | bytes 8388640 | tf_op jit(solution)/shard_map/all_to_all | solution.py:44
  230.6 8.9 %gather_fusion.2 = bf16[64,128,512]{2,1,0:T(8,128)(2,1)} fusion(bf16[64,128,512]{2,1,0:T(8,128)(2,1)} %bitcast.9, s32[1024]{0:T(1024)S(1)} %pad_clamp_fusion), kind=kCustom, calls=%fused_computation.2 | custom fusion | bytes 16777472 | tf_op jit(solution)/shard_map/gather | solution.py:45
  239.5 5.7 %fusion.4 = (f32[8,128]{1,0:T(8,128)S(1)}, f32[8,128,8,128]{1,3,2,0:T(8,128)S(1)}) fusion(pred[8,8]{1,0:T(8,128)(4,1)S(1)} %iota_compare_fusion.5, bf16[8,128,512,1]{2,1,3,0:T(8,128)(2,1)S(1)} %bitcast.50, bf16[8,8,128,512]{3,2,1,0:T(8,128)(2,1)} %bitcast.44), kind=kOutput, calls=%fused_computation.15 | convolution fusion | flops 1076886528 | bytes 13635648 | tf_op jit(solution)/shard_map/brd,bkcd->brkc/dot_general | solution.py:46
  245.2 1.7 fusion
  246.9 0.6 subtract_bitcast_fusion
  247.6 4.6 convolution_convert_fusion
  252.2 8.9 %gather_fusion.3 = bf16[64,128,512]{2,1,0:T(8,128)(2,1)} fusion(bf16[64,128,512]{2,1,0:T(8,128)(2,1)} %bitcast.48, s32[1024]{0:T(1024)S(1)} %pad_clamp_fusion.2), kind=kCustom, calls=%fused_computation.3 | custom fusion | bytes 16777472 | tf_op jit(solution)/shard_map/gather | solution.py:68
  261.1 6.5 %all-to-all-start.2 = ((bf16[32,2,128,512]{3,2,1,0:T(8,128)(2,1)}), bf16[32,2,128,512]{3,2,1,0:T(8,128)(2,1)}, u32[]{:S(2)}, u32[]{:S(2)}) async-start(bf16[32,2,128,512]{3,2,1,0:T(8,128)(2,1)} %bitcast.47), calls=%async_computation.2 | async-start | bytes 16777216 | tf_op jit(solution)/shard_map/all_to_all | solution.py:69
  267.6 0.2 reduce-scatter.2.cloned.1.call-start
  267.8 0.5 broadcast.256
  268.3 0.7 reduce.5
  269.1 188.5 %all-to-all-done.2 = bf16[32,2,128,512]{3,2,1,0:T(8,128)(2,1)} async-done(((bf16[32,2,128,512]{3,2,1,0:T(8,128)(2,1)}), bf16[32,2,128,512]{3,2,1,0:T(8,128)(2,1)}, u32[]{:S(2)}, u32[]{:S(2)}) %all-to-all-start.2) | async-done | bytes 8388640 | tf_op jit(solution)/shard_map/all_to_all | solution.py:69
  457.6 11.8 %copy.41 = bf16[8,8,128,512]{3,1,2,0:T(8,128)(2,1)} copy(bf16[8,8,128,512]{3,2,1,0:T(8,128)(2,1)} %bitcast.23) | data formatting | bytes 16777216
  469.3 7.3 %fusion.14 = f32[24,65536]{1,0:T(8,128)} fusion(bf16[64,65536]{1,0:T(8,128)(2,1)} %bitcast.49, s32[64]{0:T(128)S(1)} %eq.76), kind=kOutput, calls=%fused_computation.33 | convolution fusion | flops 201328128 | bytes 14680320 | tf_op jit(solution)/shard_map/dot_general | solution.py:79
  476.6 6.8 %reshape.281 = f32[3072,512]{1,0:T(8,128)} reshape(f32[24,65536]{1,0:T(8,128)} %fusion.14) | data formatting | bytes 12582912 | tf_op jit(solution)/shard_map/reshape | solution.py:80
  483.5 6.6 %copy.37 = f32[3072,512]{0,1:T(8,128)} copy(f32[3072,512]{1,0:T(8,128)} %reshape.281) | data formatting | bytes 12582912 | tf_op jit(solution)/shard_map/reshape | solution.py:80
  490.1 8.6 %convert_bitcast_fusion = bf16[8,128,8,512]{1,3,2,0:T(8,128)(2,1)S(1)} fusion(bf16[8,8,128,512]{3,2,1,0:T(8,128)(2,1)} %bitcast.45, f32[8,128,8,128]{1,3,2,0:T(8,128)} %copy-done.2, f32[8,128]{1,0:T(8,128)S(1)} %get-tuple-element.6, pred[8,128,128]{1,2,0:T(8,128)(4,1)S(1)} %iota_compare_fusion, pred[8,8]{1,0:T(8,128)(4,1)S(1)} %iota_compare_fusion.5, ...), kind=kOutput, calls=%fused_computation.5 | convolution fusion | flops 1086324736 | bytes 21106760 | tf_op jit(solution)/shard_map/brkc,bkcd->brkd/dot_general | solution.py:60
  498.7 2.8 convert_reduce_fusion
  501.5 3.0 copy.36
  504.5 2.6 fusion.8
  507.2 2.7 fusion.11
  509.9 23.2 %reduce-scatter.2.cloned.1.call-done = f32[3072,64]{0,1:T(8,128)} async-done(((f32[3072,512]{0,1:T(8,128)}), f32[3072,64]{0,1:T(8,128)}) %reduce-scatter.2.cloned.1.call-update) | async-done | bytes 786448 | tf_op jit(solution)/shard_map/reduce_scatter | solution.py:81
  (41 shorter events, 1.4 us)
Async XLA Ops:
  7.2 23.7 %copy-start = (bf16[3072,512]{1,0:T(8,128)(2,1)S(1)}, bf16[3072,512]{1,0:T(8,128)(2,1)}, u32[]{:S(2)}) copy-start(bf16[3072,512]{1,0:T(8,128)(2,1)} %param.6) | copy-start | bytes 9437188
  36.4 5.3 copy-start.5
  36.4 5.5 %copy-start.4 = (bf16[1024,512]{1,0:T(8,128)(2,1)S(1)}, bf16[1024,512]{1,0:T(8,128)(2,1)}, u32[]{:S(2)}) copy-start(bf16[1024,512]{1,0:T(8,128)(2,1)} %param.5) | copy-start | bytes 3145732
  36.4 5.7 %copy-start.7 = (s32[8]{0:T(128)S(1)}, s32[8]{0:T(128)}, u32[]{:S(2)}) copy-start(s32[8]{0:T(128)} %param.8) | copy-start | bytes 100
  36.4 5.8 %copy-start.6 = (s32[1024]{0:T(1024)S(1)}, s32[1024]{0:T(1024)}, u32[]{:S(2)}) copy-start(s32[1024]{0:T(1024)} %param.9) | copy-start | bytes 12292
  36.4 194.2 %all-to-all-start.1 = ((bf16[32,2,128,512]{3,2,1,0:T(8,128)(2,1)}), bf16[32,2,128,512]{3,2,1,0:T(8,128)(2,1)}, u32[]{:S(2)}, u32[]{:S(2)}) async-start(bf16[32,2,128,512]{3,2,1,0:T(8,128)(2,1)} %bitcast.46), calls=%async_computation.1 | async-start | bytes 16777216 | tf_op jit(solution)/shard_map/all_to_all | solution.py:44
  245.2 6.9 %copy-start.2 = (f32[8,128,8,128]{1,3,2,0:T(8,128)}, f32[8,128,8,128]{1,3,2,0:T(8,128)S(1)}, u32[]{:S(2)}) copy-start(f32[8,128,8,128]{1,3,2,0:T(8,128)S(1)} %get-tuple-element.14) | copy-start | bytes 12582916
  261.1 196.5 %all-to-all-start.2 = ((bf16[32,2,128,512]{3,2,1,0:T(8,128)(2,1)}), bf16[32,2,128,512]{3,2,1,0:T(8,128)(2,1)}, u32[]{:S(2)}, u32[]{:S(2)}) async-start(bf16[32,2,128,512]{3,2,1,0:T(8,128)(2,1)} %bitcast.47), calls=%async_computation.2 | async-start | bytes 16777216 | tf_op jit(solution)/shard_map/all_to_all | solution.py:69
  267.6 265.5 %reduce-scatter.2.cloned.1.call-start = ((), (), s32[]{:S(2)}) async-start(), calls=%async_computation.4 | async-start | bytes 7077888 | tf_op jit(solution)/shard_map/reduce_scatter | solution.py:81
  501.5 31.6 %copy-start.1 = (bf16[3072,512]{1,0:T(8,128)(2,1)S(1)}, bf16[3072,512]{1,0:T(8,128)(2,1)}, u32[]{:S(2)}) copy-start(bf16[3072,512]{1,0:T(8,128)(2,1)} %param.6) | copy-start | bytes 9437188
  504.5 2.6 copy-start.3
Sparse Core Ops, SparseCore 0:
  490.2 42.7 reduce-scatter.1

commit v2 on v1

--- a/solution.py
+++ b/solution.py
@@ -1,12 +1,74 @@
+import functools
+
 import jax
 import jax.numpy as jnp
 from jax import lax
+from jax.experimental import pallas as pl
+from jax.experimental.pallas import tpu as pltpu
 from jax.sharding import PartitionSpec as P
 
 D = 512
 TILE = 128
 BR = 128
 K = 8
+
+
+MESH = pl.DeviceIdType.MESH
+
+
+def _a2a_kernel(n, src_ref, out_ref, send_sem, recv_sem, local_sem):
+    me = lax.axis_index("cls")
+    row = lax.axis_index("dp")
+    barrier = pltpu.get_barrier_semaphore()
+
+    def greet(j, carry):
+        peer = lax.rem(me + j, n)
+        pl.semaphore_signal(barrier, inc=1, device_id=(row, peer), device_id_type=MESH)
+        return carry
+
+    lax.fori_loop(1, n, greet, 0)
+    pl.semaphore_wait(barrier, n - 1)
+    local = pltpu.make_async_copy(src_ref.at[me], out_ref.at[me], local_sem)
+    local.start()
+
+    def remote(j):
+        peer = lax.rem(me + j, n)
+        return pltpu.make_async_remote_copy(
+            src_ref=src_ref.at[peer],
+            dst_ref=out_ref.at[me],
+            send_sem=send_sem.at[j],
+            recv_sem=recv_sem.at[j],
+            device_id=(row, peer),
+            device_id_type=MESH,
+        )
+
+    def launch(j, carry):
+        remote(j).start()
+        return carry
+
+    def finish(j, carry):
+        remote(j).wait()
+        return carry
+
+    lax.fori_loop(1, n, launch, 0)
+    lax.fori_loop(1, n, finish, 0)
+    local.wait()
+
+
+def cls_all_to_all(x, cid):
+    n = x.shape[0]
+    return pl.pallas_call(
+        functools.partial(_a2a_kernel, n),
+        out_shape=jax.ShapeDtypeStruct(x.shape, x.dtype),
+        in_specs=[pl.BlockSpec(memory_space=pl.ANY)],
+        out_specs=pl.BlockSpec(memory_space=pl.ANY),
+        scratch_shapes=[
+            pltpu.SemaphoreType.DMA((n,)),
+            pltpu.SemaphoreType.DMA((n,)),
+            pltpu.SemaphoreType.DMA,
+        ],
+        compiler_params=pltpu.CompilerParams(collective_id=cid, has_side_effects=True),
+    )(x)
 
 
 logit_scale = 4.0
@@ -39,9 +101,9 @@
     valid_entry = entries[None, :] < tile_count[:, None]
     pos_cols = labels.reshape(blocks, BR) - hard_tiles[:, 0:1] * TILE
     tile_table = proxies.reshape(tile_dev, TILE, D)
-    wanted = lax.all_to_all(request_ids, "cls", split_axis=0, concat_axis=0, tiled=True)
+    wanted = cls_all_to_all(request_ids, 0)
     outgoing = tile_table[wanted]
-    fetched = lax.all_to_all(outgoing, "cls", split_axis=0, concat_axis=0, tiled=True)
+    fetched = cls_all_to_all(outgoing, 1)
     candidates = fetched.reshape(pair_count, TILE, D)[slot_of].reshape(blocks, K, TILE, D)
     logits = logit_scale * jnp.einsum(
         "brd,bkcd->brkc", unit_blocks, candidates, preferred_element_type=jnp.float32
@@ -66,7 +128,7 @@
         "brkc,brd->bkcd", dscore, unit_blocks, preferred_element_type=jnp.float32
     ).astype(jnp.bfloat16)
     pair_grads = pair_grads.reshape(pair_count, TILE, D)[holder].reshape(groups, capacity, TILE, D)
-    returned = lax.all_to_all(pair_grads, "cls", split_axis=0, concat_axis=0, tiled=True)
+    returned = cls_all_to_all(pair_grads, 2)
     got_ids = wanted.reshape(pair_count)
     got_terms = returned.reshape(pair_count, TILE * D)
     row_loss = (log_total - positive).reshape(-1)

time: 541 us -> 613 us (1.13)
  Pallas kernels: 0 us -> 435 us
  waiting for transfers between devices: 400 us -> 63.2 us
  blocking collectives: 20.2 us -> 0 us
  starting transfers between devices: 11.8 us -> 0.04 us
    pallas_call x0 -> x3, Pallas kernels: none -> 435 us  [cls_all_to_all(): pl.pallas_call(functools.partial(_a2a_kernel, n), out_shape=jax.ShapeDtyp...]
    all_to_all x2 -> x0, waiting for transfers between devices: 376 us -> none  [the longest x1 188 us: per_device(): lax.all_to_all(pair_grads, 'cls', split_axis=0, concat_axis=0, tiled=True)]
    reduce_scatter x1, waiting for transfers between devices: 23.2 us -> 63.1 us  [per_device(): proxy_share = lax.psum_scatter(owned, 'dp', scatter_dimension=1, tiled=True)]
    all_to_all x1 -> x0, blocking collectives: 20.2 us -> none  [per_device(): lax.all_to_all(request_ids, 'cls', split_axis=0, concat_axis=0, tiled=True)]
    all_to_all x2 -> x0, starting transfers between devices: 11.6 us -> none  [the longest x1 6.48 us: per_device(): lax.all_to_all(pair_grads, 'cls', split_axis=0, concat_axis=0, tiled=True)]
  transfers between devices with their start and end apart: 3 -> 1, of which waited for: 3 -> 1; matrix products, arithmetic and copies ran while one was open for 4% -> 3% of each run, Pallas kernels for 0% -> 0%
where the time goes in v2:
time: 613 us; the launch traced here: 612 us
  Pallas kernels  435 us (71%)
  waiting for transfers between devices  63.2 us (10%)
  local copies, waits for them, and re-layouts  54.5 us (9%)
  matrix products  26.2 us (4%)
  other arithmetic  19.2 us (3%)
  between operations  14.2 us (2%)
    pallas_call x3, Pallas kernels, cls_all_to_all(): pl.pallas_call(functools.partial(_a2a_kernel, n), out_shape=jax.ShapeDtyp...  435 us
    reduce_scatter x1, waiting for transfers between devices, per_device(): proxy_share = lax.psum_scatter(owned, 'dp', scatter_dimension=1, tiled=True)  63.1 us
    reshape x2, local copies, waits for them, and re-layouts, per_device(): owned = owned.reshape(tile_dev * TILE, D)  13.5 us
  transfers between devices with their start and end apart: 1, of which 1 were waited for; matrix products, arithmetic and copies ran while one was open for 3% of the time, Pallas kernels for 0%

profile of v2, /device:TPU:1, one launch (start us, length us, event | category | flops | bytes accessed | tf_op | source)
XLA Modules:
  0.0 611.9 jit_solution(13992261489930254936)
XLA Ops:
  7.2 1.0 multiply_reduce_fusion
  8.2 0.7 compare_and_fusion
  8.9 0.7 broadcast_divide_fusion
  9.9 0.2 select_reduce_fusion.1
  10.3 0.8 gather_fusion
  11.0 0.7 reshape.244.src_ref
  11.8 14.5 %shard_map.76 = s32[32,2]{1,0:T(8,128)} custom-call(s32[32,2]{1,0:T(8,128)} %reshape.244.src_ref), custom_call_target="tpu_custom_call" | custom-call | tf_op jit(solution)/shard_map/pallas_call | solution.py:60
  26.2 0.8 eq.76
  27.0 0.7 compare_select_fusion
  27.8 0.7 iota_compare_fusion.5
  28.6 1.5 fusion.12
  30.2 0.8 bitcast_subtract_fusion
  31.1 2.5 fusion.7
  33.6 5.5 gather_fusion.1
  39.1 197.5 %shard_map.77 = bf16[32,2,128,512]{3,2,1,0:T(8,128)(2,1)} custom-call(bf16[32,2,128,512]{3,2,1,0:T(8,128)(2,1)} %bitcast.46), custom_call_target="tpu_custom_call" | custom-call | tf_op jit(solution)/shard_map/pallas_call | solution.py:60
  236.7 9.0 %gather_fusion.2 = bf16[64,128,512]{2,1,0:T(8,128)(2,1)} fusion(bf16[64,128,512]{2,1,0:T(8,128)(2,1)} %bitcast.43, s32[1024]{0:T(1024)S(1)} %pad_clamp_fusion), kind=kCustom, calls=%fused_computation.2 | custom fusion | bytes 16777472 | tf_op jit(solution)/shard_map/gather | solution.py:107
  245.7 5.7 fusion.4
  251.4 1.7 fusion
  253.1 0.6 subtract_bitcast_fusion
  253.7 4.6 convolution_convert_fusion
  258.3 8.9 %gather_fusion.3 = bf16[64,128,512]{2,1,0:T(8,128)(2,1)} fusion(bf16[64,128,512]{2,1,0:T(8,128)(2,1)} %bitcast.44, s32[1024]{0:T(1024)S(1)} %pad_clamp_fusion.2), kind=kCustom, calls=%fused_computation.3 | custom fusion | bytes 16777472 | tf_op jit(solution)/shard_map/gather | solution.py:130
  267.2 222.6 %shard_map.78 = bf16[32,2,128,512]{3,2,1,0:T(8,128)(2,1)} custom-call(bf16[32,2,128,512]{3,2,1,0:T(8,128)(2,1)} %bitcast.45), custom_call_target="tpu_custom_call" | custom-call | tf_op jit(solution)/shard_map/pallas_call | solution.py:60
  489.9 11.7 %copy.35 = bf16[8,8,128,512]{3,1,2,0:T(8,128)(2,1)} copy(bf16[8,8,128,512]{3,2,1,0:T(8,128)(2,1)} %bitcast.48) | data formatting | bytes 16777216
  501.6 7.2 %fusion.14 = f32[24,65536]{1,0:T(8,128)} fusion(bf16[64,65536]{1,0:T(8,128)(2,1)} %bitcast.47, s32[64]{0:T(128)S(1)} %eq.76), kind=kOutput, calls=%fused_computation.34 | convolution fusion | flops 201328128 | bytes 14680320 | tf_op jit(solution)/shard_map/dot_general | solution.py:141
  508.9 6.8 %reshape.252 = f32[3072,512]{1,0:T(8,128)} reshape(f32[24,65536]{1,0:T(8,128)} %fusion.14) | data formatting | bytes 12582912 | tf_op jit(solution)/shard_map/reshape | solution.py:142
  515.7 6.6 %copy.29 = f32[3072,512]{0,1:T(8,128)} copy(f32[3072,512]{1,0:T(8,128)} %reshape.252) | data formatting | bytes 12582912 | tf_op jit(solution)/shard_map/reshape | solution.py:142
  522.3 8.6 %convert_bitcast_fusion = bf16[8,128,8,512]{1,3,2,0:T(8,128)(2,1)S(1)} fusion(bf16[8,8,128,512]{3,2,1,0:T(8,128)(2,1)} %bitcast.42, f32[8,128,8,128]{1,3,2,0:T(8,128)} %copy-done.2, f32[8,128]{1,0:T(8,128)S(1)} %get-tuple-element.6, pred[8,128,128]{1,2,0:T(8,128)(4,1)S(1)} %iota_compare_fusion, pred[8,8]{1,0:T(8,128)(4,1)S(1)} %iota_compare_fusion.5, ...), kind=kOutput, calls=%fused_computation.5 | convolution fusion | flops 1086324736 | bytes 21106760 | tf_op jit(solution)/shard_map/brkc,bkcd->brkd/dot_general | solution.py:122
  531.0 2.8 convert_reduce_fusion
  533.7 3.0 copy.28
  536.8 2.5 fusion.8
  539.3 2.7 fusion.11
  542.0 63.1 %reduce-scatter.2.cloned.1.call-done = f32[3072,64]{0,1:T(8,128)} async-done(((f32[3072,512]{0,1:T(8,128)}), f32[3072,64]{0,1:T(8,128)}) %reduce-scatter.2.cloned.1.call-update) | async-done | bytes 786448 | tf_op jit(solution)/shard_map/reduce_scatter | solution.py:143
  (29 shorter events, 0.8 us)
Async XLA Ops:
  7.2 26.4 %copy-start = (bf16[3072,512]{1,0:T(8,128)(2,1)S(1)}, bf16[3072,512]{1,0:T(8,128)(2,1)}, u32[]{:S(2)}) copy-start(bf16[3072,512]{1,0:T(8,128)(2,1)} %param.6) | copy-start | bytes 9437188
  7.2 597.9 %reduce-scatter.2.cloned.1.call-start = ((), (), s32[]{:S(2)}) async-start(), calls=%async_computation.1 | async-start | bytes 7077888 | tf_op jit(solution)/shard_map/reduce_scatter | solution.py:143
  236.6 9.0 %copy-start.4 = (bf16[1024,512]{1,0:T(8,128)(2,1)S(1)}, bf16[1024,512]{1,0:T(8,128)(2,1)}, u32[]{:S(2)}) copy-start(bf16[1024,512]{1,0:T(8,128)(2,1)} %fusion.7) | copy-start | bytes 3145732
  251.4 6.9 %copy-start.2 = (f32[8,128,8,128]{1,3,2,0:T(8,128)}, f32[8,128,8,128]{1,3,2,0:T(8,128)S(1)}, u32[]{:S(2)}) copy-start(f32[8,128,8,128]{1,3,2,0:T(8,128)S(1)} %get-tuple-element.14) | copy-start | bytes 12582916
  533.7 71.4 %copy-start.1 = (bf16[3072,512]{1,0:T(8,128)(2,1)S(1)}, bf16[3072,512]{1,0:T(8,128)(2,1)}, u32[]{:S(2)}) copy-start(bf16[3072,512]{1,0:T(8,128)(2,1)} %param.6) | copy-start | bytes 9437188
  536.8 2.5 copy-start.3
Sparse Core Ops, SparseCore 0:
  522.5 82.5 reduce-scatter.1

commit v3 on v2

--- a/solution.py
+++ b/solution.py
@@ -73,6 +73,94 @@
 
 logit_scale = 4.0
 epsilon = 1e-06
+
+
+def _block_kernel(slot_ref, count_ref, emb_ref, pos_ref, *rest):
+    tiles = rest[:K]
+    loss_ref, grad_ref, pair_hbm, pair_buf, pair_sem = rest[K:]
+    b = pl.program_id(0)
+    emb = emb_ref[0].astype(jnp.float32)
+    inverse_norm = lax.rsqrt(jnp.sum(emb * emb, axis=1, keepdims=True) + epsilon)
+    unit_exact = emb * inverse_norm
+    unit_rows = unit_exact.astype(jnp.bfloat16)
+    count = count_ref[b]
+    columns = lax.broadcasted_iota(jnp.int32, (BR, TILE), 1)
+    hit = columns == pos_ref[0]
+    logits = []
+    for k in range(K):
+        cand = tiles[k][0]
+        lg = logit_scale * lax.dot_general(
+            unit_rows, cand, (((1,), (1,)), ((), ())), preferred_element_type=jnp.float32
+        )
+        logits.append(lg)
+    masked = [jnp.where(k < count, logits[k], -1e30) for k in range(K)]
+    peak = masked[0].max(axis=1, keepdims=True)
+    for k in range(1, K):
+        peak = jnp.maximum(peak, masked[k].max(axis=1, keepdims=True))
+    total = jnp.zeros_like(peak)
+    for k in range(K):
+        total = total + jnp.sum(jnp.exp(masked[k] - peak), axis=1, keepdims=True)
+    log_total = peak + jnp.log(total)
+    positive = jnp.sum(jnp.where(hit, logits[0], 0.0), axis=1, keepdims=True)
+    loss_ref[0] = log_total - positive
+    grad_unit = jnp.zeros((BR, D), jnp.float32)
+    for k in range(K):
+        probabilities = jnp.exp(masked[k] - log_total)
+        if k == 0:
+            probabilities = probabilities - jnp.where(hit, 1.0, 0.0)
+        dscore = (logit_scale * probabilities).astype(jnp.bfloat16)
+        cand = tiles[k][0]
+        terms = jnp.dot(dscore, cand, preferred_element_type=jnp.float32)
+        grad_unit = grad_unit + terms.astype(jnp.bfloat16).astype(jnp.float32)
+        pair_buf[k] = lax.dot_general(
+            dscore, unit_rows, (((0,), (0,)), ((), ())), preferred_element_type=jnp.float32
+        ).astype(jnp.bfloat16)
+    copies = []
+    for k in range(K):
+        cp = pltpu.make_async_copy(pair_buf.at[k], pair_hbm.at[slot_ref[b * K + k]], pair_sem.at[k])
+        cp.start()
+        copies.append(cp)
+    radial = jnp.sum(unit_exact * grad_unit, axis=1, keepdims=True)
+    grad_ref[0] = ((grad_unit - unit_exact * radial) * inverse_norm).astype(grad_ref.dtype)
+    for cp in copies:
+        cp.wait()
+
+
+def block_step(slot_of, tile_count, emb_blocks, pos_cols, fetched):
+    blocks = emb_blocks.shape[0]
+    pairs = fetched.shape[0]
+
+    def tile_spec(k):
+        return pl.BlockSpec((1, TILE, D), lambda b, slot, cnt: (slot[b * K + k], 0, 0))
+
+    grid_spec = pltpu.PrefetchScalarGridSpec(
+        num_scalar_prefetch=2,
+        grid=(blocks,),
+        in_specs=[
+            pl.BlockSpec((1, BR, D), lambda b, slot, cnt: (b, 0, 0)),
+            pl.BlockSpec((1, BR, 1), lambda b, slot, cnt: (b, 0, 0)),
+        ]
+        + [tile_spec(k) for k in range(K)],
+        out_specs=[
+            pl.BlockSpec((1, BR, 1), lambda b, slot, cnt: (b, 0, 0)),
+            pl.BlockSpec((1, BR, D), lambda b, slot, cnt: (b, 0, 0)),
+            pl.BlockSpec(memory_space=pl.ANY),
+        ],
+        scratch_shapes=[
+            pltpu.VMEM((K, TILE, D), jnp.bfloat16),
+            pltpu.SemaphoreType.DMA((K,)),
+        ],
+    )
+    return pl.pallas_call(
+        _block_kernel,
+        grid_spec=grid_spec,
+        out_shape=[
+            jax.ShapeDtypeStruct((blocks, BR, 1), jnp.float32),
+            jax.ShapeDtypeStruct((blocks, BR, D), jnp.bfloat16),
+            jax.ShapeDtypeStruct((pairs, TILE, D), jnp.bfloat16),
+        ],
+        compiler_params=pltpu.CompilerParams(vmem_limit_bytes=48 * 1024 * 1024),
+    )(slot_of, tile_count, emb_blocks, pos_cols, *([fetched] * K))
 
 
 def per_device(embeddings, proxies, hard_tiles, tile_count, labels):
@@ -91,57 +179,26 @@
     slot_of = owners * capacity + rank_order
     holder = jnp.sum(jnp.where(slot_of[None, :] == counter[:, None], counter[None, :], 0), axis=1)
     request_ids = local_ids[holder].reshape(groups, capacity)
-    emb_exact = embeddings.astype(jnp.float32)
-    inverse_norm = lax.rsqrt(jnp.sum(emb_exact * emb_exact, axis=1, keepdims=True) + epsilon)
-    unit_exact = emb_exact * inverse_norm
-    unit_rows = unit_exact.astype(jnp.bfloat16)
-    unit_blocks = unit_rows.reshape(blocks, BR, D)
-    entries = jnp.arange(K, dtype=jnp.int32)
-    columns = jnp.arange(TILE, dtype=jnp.int32)
-    valid_entry = entries[None, :] < tile_count[:, None]
-    pos_cols = labels.reshape(blocks, BR) - hard_tiles[:, 0:1] * TILE
     tile_table = proxies.reshape(tile_dev, TILE, D)
     wanted = cls_all_to_all(request_ids, 0)
     outgoing = tile_table[wanted]
-    fetched = cls_all_to_all(outgoing, 1)
-    candidates = fetched.reshape(pair_count, TILE, D)[slot_of].reshape(blocks, K, TILE, D)
-    logits = logit_scale * jnp.einsum(
-        "brd,bkcd->brkc", unit_blocks, candidates, preferred_element_type=jnp.float32
-    )
-    masked = jnp.where(valid_entry[:, None, :, None], logits, -1e30)
-    peak_row = jnp.max(masked, axis=(2, 3))
-    total_row = jnp.sum(jnp.exp(masked - peak_row[:, :, None, None]), axis=(2, 3))
-    log_total = peak_row + jnp.log(total_row)
-    positive_hit = (
-        (entries == 0)[None, None, :, None]
-        & (columns[None, None, None, :] == pos_cols[:, :, None, None])
-    ).astype(jnp.float32)
-    positive = jnp.sum(logits * positive_hit, axis=(2, 3))
-    probabilities = jnp.exp(masked - log_total[:, :, None, None])
-    dscore = (logit_scale * (probabilities - positive_hit)).astype(jnp.bfloat16)
-    tile_terms = jnp.einsum(
-        "brkc,bkcd->brkd", dscore, candidates, preferred_element_type=jnp.float32
-    ).astype(jnp.bfloat16)
-    tile_terms = lax.optimization_barrier(tile_terms)
-    grad_unit = jnp.sum(tile_terms.astype(jnp.float32), axis=2)
-    pair_grads = jnp.einsum(
-        "brkc,brd->bkcd", dscore, unit_blocks, preferred_element_type=jnp.float32
-    ).astype(jnp.bfloat16)
-    pair_grads = pair_grads.reshape(pair_count, TILE, D)[holder].reshape(groups, capacity, TILE, D)
-    returned = cls_all_to_all(pair_grads, 2)
+    fetched = lax.all_to_all(outgoing, "cls", split_axis=0, concat_axis=0, tiled=True)
+    fetched = fetched.reshape(pair_count, TILE, D)
+    pos_cols = labels.reshape(blocks, BR, 1) - hard_tiles[:, 0:1, None] * TILE
+    loss, embed_grad, pair_grads = block_step(
+        slot_of, tile_count, embeddings.reshape(blocks, BR, D), pos_cols, fetched
+    )
+    pair_grads = pair_grads.reshape(groups, capacity, TILE, D)
+    returned = lax.all_to_all(pair_grads, "cls", split_axis=0, concat_axis=0, tiled=True)
     got_ids = wanted.reshape(pair_count)
     got_terms = returned.reshape(pair_count, TILE * D)
-    row_loss = (log_total - positive).reshape(-1)
-    grad_flat = grad_unit.reshape(-1, D)
-    radial = jnp.sum(unit_exact * grad_flat, axis=1, keepdims=True)
-    embed_grad = ((grad_flat - unit_exact * radial) * inverse_norm).astype(jnp.bfloat16)
     select_rows = (jnp.arange(tile_dev, dtype=jnp.int32)[:, None] == got_ids[None, :]).astype(
         jnp.bfloat16
     )
     owned = jnp.dot(select_rows, got_terms, preferred_element_type=jnp.float32)
     owned = owned.reshape(tile_dev * TILE, D)
     proxy_share = lax.psum_scatter(owned, "dp", scatter_dimension=1, tiled=True)
-    return (row_loss, embed_grad, proxy_share)
+    return (loss.reshape(-1), embed_grad.reshape(-1, D), proxy_share)
 
 
 def solution(mesh):

time: 613 us -> 531 us (0.87)
  Pallas kernels: 435 us -> 36.9 us
  waiting for transfers between devices: 63.2 us -> 420 us
  local copies, waits for them, and re-layouts: 54.5 us -> 33.8 us
  matrix products: 26.2 us -> 7.28 us
  other arithmetic: 19.2 us -> 4.76 us
  starting transfers between devices: 0.04 us -> 13.8 us
    pallas_call x3 -> x1, Pallas kernels: 435 us -> 14.5 us  [cls_all_to_all(): pl.pallas_call(functools.partial(_a2a_kernel, n), out_shape=jax.ShapeDtyp...]
    all_to_all x0 -> x2, waiting for transfers between devices: none -> 378 us  [the longest x1 189 us: per_device(): lax.all_to_all(outgoing, 'cls', split_axis=0, concat_axis=0, tiled=True)]
    pallas_call x0 -> x1, Pallas kernels: none -> 22.5 us  [block_step(): pl.pallas_call(_block_kernel, grid_spec=grid_spec, out_shape=[jax.ShapeDt...]
    reduce_scatter x1, waiting for transfers between devices: 63.1 us -> 42.2 us  [per_device(): proxy_share = lax.psum_scatter(owned, 'dp', scatter_dimension=1, tiled=True)]
    dot_general x3 -> x0, matrix products: 18.9 us -> none  [the longest x1 8.61 us: per_device(): jnp.einsum('brkc,bkcd->brkd', dscore, candidates, preferred_element_type=...]
    gather x2 -> x0, local copies, waits for them, and re-layouts: 17.9 us -> none  [the longest x1 9 us: per_device(): fetched.reshape(pair_count, TILE, D)[slot_of].reshape(blocks, K, TILE, D)]
    all_to_all x0 -> x2, starting transfers between devices: none -> 13.5 us  [the longest x1 7.37 us: per_device(): lax.all_to_all(outgoing, 'cls', split_axis=0, concat_axis=0, tiled=True)]
    reduce_sum x4 -> x0, other arithmetic: 8.49 us -> none  [the longest x1 2.76 us: per_device(): grad_unit = jnp.sum(tile_terms.astype(jnp.float32), axis=2)]
  transfers between devices with their start and end apart: 1 -> 3, of which waited for: 1 -> 3; matrix products, arithmetic and copies ran while one was open for 3% -> 0% of each run, Pallas kernels for 0% -> 0%
where the time goes in v3:
time: 531 us
  waiting for transfers between devices  420 us (79%)
  Pallas kernels  36.9 us (7%)
  local copies, waits for them, and re-layouts  33.8 us (6%)
  between operations  14.2 us (3%)
  starting transfers between devices  13.8 us (3%)
  matrix products  7.28 us (1%)
    all_to_all x1, waiting for transfers between devices, per_device(): lax.all_to_all(outgoing, 'cls', split_axis=0, concat_axis=0, tiled=True)  189 us
    all_to_all x1, waiting for transfers between devices, per_device(): lax.all_to_all(pair_grads, 'cls', split_axis=0, concat_axis=0, tiled=True)  189 us
    reduce_scatter x1, waiting for transfers between devices, per_device(): proxy_share = lax.psum_scatter(owned, 'dp', scatter_dimension=1, tiled=True)  42.2 us
    pallas_call x1, Pallas kernels, block_step(): pl.pallas_call(_block_kernel, grid_spec=grid_spec, out_shape=[jax.ShapeDt...  22.5 us
    pallas_call x1, Pallas kernels, cls_all_to_all(): pl.pallas_call(functools.partial(_a2a_kernel, n), out_shape=jax.ShapeDtyp...  14.5 us
    reshape x2, local copies, waits for them, and re-layouts, per_device(): owned = owned.reshape(tile_dev * TILE, D)  13.6 us
    unnamed x17, local copies, waits for them, and re-layouts  12.6 us
  transfers between devices with their start and end apart: 3, of which 3 were waited for; matrix products, arithmetic and copies ran while one was open for 0% of the time, Pallas kernels for 0%

profile of v3, /device:TPU:1, one launch (start us, length us, event | category | flops | bytes accessed | tf_op | source)
XLA Modules:
  0.0 530.9 jit_solution(14584273882352721015)
XLA Ops:
  7.2 0.0 copy-start
  7.2 0.8 sign_compare_fusion
  8.0 0.8 broadcast_remainder_fusion
  8.8 0.1 ne.51
  8.9 0.1 rem.30
  9.0 0.1 div.21
  9.1 0.2 select_reduce_fusion.1
  9.3 0.1 select_reduce_fusion
  9.4 0.8 gather_fusion
  10.2 0.7 reshape.152.src_ref
  10.9 14.5 %shard_map.76 = s32[32,2]{1,0:T(8,128)} custom-call(s32[32,2]{1,0:T(8,128)} %reshape.152.src_ref), custom_call_target="tpu_custom_call" | custom-call | tf_op jit(solution)/shard_map/pallas_call | solution.py:60
  25.4 0.7 compare_select_fusion
  26.1 0.1 reshape.169
  26.2 5.5 %gather_fusion.1 = bf16[64,128,512]{2,1,0:T(8,128)(2,1)} fusion(bf16[24,128,512]{2,1,0:T(8,128)(2,1)S(1)} %bitcast.16, s32[1024]{0:T(1024)S(1)} %pad_clamp_fusion), kind=kCustom, calls=%fused_computation.1 | custom fusion | bytes 16777472 | tf_op jit(solution)/shard_map/gather | solution.py:184
  31.8 7.4 %all-to-all-start = ((bf16[32,2,128,512]{3,2,1,0:T(8,128)(2,1)}), bf16[32,2,128,512]{3,2,1,0:T(8,128)(2,1)}, u32[]{:S(2)}, u32[]{:S(2)}) async-start(bf16[32,2,128,512]{3,2,1,0:T(8,128)(2,1)} %bitcast.18), calls=%async_computation | async-start | bytes 16777216 | tf_op jit(solution)/shard_map/all_to_all | solution.py:185
  39.2 0.2 copy.13
  39.4 0.1 multiply_reduce_fusion
  39.5 0.1 broadcast_subtract_fusion.pos_ref
  39.6 188.9 %all-to-all-done = bf16[32,2,128,512]{3,2,1,0:T(8,128)(2,1)} async-done(((bf16[32,2,128,512]{3,2,1,0:T(8,128)(2,1)}), bf16[32,2,128,512]{3,2,1,0:T(8,128)(2,1)}, u32[]{:S(2)}, u32[]{:S(2)}) %all-to-all-start) | async-done | bytes 8388640 | tf_op jit(solution)/shard_map/all_to_all | solution.py:185
  228.6 22.5 %shard_map.77 = (f32[8,128,1]{2,1,0:T(8,128)S(1)}, bf16[8,128,512]{2,1,0:T(8,128)(2,1)}, bf16[64,128,512]{2,1,0:T(8,128)(2,1)}) custom-call(s32[64]{0:T(128)S(1)} %multiply_add_fusion.slot_ref, s32[8]{0:T(128)S(1)} %copy-done.4, bf16[8,128,512]{2,1,0:T(8,128)(2,1)S(1)} %bitcast.17, s32[8,128,1]{2,1,0:T(8,128)S(1)} %broadcast_subtract_fusion.pos_ref, ...), custom_call_target="tpu_custom_call" | custom-call | tf_op jit(solution)/shard_map/pallas_call | solution.py:154
  251.1 0.8 copy-done.3
  251.9 6.2 %all-to-all-start.1 = ((bf16[32,2,128,512]{3,2,1,0:T(8,128)(2,1)}), bf16[32,2,128,512]{3,2,1,0:T(8,128)(2,1)}, u32[]{:S(2)}, u32[]{:S(2)}) async-start(bf16[32,2,128,512]{3,2,1,0:T(8,128)(2,1)} %bitcast.20), calls=%async_computation.1 | async-start | bytes 16777216 | tf_op jit(solution)/shard_map/all_to_all | solution.py:192
  258.0 0.2 reduce-scatter.2.cloned.1.call-start
  258.3 0.1 eq.47
  258.4 188.9 %all-to-all-done.1 = bf16[32,2,128,512]{3,2,1,0:T(8,128)(2,1)} async-done(((bf16[32,2,128,512]{3,2,1,0:T(8,128)(2,1)}), bf16[32,2,128,512]{3,2,1,0:T(8,128)(2,1)}, u32[]{:S(2)}, u32[]{:S(2)}) %all-to-all-start.1) | async-done | bytes 8388640 | tf_op jit(solution)/shard_map/all_to_all | solution.py:192
  447.3 11.8 %copy.16 = bf16[8,8,128,512]{3,1,2,0:T(8,128)(2,1)} copy(bf16[8,8,128,512]{3,2,1,0:T(8,128)(2,1)} %bitcast.11) | data formatting | bytes 16777216
  459.0 7.3 %fusion.1 = f32[24,65536]{1,0:T(8,128)} fusion(bf16[64,65536]{1,0:T(8,128)(2,1)} %bitcast.19, s32[64]{0:T(128)S(1)} %eq.47), kind=kOutput, calls=%fused_computation.10 | convolution fusion | flops 201328128 | bytes 14680320 | tf_op jit(solution)/shard_map/dot_general | solution.py:198
  466.3 7.1 %reshape.158 = f32[3072,512]{1,0:T(8,128)} reshape(f32[24,65536]{1,0:T(8,128)} %fusion.1) | data formatting | bytes 12582912 | tf_op jit(solution)/shard_map/reshape | solution.py:199
  473.4 6.5 %copy.15 = f32[3072,512]{0,1:T(8,128)} copy(f32[3072,512]{1,0:T(8,128)} %reshape.158) | data formatting | bytes 12582912 | tf_op jit(solution)/shard_map/reshape | solution.py:199
  479.9 0.0 reduce-scatter.2.cloned.1.call-update
  479.9 1.8 reduce.1
  481.8 42.2 %reduce-scatter.2.cloned.1.call-done = f32[3072,64]{0,1:T(8,128)} async-done(((f32[3072,512]{0,1:T(8,128)}), f32[3072,64]{0,1:T(8,128)}) %reduce-scatter.2.cloned.1.call-update) | async-done | bytes 786448 | tf_op jit(solution)/shard_map/reduce_scatter | solution.py:200
  (19 shorter events, 0.1 us)
Async XLA Ops:
  7.2 19.1 %copy-start = (bf16[3072,512]{1,0:T(8,128)(2,1)S(1)}, bf16[3072,512]{1,0:T(8,128)(2,1)}, u32[]{:S(2)}) copy-start(bf16[3072,512]{1,0:T(8,128)(2,1)} %param.6) | copy-start | bytes 9437188
  31.8 7.4 %copy-start.7 = (s32[1024]{0:T(1024)S(1)}, s32[1024]{0:T(1024)}, u32[]{:S(2)}) copy-start(s32[1024]{0:T(1024)} %param.9) | copy-start | bytes 12292
  31.8 7.6 %copy-start.6 = (s32[8,8]{1,0:T(8,128)S(1)}, s32[8,8]{1,0:T(8,128)}, u32[]{:S(2)}) copy-start(s32[8,8]{1,0:T(8,128)} %param.7) | copy-start | bytes 772
  31.8 196.8 %copy-start.2 = (bf16[1024,512]{1,0:T(8,128)(2,1)S(1)}, bf16[1024,512]{1,0:T(8,128)(2,1)}, u32[]{:S(2)}) copy-start(bf16[1024,512]{1,0:T(8,128)(2,1)} %param.5) | copy-start | bytes 3145732
  31.8 196.8 %copy-start.4 = (s32[8]{0:T(128)S(1)}, s32[8]{0:T(128)}, u32[]{:S(2)}) copy-start(s32[8]{0:T(128)} %count_ref.1) | copy-start | bytes 100
  31.8 196.8 %all-to-all-start = ((bf16[32,2,128,512]{3,2,1,0:T(8,128)(2,1)}), bf16[32,2,128,512]{3,2,1,0:T(8,128)(2,1)}, u32[]{:S(2)}, u32[]{:S(2)}) async-start(bf16[32,2,128,512]{3,2,1,0:T(8,128)(2,1)} %bitcast.18), calls=%async_computation | async-start | bytes 16777216 | tf_op jit(solution)/shard_map/all_to_all | solution.py:185
  251.1 0.8 copy-start.3
  251.1 7.2 %copy-start.5 = (s32[32,2]{1,0:T(8,128)S(1)}, s32[32,2]{1,0:T(8,128)}, u32[]{:S(2)}) copy-start(s32[32,2]{1,0:T(8,128)} %shard_map.76) | copy-start | bytes 772
  251.9 195.4 %all-to-all-start.1 = ((bf16[32,2,128,512]{3,2,1,0:T(8,128)(2,1)}), bf16[32,2,128,512]{3,2,1,0:T(8,128)(2,1)}, u32[]{:S(2)}, u32[]{:S(2)}) async-start(bf16[32,2,128,512]{3,2,1,0:T(8,128)(2,1)} %bitcast.20), calls=%async_computation.1 | async-start | bytes 16777216 | tf_op jit(solution)/shard_map/all_to_all | solution.py:192
  258.0 266.0 %reduce-scatter.2.cloned.1.call-start = ((), (), s32[]{:S(2)}) async-start(), calls=%async_computation.3 | async-start | bytes 7077888 | tf_op jit(solution)/shard_map/reduce_scatter | solution.py:200
  466.3 57.7 %copy-start.1 = (bf16[3072,512]{1,0:T(8,128)(2,1)S(1)}, bf16[3072,512]{1,0:T(8,128)(2,1)}, u32[]{:S(2)}) copy-start(bf16[3072,512]{1,0:T(8,128)(2,1)} %param.6) | copy-start | bytes 9437188
Sparse Core Ops, SparseCore 0:
  480.1 43.9 reduce-scatter.1

commit v4 on v3

--- a/solution.py
+++ b/solution.py
@@ -161,6 +161,34 @@
         ],
         compiler_params=pltpu.CompilerParams(vmem_limit_bytes=48 * 1024 * 1024),
     )(slot_of, tile_count, emb_blocks, pos_cols, *([fetched] * K))
+
+
+def _owned_kernel(ids_ref, grad_ref, out_ref):
+    s = pl.program_id(0)
+
+    @pl.when(s == 0)
+    def _():
+        out_ref[...] = jnp.zeros_like(out_ref)
+
+    start = pl.multiple_of(ids_ref[s] * TILE, TILE)
+    columns = pl.ds(start, TILE)
+    out_ref[:, columns] += grad_ref[0].astype(jnp.float32).T
+
+
+def owned_columns(got_ids, returned, tile_dev):
+    pairs = returned.shape[0]
+    grid_spec = pltpu.PrefetchScalarGridSpec(
+        num_scalar_prefetch=1,
+        grid=(pairs,),
+        in_specs=[pl.BlockSpec((1, TILE, D), lambda s, ids: (s, 0, 0))],
+        out_specs=pl.BlockSpec((D, tile_dev * TILE), lambda s, ids: (0, 0)),
+    )
+    return pl.pallas_call(
+        _owned_kernel,
+        grid_spec=grid_spec,
+        out_shape=jax.ShapeDtypeStruct((D, tile_dev * TILE), jnp.float32),
+        compiler_params=pltpu.CompilerParams(vmem_limit_bytes=48 * 1024 * 1024),
+    )(got_ids, returned)
 
 
 def per_device(embeddings, proxies, hard_tiles, tile_count, labels):
@@ -191,13 +219,8 @@
     pair_grads = pair_grads.reshape(groups, capacity, TILE, D)
     returned = lax.all_to_all(pair_grads, "cls", split_axis=0, concat_axis=0, tiled=True)
     got_ids = wanted.reshape(pair_count)
-    got_terms = returned.reshape(pair_count, TILE * D)
-    select_rows = (jnp.arange(tile_dev, dtype=jnp.int32)[:, None] == got_ids[None, :]).astype(
-        jnp.bfloat16
-    )
-    owned = jnp.dot(select_rows, got_terms, preferred_element_type=jnp.float32)
-    owned = owned.reshape(tile_dev * TILE, D)
-    proxy_share = lax.psum_scatter(owned, "dp", scatter_dimension=1, tiled=True)
+    owned_t = owned_columns(got_ids, returned.reshape(pair_count, TILE, D), tile_dev)
+    proxy_share = lax.psum_scatter(owned_t, "dp", scatter_dimension=0, tiled=True).T
     return (loss.reshape(-1), embed_grad.reshape(-1, D), proxy_share)
 
 

time: 531 us -> 539 us (1.015)
  Pallas kernels: 36.9 us -> 74.1 us
  local copies, waits for them, and re-layouts: 33.8 us -> 11.6 us
  matrix products: 7.28 us -> 0 us
    pallas_call x0 -> x1, Pallas kernels: none -> 37.1 us  [owned_columns(): pl.pallas_call(_owned_kernel, grid_spec=grid_spec, out_shape=jax.ShapeDty...]
    reshape x2 -> x1, local copies, waits for them, and re-layouts: 13.6 us -> 0.1 us  [per_device(): got_ids = wanted.reshape(pair_count)]
    unnamed x17 -> x16, local copies, waits for them, and re-layouts: 12.6 us -> 3.07 us
    dot_general x1 -> x0, matrix products: 7.28 us -> none  [per_device(): owned = jnp.dot(select_rows, got_terms, preferred_element_type=jnp.float32)]
  transfers between devices with their start and end apart: 3 -> 3, of which waited for: 3 -> 3; matrix products, arithmetic and copies ran while one was open for 0% -> 1% of each run, Pallas kernels for 0% -> 0%
where the time goes in v4:
time: 539 us; the launch traced here: 538 us
  waiting for transfers between devices  418 us (78%)
  Pallas kernels  74.1 us (14%)
  between operations  14.2 us (3%)
  starting transfers between devices  13.6 us (3%)
  local copies, waits for them, and re-layouts  11.6 us (2%)
  other arithmetic  6.59 us (1%)
    all_to_all x1, waiting for transfers between devices, per_device(): lax.all_to_all(pair_grads, 'cls', split_axis=0, concat_axis=0, tiled=True)  189 us
    all_to_all x1, waiting for transfers between devices, per_device(): lax.all_to_all(outgoing, 'cls', split_axis=0, concat_axis=0, tiled=True)  186 us
    reduce_scatter x1, waiting for transfers between devices, per_device(): lax.psum_scatter(owned_t, 'dp', scatter_dimension=0, tiled=True)  42.6 us
    pallas_call x1, Pallas kernels, owned_columns(): pl.pallas_call(_owned_kernel, grid_spec=grid_spec, out_shape=jax.ShapeDty...  37.1 us
    pallas_call x1, Pallas kernels, block_step(): pl.pallas_call(_block_kernel, grid_spec=grid_spec, out_shape=[jax.ShapeDt...  22.6 us
    pallas_call x1, Pallas kernels, cls_all_to_all(): pl.pallas_call(functools.partial(_a2a_kernel, n), out_shape=jax.ShapeDtyp...  14.5 us
  transfers between devices with their start and end apart: 3, of which 3 were waited for; matrix products, arithmetic and copies ran while one was open for 1% of the time, Pallas kernels for 0%

profile of v4, /device:TPU:1, one launch (start us, length us, event | category | flops | bytes accessed | tf_op | source)
XLA Modules:
  0.0 538.1 jit_solution(10429212188185600582)
XLA Ops:
  7.2 0.0 copy-start
  7.2 0.8 sign_compare_fusion
  8.0 0.8 broadcast_remainder_fusion
  8.8 0.1 ne.51
  8.9 0.1 rem.30
  9.0 0.1 div.21
  9.1 0.2 select_reduce_fusion.1
  9.3 0.1 select_reduce_fusion
  9.4 0.8 gather_fusion
  10.2 0.7 reshape.151.src_ref
  10.9 14.5 %shard_map.76 = s32[32,2]{1,0:T(8,128)} custom-call(s32[32,2]{1,0:T(8,128)} %reshape.151.src_ref), custom_call_target="tpu_custom_call" | custom-call | tf_op jit(solution)/shard_map/pallas_call | solution.py:60
  25.4 0.7 compare_select_fusion
  26.1 0.1 reshape.168
  26.2 0.0 copy-done
  26.2 5.5 %gather_fusion.1 = bf16[64,128,512]{2,1,0:T(8,128)(2,1)} fusion(bf16[24,128,512]{2,1,0:T(8,128)(2,1)S(1)} %bitcast.14, s32[1024]{0:T(1024)S(1)} %pad_clamp_fusion), kind=kCustom, calls=%fused_computation.1 | custom fusion | bytes 16777472 | tf_op jit(solution)/shard_map/gather | solution.py:212
  31.8 7.4 %all-to-all-start = ((bf16[32,2,128,512]{3,2,1,0:T(8,128)(2,1)}), bf16[32,2,128,512]{3,2,1,0:T(8,128)(2,1)}, u32[]{:S(2)}, u32[]{:S(2)}) async-start(bf16[32,2,128,512]{3,2,1,0:T(8,128)(2,1)} %bitcast.16), calls=%async_computation | async-start | bytes 16777216 | tf_op jit(solution)/shard_map/all_to_all | solution.py:213
  39.1 1.0 copy.10
  40.2 0.1 multiply_reduce_fusion
  40.3 1.9 broadcast_subtract_fusion.pos_ref
  42.2 186.4 %all-to-all-done = bf16[32,2,128,512]{3,2,1,0:T(8,128)(2,1)} async-done(((bf16[32,2,128,512]{3,2,1,0:T(8,128)(2,1)}), bf16[32,2,128,512]{3,2,1,0:T(8,128)(2,1)}, u32[]{:S(2)}, u32[]{:S(2)}) %all-to-all-start) | async-done | bytes 8388640 | tf_op jit(solution)/shard_map/all_to_all | solution.py:213
  228.6 1.0 copy-done.1
  229.6 1.2 copy-done.2
  230.9 22.6 %shard_map.77 = (f32[8,128,1]{2,1,0:T(8,128)S(1)}, bf16[8,128,512]{2,1,0:T(8,128)(2,1)}, bf16[64,128,512]{2,1,0:T(8,128)(2,1)}) custom-call(s32[64]{0:T(128)S(1)} %multiply_add_fusion.slot_ref, s32[8]{0:T(128)S(1)} %copy-done.4, bf16[8,128,512]{2,1,0:T(8,128)(2,1)S(1)} %bitcast.15, s32[8,128,1]{2,1,0:T(8,128)S(1)} %copy-done.1, ...), custom_call_target="tpu_custom_call" | custom-call | tf_op jit(solution)/shard_map/pallas_call | solution.py:154
  253.5 0.8 copy-done.3
  254.2 6.1 %all-to-all-start.1 = ((bf16[32,2,128,512]{3,2,1,0:T(8,128)(2,1)}), bf16[32,2,128,512]{3,2,1,0:T(8,128)(2,1)}, u32[]{:S(2)}, u32[]{:S(2)}) async-start(bf16[32,2,128,512]{3,2,1,0:T(8,128)(2,1)} %bitcast.17), calls=%async_computation.1 | async-start | bytes 16777216 | tf_op jit(solution)/shard_map/all_to_all | solution.py:220
  260.4 0.0 reduce-scatter.2.cloned.1.call-start
  260.4 0.1 reshape.155.ids_ref
  260.6 189.1 %all-to-all-done.1 = bf16[32,2,128,512]{3,2,1,0:T(8,128)(2,1)} async-done(((bf16[32,2,128,512]{3,2,1,0:T(8,128)(2,1)}), bf16[32,2,128,512]{3,2,1,0:T(8,128)(2,1)}, u32[]{:S(2)}, u32[]{:S(2)}) %all-to-all-start.1) | async-done | bytes 8388640 | tf_op jit(solution)/shard_map/all_to_all | solution.py:220
  449.7 37.1 %shard_map.78 = f32[512,3072]{1,0:T(8,128)} custom-call(s32[64]{0:T(128)S(1)} %reshape.155.ids_ref, bf16[64,128,512]{2,1,0:T(8,128)(2,1)} %bitcast.9.grad_ref), custom_call_target="tpu_custom_call" | custom-call | tf_op jit(solution)/shard_map/pallas_call | solution.py:186
  486.8 0.0 reduce-scatter.2.cloned.1.call-update
  486.8 1.8 reduce.1
  488.6 42.6 %reduce-scatter.2.cloned.1.call-done = f32[64,3072]{1,0:T(8,128)} async-done(((f32[512,3072]{1,0:T(8,128)}), f32[64,3072]{1,0:T(8,128)}) %reduce-scatter.2.cloned.1.call-update) | async-done | bytes 786448 | tf_op jit(solution)/shard_map/reduce_scatter | solution.py:223
  (16 shorter events, 0.0 us)
Async XLA Ops:
  7.2 19.1 %copy-start = (bf16[3072,512]{1,0:T(8,128)(2,1)S(1)}, bf16[3072,512]{1,0:T(8,128)(2,1)}, u32[]{:S(2)}) copy-start(bf16[3072,512]{1,0:T(8,128)(2,1)} %param.6) | copy-start | bytes 9437188
  31.8 7.4 %copy-start.7 = (s32[1024]{0:T(1024)S(1)}, s32[1024]{0:T(1024)}, u32[]{:S(2)}) copy-start(s32[1024]{0:T(1024)} %param.9) | copy-start | bytes 12292
  31.8 8.4 %copy-start.6 = (s32[8,8]{1,0:T(8,128)S(1)}, s32[8,8]{1,0:T(8,128)}, u32[]{:S(2)}) copy-start(s32[8,8]{1,0:T(8,128)} %param.7) | copy-start | bytes 772
  31.8 196.8 %copy-start.4 = (s32[8]{0:T(128)S(1)}, s32[8]{0:T(128)}, u32[]{:S(2)}) copy-start(s32[8]{0:T(128)} %count_ref.1) | copy-start | bytes 100
  31.8 196.8 %all-to-all-start = ((bf16[32,2,128,512]{3,2,1,0:T(8,128)(2,1)}), bf16[32,2,128,512]{3,2,1,0:T(8,128)(2,1)}, u32[]{:S(2)}, u32[]{:S(2)}) async-start(bf16[32,2,128,512]{3,2,1,0:T(8,128)(2,1)} %bitcast.16), calls=%async_computation | async-start | bytes 16777216 | tf_op jit(solution)/shard_map/all_to_all | solution.py:213
  228.6 1.0 copy-start.1
  229.6 1.2 copy-start.2
  253.4 0.8 copy-start.3
  254.2 6.2 %copy-start.5 = (s32[32,2]{1,0:T(8,128)S(1)}, s32[32,2]{1,0:T(8,128)}, u32[]{:S(2)}) copy-start(s32[32,2]{1,0:T(8,128)} %shard_map.76) | copy-start | bytes 772
  254.2 195.5 %all-to-all-start.1 = ((bf16[32,2,128,512]{3,2,1,0:T(8,128)(2,1)}), bf16[32,2,128,512]{3,2,1,0:T(8,128)(2,1)}, u32[]{:S(2)}, u32[]{:S(2)}) async-start(bf16[32,2,128,512]{3,2,1,0:T(8,128)(2,1)} %bitcast.17), calls=%async_computation.1 | async-start | bytes 16777216 | tf_op jit(solution)/shard_map/all_to_all | solution.py:220
  260.4 270.8 %reduce-scatter.2.cloned.1.call-start = ((), (), s32[]{:S(2)}) async-start(), calls=%async_computation.3 | async-start | bytes 7077888 | tf_op jit(solution)/shard_map/reduce_scatter | solution.py:223
Sparse Core Ops, SparseCore 0:
  486.9 44.2 reduce-scatter.1

commit v5 on v4

--- a/solution.py
+++ b/solution.py
@@ -77,7 +77,7 @@
 
 def _block_kernel(slot_ref, count_ref, emb_ref, pos_ref, *rest):
     tiles = rest[:K]
-    loss_ref, grad_ref, pair_hbm, pair_buf, pair_sem = rest[K:]
+    loss_ref, grad_ref, pair_lo, pair_hi, pair_buf, pair_sem = rest[K:]
     b = pl.program_id(0)
     emb = emb_ref[0].astype(jnp.float32)
     inverse_norm = lax.rsqrt(jnp.sum(emb * emb, axis=1, keepdims=True) + epsilon)
@@ -116,10 +116,15 @@
             dscore, unit_rows, (((0,), (0,)), ((), ())), preferred_element_type=jnp.float32
         ).astype(jnp.bfloat16)
     copies = []
-    for k in range(K):
-        cp = pltpu.make_async_copy(pair_buf.at[k], pair_hbm.at[slot_ref[b * K + k]], pair_sem.at[k])
-        cp.start()
-        copies.append(cp)
+    half = TILE // 2
+    for k in range(K):
+        slot = slot_ref[b * K + k]
+        for h, dst in enumerate((pair_lo, pair_hi)):
+            cp = pltpu.make_async_copy(
+                pair_buf.at[k, pl.ds(h * half, half)], dst.at[slot], pair_sem.at[k, h]
+            )
+            cp.start()
+            copies.append(cp)
     radial = jnp.sum(unit_exact * grad_unit, axis=1, keepdims=True)
     grad_ref[0] = ((grad_unit - unit_exact * radial) * inverse_norm).astype(grad_ref.dtype)
     for cp in copies:
@@ -145,10 +150,11 @@
             pl.BlockSpec((1, BR, 1), lambda b, slot, cnt: (b, 0, 0)),
             pl.BlockSpec((1, BR, D), lambda b, slot, cnt: (b, 0, 0)),
             pl.BlockSpec(memory_space=pl.ANY),
+            pl.BlockSpec(memory_space=pl.ANY),
         ],
         scratch_shapes=[
             pltpu.VMEM((K, TILE, D), jnp.bfloat16),
-            pltpu.SemaphoreType.DMA((K,)),
+            pltpu.SemaphoreType.DMA((K, 2)),
         ],
     )
     return pl.pallas_call(
@@ -157,7 +163,8 @@
         out_shape=[
             jax.ShapeDtypeStruct((blocks, BR, 1), jnp.float32),
             jax.ShapeDtypeStruct((blocks, BR, D), jnp.bfloat16),
-            jax.ShapeDtypeStruct((pairs, TILE, D), jnp.bfloat16),
+            jax.ShapeDtypeStruct((pairs, TILE // 2, D), jnp.bfloat16),
+            jax.ShapeDtypeStruct((pairs, TILE // 2, D), jnp.bfloat16),
         ],
         compiler_params=pltpu.CompilerParams(vmem_limit_bytes=48 * 1024 * 1024),
     )(slot_of, tile_count, emb_blocks, pos_cols, *([fetched] * K))
@@ -170,23 +177,23 @@
     def _():
         out_ref[...] = jnp.zeros_like(out_ref)
 
-    start = pl.multiple_of(ids_ref[s] * TILE, TILE)
-    columns = pl.ds(start, TILE)
-    out_ref[:, columns] += grad_ref[0].astype(jnp.float32).T
-
-
-def owned_columns(got_ids, returned, tile_dev):
-    pairs = returned.shape[0]
+    rows = grad_ref.shape[1]
+    start = pl.multiple_of(ids_ref[s] * rows, rows)
+    out_ref[pl.ds(start, rows), :] += grad_ref[0].astype(jnp.float32)
+
+
+def owned_rows(got_ids, returned, tile_dev):
+    pairs, rows, _ = returned.shape
     grid_spec = pltpu.PrefetchScalarGridSpec(
         num_scalar_prefetch=1,
         grid=(pairs,),
-        in_specs=[pl.BlockSpec((1, TILE, D), lambda s, ids: (s, 0, 0))],
-        out_specs=pl.BlockSpec((D, tile_dev * TILE), lambda s, ids: (0, 0)),
+        in_specs=[pl.BlockSpec((1, rows, D), lambda s, ids: (s, 0, 0))],
+        out_specs=pl.BlockSpec((tile_dev * rows, D), lambda s, ids: (0, 0)),
     )
     return pl.pallas_call(
         _owned_kernel,
         grid_spec=grid_spec,
-        out_shape=jax.ShapeDtypeStruct((D, tile_dev * TILE), jnp.float32),
+        out_shape=jax.ShapeDtypeStruct((tile_dev * rows, D), jnp.float32),
         compiler_params=pltpu.CompilerParams(vmem_limit_bytes=48 * 1024 * 1024),
     )(got_ids, returned)
 
@@ -213,14 +220,18 @@
     fetched = lax.all_to_all(outgoing, "cls", split_axis=0, concat_axis=0, tiled=True)
     fetched = fetched.reshape(pair_count, TILE, D)
     pos_cols = labels.reshape(blocks, BR, 1) - hard_tiles[:, 0:1, None] * TILE
-    loss, embed_grad, pair_grads = block_step(
+    loss, embed_grad, pair_lo, pair_hi = block_step(
         slot_of, tile_count, embeddings.reshape(blocks, BR, D), pos_cols, fetched
     )
-    pair_grads = pair_grads.reshape(groups, capacity, TILE, D)
-    returned = lax.all_to_all(pair_grads, "cls", split_axis=0, concat_axis=0, tiled=True)
     got_ids = wanted.reshape(pair_count)
-    owned_t = owned_columns(got_ids, returned.reshape(pair_count, TILE, D), tile_dev)
-    proxy_share = lax.psum_scatter(owned_t, "dp", scatter_dimension=0, tiled=True).T
+    shares = []
+    for part in (pair_lo, pair_hi):
+        part = part.reshape(groups, capacity, TILE // 2, D)
+        returned = lax.all_to_all(part, "cls", split_axis=0, concat_axis=0, tiled=True)
+        owned = owned_rows(got_ids, returned.reshape(pair_count, TILE // 2, D), tile_dev)
+        share = lax.psum_scatter(owned, "dp", scatter_dimension=1, tiled=True)
+        shares.append(share.reshape(tile_dev, 1, TILE // 2, -1))
+    proxy_share = jnp.concatenate(shares, axis=1).reshape(tile_dev * TILE, -1)
     return (loss.reshape(-1), embed_grad.reshape(-1, D), proxy_share)
 
 

time: 539 us -> 547 us (1.015)
  waiting for transfers between devices: 418 us -> 277 us
  blocking collectives: 0 us -> 98.9 us
  local copies, waits for them, and re-layouts: 11.6 us -> 33.1 us
  Pallas kernels: 74.1 us -> 93.7 us
    all_to_all x1, waiting for transfers between devices: 189 us -> 58.7 us  [per_device(): lax.all_to_all(part, 'cls', split_axis=0, concat_axis=0, tiled=True)]
    all_to_all x0 -> x1, blocking collectives: none -> 98.9 us  [per_device(): lax.all_to_all(part, 'cls', split_axis=0, concat_axis=0, tiled=True)]
    reduce_scatter x1 -> x0, waiting for transfers between devices: 42.6 us -> none  [per_device(): lax.psum_scatter(owned_t, 'dp', scatter_dimension=0, tiled=True)]
    unnamed x1 -> x4, waiting for transfers between devices: 0.02 us -> 32 us
    pallas_call x1 -> x2, Pallas kernels: 37.1 us -> 57.1 us  [owned_rows(): pl.pallas_call(_owned_kernel, grid_spec=grid_spec, out_shape=jax.ShapeDty...]
    unnamed x16 -> x24, local copies, waits for them, and re-layouts: 3.07 us -> 17 us
  transfers between devices with their start and end apart: 3 -> 4, of which waited for: 3 -> 3; matrix products, arithmetic and copies ran while one was open for 1% -> 3% of each run, Pallas kernels for 0% -> 11%
where the time goes in v5:
time: 547 us; the launch traced here: 541 us
  waiting for transfers between devices  277 us (51%)
  blocking collectives  98.9 us (18%)
  Pallas kernels  93.7 us (17%)
  local copies, waits for them, and re-layouts  33.1 us (6%)
  starting transfers between devices  14.5 us (3%)
  between operations  14.2 us (3%)
  other arithmetic  9.31 us (2%)
    all_to_all x1, waiting for transfers between devices, per_device(): lax.all_to_all(outgoing, 'cls', split_axis=0, concat_axis=0, tiled=True)  186 us
    all_to_all x1, blocking collectives, per_device(): lax.all_to_all(part, 'cls', split_axis=0, concat_axis=0, tiled=True)  98.9 us
    all_to_all x1, waiting for transfers between devices, per_device(): lax.all_to_all(part, 'cls', split_axis=0, concat_axis=0, tiled=True)  58.7 us
    pallas_call x2, Pallas kernels, owned_rows(): pl.pallas_call(_owned_kernel, grid_spec=grid_spec, out_shape=jax.ShapeDty...  57.1 us
    unnamed x4, waiting for transfers between devices  32 us
    pallas_call x1, Pallas kernels, block_step(): pl.pallas_call(_block_kernel, grid_spec=grid_spec, out_shape=[jax.ShapeDt...  22.1 us
    unnamed x24, local copies, waits for them, and re-layouts  17 us
    pallas_call x1, Pallas kernels, cls_all_to_all(): pl.pallas_call(functools.partial(_a2a_kernel, n), out_shape=jax.ShapeDtyp...  14.5 us
  transfers between devices with their start and end apart: 4, of which 3 were waited for; matrix products, arithmetic and copies ran while one was open for 3% of the time, Pallas kernels for 11%

profile of v5, /device:TPU:1, one launch (start us, length us, event | category | flops | bytes accessed | tf_op | source)
XLA Modules:
  0.0 540.8 jit_solution(351826010786584222)
XLA Ops:
  7.2 0.8 sign_compare_fusion
  8.0 0.8 broadcast_remainder_fusion
  9.1 0.2 select_reduce_fusion.1
  9.4 0.8 gather_fusion
  10.2 0.7 reshape.166.src_ref
  10.9 14.5 %shard_map.76 = s32[32,2]{1,0:T(8,128)} custom-call(s32[32,2]{1,0:T(8,128)} %reshape.166.src_ref), custom_call_target="tpu_custom_call" | custom-call | tf_op jit(solution)/shard_map/pallas_call | solution.py:60
  25.4 0.7 compare_select_fusion
  26.2 5.5 %gather_fusion.1 = bf16[64,128,512]{2,1,0:T(8,128)(2,1)} fusion(bf16[24,128,512]{2,1,0:T(8,128)(2,1)S(1)} %bitcast.23, s32[1024]{0:T(1024)S(1)} %pad_clamp_fusion), kind=kCustom, calls=%fused_computation.1 | custom fusion | bytes 16777472 | tf_op jit(solution)/shard_map/gather | solution.py:219
  31.8 7.3 %all-to-all-start = ((bf16[32,2,128,512]{3,2,1,0:T(8,128)(2,1)}), bf16[32,2,128,512]{3,2,1,0:T(8,128)(2,1)}, u32[]{:S(2)}, u32[]{:S(2)}) async-start(bf16[32,2,128,512]{3,2,1,0:T(8,128)(2,1)} %bitcast.25), calls=%async_computation | async-start | bytes 16777216 | tf_op jit(solution)/shard_map/all_to_all | solution.py:220
  39.1 1.0 copy.15
  40.2 0.1 multiply_reduce_fusion
  40.3 1.9 broadcast_subtract_fusion.pos_ref
  42.2 186.4 %all-to-all-done = bf16[32,2,128,512]{3,2,1,0:T(8,128)(2,1)} async-done(((bf16[32,2,128,512]{3,2,1,0:T(8,128)(2,1)}), bf16[32,2,128,512]{3,2,1,0:T(8,128)(2,1)}, u32[]{:S(2)}, u32[]{:S(2)}) %all-to-all-start) | async-done | bytes 8388640 | tf_op jit(solution)/shard_map/all_to_all | solution.py:220
  228.6 1.0 copy-done.3
  229.7 1.2 copy-done.4
  230.9 22.1 %shard_map.77 = (f32[8,128,1]{2,1,0:T(8,128)S(1)}, bf16[8,128,512]{2,1,0:T(8,128)(2,1)}, bf16[64,64,512]{2,1,0:T(8,128)(2,1)}, bf16[64,64,512]{2,1,0:T(8,128)(2,1)}) custom-call(s32[64]{0:T(128)S(1)} %multiply_add_fusion.slot_ref, s32[8]{0:T(128)S(1)} %copy-done.6, bf16[8,128,512]{2,1,0:T(8,128)(2,1)S(1)} %bitcast.24, s32[8,128,1]{2,1,0:T(8,128)S(1)} %copy-done.3, ...), custom_call_target="tpu_custom_call" | custom-call | tf_op jit(solution)/shard_map/pallas_call | solution.py:160
  253.1 98.9 %all_to_all.15 = bf16[32,2,64,512]{3,2,1,0:T(8,128)(2,1)} all-to-all(bf16[32,2,64,512]{3,2,1,0:T(8,128)(2,1)} %bitcast.30), channel_id=1, replica_groups=mesh['dp'=8,'cls'=32] {'cls'}, dimensions={0} | all-to-all | bytes 8388608 | tf_op jit(solution)/shard_map/all_to_all | solution.py:230
  352.0 7.1 %all-to-all-start.1 = ((bf16[32,2,64,512]{3,2,1,0:T(8,128)(2,1)}), bf16[32,2,64,512]{3,2,1,0:T(8,128)(2,1)}, u32[]{:S(2)}, u32[]{:S(2)}) async-start(bf16[32,2,64,512]{3,2,1,0:T(8,128)(2,1)} %bitcast.29), calls=%async_computation.1 | async-start | bytes 8388608 | tf_op jit(solution)/shard_map/all_to_all | solution.py:230
  359.2 28.6 %shard_map.79 = f32[1536,512]{1,0:T(8,128)S(1)} custom-call(s32[64]{0:T(128)S(1)} %reshape.170.ids_ref, bf16[64,64,512]{2,1,0:T(8,128)(2,1)} %bitcast.26), custom_call_target="tpu_custom_call" | custom-call | tf_op jit(solution)/shard_map/pallas_call | solution.py:193
  387.8 1.6 copy-done.2
  389.4 3.6 copy.20
  393.1 58.7 %all-to-all-done.1 = bf16[32,2,64,512]{3,2,1,0:T(8,128)(2,1)} async-done(((bf16[32,2,64,512]{3,2,1,0:T(8,128)(2,1)}), bf16[32,2,64,512]{3,2,1,0:T(8,128)(2,1)}, u32[]{:S(2)}, u32[]{:S(2)}) %all-to-all-start.1) | async-done | bytes 4194336 | tf_op jit(solution)/shard_map/all_to_all | solution.py:230
  451.8 28.5 %shard_map.78 = f32[1536,512]{1,0:T(8,128)S(1)} custom-call(s32[64]{0:T(128)S(1)} %reshape.170.ids_ref, bf16[64,64,512]{2,1,0:T(8,128)(2,1)} %bitcast.13.grad_ref), custom_call_target="tpu_custom_call" | custom-call | tf_op jit(solution)/shard_map/pallas_call | solution.py:193
  480.4 1.7 copy-done.1
  482.1 3.5 copy.18
  485.6 1.8 reduce.1
  487.5 2.1 copy.21
  489.6 31.9 %reduce-scatter.7.cloned.1.call-done = f32[64,1536]{1,0:T(8,128)} async-done(((f32[512,1536]{1,0:T(8,128)}), f32[64,1536]{1,0:T(8,128)}) %reduce-scatter.7.cloned.1.call-update) | async-done | bytes 393232
  521.5 2.2 copy.19
  523.7 2.7 pad_maximum_fusion
  526.4 3.8 copy.17
  530.2 3.7 reshape.177
  (32 shorter events, 0.7 us)
Async XLA Ops:
  7.2 19.1 %copy-start = (bf16[3072,512]{1,0:T(8,128)(2,1)S(1)}, bf16[3072,512]{1,0:T(8,128)(2,1)}, u32[]{:S(2)}) copy-start(bf16[3072,512]{1,0:T(8,128)(2,1)} %param.6) | copy-start | bytes 9437188
  31.8 7.4 %copy-start.9 = (s32[1024]{0:T(1024)S(1)}, s32[1024]{0:T(1024)}, u32[]{:S(2)}) copy-start(s32[1024]{0:T(1024)} %param.9) | copy-start | bytes 12292
  31.8 8.4 %copy-start.8 = (s32[8,8]{1,0:T(8,128)S(1)}, s32[8,8]{1,0:T(8,128)}, u32[]{:S(2)}) copy-start(s32[8,8]{1,0:T(8,128)} %param.7) | copy-start | bytes 772
  31.8 196.9 %copy-start.6 = (s32[8]{0:T(128)S(1)}, s32[8]{0:T(128)}, u32[]{:S(2)}) copy-start(s32[8]{0:T(128)} %count_ref.1) | copy-start | bytes 100
  31.8 196.9 %all-to-all-start = ((bf16[32,2,128,512]{3,2,1,0:T(8,128)(2,1)}), bf16[32,2,128,512]{3,2,1,0:T(8,128)(2,1)}, u32[]{:S(2)}, u32[]{:S(2)}) async-start(bf16[32,2,128,512]{3,2,1,0:T(8,128)(2,1)} %bitcast.25), calls=%async_computation | async-start | bytes 16777216 | tf_op jit(solution)/shard_map/all_to_all | solution.py:220
  228.6 1.0 copy-start.3
  229.7 1.2 copy-start.4
  253.0 99.0 %copy-start.5 = (f32[8,128,1]{2,1,0:T(8,128)}, f32[8,128,1]{2,1,0:T(8,128)S(1)}, u32[]{:S(2)}) copy-start(f32[8,128,1]{2,1,0:T(8,128)S(1)} %get-tuple-element.7) | copy-start | bytes 12292
  352.0 7.1 %copy-start.7 = (s32[32,2]{1,0:T(8,128)S(1)}, s32[32,2]{1,0:T(8,128)}, u32[]{:S(2)}) copy-start(s32[32,2]{1,0:T(8,128)} %shard_map.76) | copy-start | bytes 772
  352.0 99.8 %all-to-all-start.1 = ((bf16[32,2,64,512]{3,2,1,0:T(8,128)(2,1)}), bf16[32,2,64,512]{3,2,1,0:T(8,128)(2,1)}, u32[]{:S(2)}, u32[]{:S(2)}) async-start(bf16[32,2,64,512]{3,2,1,0:T(8,128)(2,1)} %bitcast.29), calls=%async_computation.1 | async-start | bytes 8388608 | tf_op jit(solution)/shard_map/all_to_all | solution.py:230
  359.1 128.4 %reduce-scatter.9.cloned.1.call-start = ((), (), s32[]{:S(2)}) async-start(), calls=%async_computation.6 | async-start | bytes 3538944
  387.8 1.6 copy-start.2
  393.0 128.5 %reduce-scatter.7.cloned.1.call-start = ((), (), s32[]{:S(2)}) async-start(), calls=%async_computation.5 | async-start | bytes 3538944
  480.3 1.7 copy-start.1
Sparse Core Ops, SparseCore 0:
  393.1 39.4 reduce-scatter.8
  485.7 35.7 reduce-scatter.6

commit v6 on v3

--- a/solution.py
+++ b/solution.py
@@ -196,8 +196,9 @@
         jnp.bfloat16
     )
     owned = jnp.dot(select_rows, got_terms, preferred_element_type=jnp.float32)
-    owned = owned.reshape(tile_dev * TILE, D)
+    owned = owned.astype(jnp.bfloat16).reshape(tile_dev * TILE, D)
     proxy_share = lax.psum_scatter(owned, "dp", scatter_dimension=1, tiled=True)
+    proxy_share = proxy_share.astype(jnp.float32)
     return (loss.reshape(-1), embed_grad.reshape(-1, D), proxy_share)
 
 

time: 531 us -> 527 us (level)
  waiting for transfers between devices: 420 us -> 409 us
    reduce_scatter x1, waiting for transfers between devices: 42.2 us -> 33.4 us  [per_device(): proxy_share = lax.psum_scatter(owned, 'dp', scatter_dimension=1, tiled=True)]
  transfers between devices with their start and end apart: 3 -> 3, of which waited for: 3 -> 3; matrix products, arithmetic and copies ran while one was open for 0% -> 1% of each run, Pallas kernels for 0% -> 0%
where the time goes in v6:
time: 527 us; the launch traced here: 524 us
  waiting for transfers between devices  409 us (78%)
  Pallas kernels  37 us (7%)
  local copies, waits for them, and re-layouts  33.1 us (6%)
  starting transfers between devices  16.2 us (3%)
  between operations  14.2 us (3%)
  other arithmetic  8.51 us (2%)
  matrix products  6.24 us (1%)
    all_to_all x1, waiting for transfers between devices, per_device(): lax.all_to_all(pair_grads, 'cls', split_axis=0, concat_axis=0, tiled=True)  190 us
    all_to_all x1, waiting for transfers between devices, per_device(): lax.all_to_all(outgoing, 'cls', split_axis=0, concat_axis=0, tiled=True)  185 us
    reduce_scatter x1, waiting for transfers between devices, per_device(): proxy_share = lax.psum_scatter(owned, 'dp', scatter_dimension=1, tiled=True)  33.4 us
    pallas_call x1, Pallas kernels, block_step(): pl.pallas_call(_block_kernel, grid_spec=grid_spec, out_shape=[jax.ShapeDt...  22.6 us
    unnamed x17, local copies, waits for them, and re-layouts  14.8 us
    pallas_call x1, Pallas kernels, cls_all_to_all(): pl.pallas_call(functools.partial(_a2a_kernel, n), out_shape=jax.ShapeDtyp...  14.4 us
  transfers between devices with their start and end apart: 3, of which 3 were waited for; matrix products, arithmetic and copies ran while one was open for 1% of the time, Pallas kernels for 0%

profile of v6, /device:TPU:1, one launch (start us, length us, event | category | flops | bytes accessed | tf_op | source)
XLA Modules:
  0.0 524.0 jit_solution(10745223934080088380)
XLA Ops:
  7.2 0.8 sign_compare_fusion
  8.0 0.8 broadcast_remainder_fusion
  8.8 0.1 ne.51
  8.9 0.1 rem.30
  9.1 0.2 select_reduce_fusion.1
  9.3 0.1 select_reduce_fusion
  9.4 0.8 gather_fusion
  10.2 0.7 reshape.152.src_ref
  10.9 14.4 %shard_map.76 = s32[32,2]{1,0:T(8,128)} custom-call(s32[32,2]{1,0:T(8,128)} %reshape.152.src_ref), custom_call_target="tpu_custom_call" | custom-call | tf_op jit(solution)/shard_map/pallas_call | solution.py:60
  25.4 0.7 compare_select_fusion
  26.1 0.1 reshape.169
  26.2 5.5 %gather_fusion.1 = bf16[64,128,512]{2,1,0:T(8,128)(2,1)} fusion(bf16[24,128,512]{2,1,0:T(8,128)(2,1)S(1)} %bitcast.16, s32[1024]{0:T(1024)S(1)} %pad_clamp_fusion), kind=kCustom, calls=%fused_computation.1 | custom fusion | bytes 16777472 | tf_op jit(solution)/shard_map/gather | solution.py:184
  31.8 7.2 %all-to-all-start = ((bf16[32,2,128,512]{3,2,1,0:T(8,128)(2,1)}), bf16[32,2,128,512]{3,2,1,0:T(8,128)(2,1)}, u32[]{:S(2)}, u32[]{:S(2)}) async-start(bf16[32,2,128,512]{3,2,1,0:T(8,128)(2,1)} %bitcast.18), calls=%async_computation | async-start | bytes 16777216 | tf_op jit(solution)/shard_map/all_to_all | solution.py:185
  39.0 1.0 copy.13
  40.0 0.1 multiply_reduce_fusion
  40.1 1.9 broadcast_subtract_fusion.pos_ref
  42.1 185.0 %all-to-all-done = bf16[32,2,128,512]{3,2,1,0:T(8,128)(2,1)} async-done(((bf16[32,2,128,512]{3,2,1,0:T(8,128)(2,1)}), bf16[32,2,128,512]{3,2,1,0:T(8,128)(2,1)}, u32[]{:S(2)}, u32[]{:S(2)}) %all-to-all-start) | async-done | bytes 8388640 | tf_op jit(solution)/shard_map/all_to_all | solution.py:185
  227.1 1.0 copy-done.1
  228.1 1.2 copy-done.2
  229.4 22.6 %shard_map.77 = (f32[8,128,1]{2,1,0:T(8,128)S(1)}, bf16[8,128,512]{2,1,0:T(8,128)(2,1)}, bf16[64,128,512]{2,1,0:T(8,128)(2,1)}) custom-call(s32[64]{0:T(128)S(1)} %multiply_add_fusion.slot_ref, s32[8]{0:T(128)S(1)} %copy-done.4, bf16[8,128,512]{2,1,0:T(8,128)(2,1)S(1)} %bitcast.17, s32[8,128,1]{2,1,0:T(8,128)S(1)} %copy-done.1, ...), custom_call_target="tpu_custom_call" | custom-call | tf_op jit(solution)/shard_map/pallas_call | solution.py:154
  252.0 0.8 copy-done.3
  252.8 8.7 %all-to-all-start.1 = ((bf16[32,2,128,512]{3,2,1,0:T(8,128)(2,1)}), bf16[32,2,128,512]{3,2,1,0:T(8,128)(2,1)}, u32[]{:S(2)}, u32[]{:S(2)}) async-start(bf16[32,2,128,512]{3,2,1,0:T(8,128)(2,1)} %bitcast.20), calls=%async_computation.1 | async-start | bytes 16777216 | tf_op jit(solution)/shard_map/all_to_all | solution.py:192
  261.5 0.2 reduce-scatter.2.cloned.1.call-start
  261.8 0.1 eq.47
  261.9 190.2 %all-to-all-done.1 = bf16[32,2,128,512]{3,2,1,0:T(8,128)(2,1)} async-done(((bf16[32,2,128,512]{3,2,1,0:T(8,128)(2,1)}), bf16[32,2,128,512]{3,2,1,0:T(8,128)(2,1)}, u32[]{:S(2)}, u32[]{:S(2)}) %all-to-all-start.1) | async-done | bytes 8388640 | tf_op jit(solution)/shard_map/all_to_all | solution.py:192
  452.1 11.8 %copy.16 = bf16[8,8,128,512]{3,1,2,0:T(8,128)(2,1)} copy(bf16[8,8,128,512]{3,2,1,0:T(8,128)(2,1)} %bitcast.11) | data formatting | bytes 16777216
  463.9 6.2 %convolution_convert_fusion = bf16[24,65536]{1,0:T(8,128)(2,1)} fusion(bf16[64,65536]{1,0:T(8,128)(2,1)} %bitcast.19, s32[64]{0:T(128)S(1)} %eq.47), kind=kOutput, calls=%fused_computation.2 | convolution fusion | flops 202900992 | bytes 11534592 | tf_op jit(solution)/shard_map/dot_general | solution.py:198
  470.1 5.2 reshape.158
  475.3 4.7 copy.15
  479.9 1.8 reduce.1
  481.8 33.4 %reduce-scatter.2.cloned.1.call-done = bf16[3072,64]{0,1:T(8,128)(2,1)} async-done(((bf16[3072,512]{0,1:T(8,128)(2,1)}), bf16[3072,64]{0,1:T(8,128)(2,1)}) %reduce-scatter.2.cloned.1.call-update) | async-done | bytes 393232 | tf_op jit(solution)/shard_map/reduce_scatter | solution.py:200
  515.2 1.9 convert_element_type.8
  (20 shorter events, 0.2 us)
Async XLA Ops:
  7.2 19.1 %copy-start = (bf16[3072,512]{1,0:T(8,128)(2,1)S(1)}, bf16[3072,512]{1,0:T(8,128)(2,1)}, u32[]{:S(2)}) copy-start(bf16[3072,512]{1,0:T(8,128)(2,1)} %param.6) | copy-start | bytes 9437188
  31.7 7.2 %copy-start.7 = (s32[1024]{0:T(1024)S(1)}, s32[1024]{0:T(1024)}, u32[]{:S(2)}) copy-start(s32[1024]{0:T(1024)} %param.9) | copy-start | bytes 12292
  31.7 8.3 %copy-start.6 = (s32[8,8]{1,0:T(8,128)S(1)}, s32[8,8]{1,0:T(8,128)}, u32[]{:S(2)}) copy-start(s32[8,8]{1,0:T(8,128)} %param.7) | copy-start | bytes 772
  31.7 195.3 %copy-start.4 = (s32[8]{0:T(128)S(1)}, s32[8]{0:T(128)}, u32[]{:S(2)}) copy-start(s32[8]{0:T(128)} %count_ref.1) | copy-start | bytes 100
  31.8 195.3 %all-to-all-start = ((bf16[32,2,128,512]{3,2,1,0:T(8,128)(2,1)}), bf16[32,2,128,512]{3,2,1,0:T(8,128)(2,1)}, u32[]{:S(2)}, u32[]{:S(2)}) async-start(bf16[32,2,128,512]{3,2,1,0:T(8,128)(2,1)} %bitcast.18), calls=%async_computation | async-start | bytes 16777216 | tf_op jit(solution)/shard_map/all_to_all | solution.py:185
  227.1 1.0 copy-start.1
  228.1 1.2 copy-start.2
  252.0 0.8 copy-start.3
  252.8 9.0 %copy-start.5 = (s32[32,2]{1,0:T(8,128)S(1)}, s32[32,2]{1,0:T(8,128)}, u32[]{:S(2)}) copy-start(s32[32,2]{1,0:T(8,128)} %shard_map.76) | copy-start | bytes 772
  252.8 199.3 %all-to-all-start.1 = ((bf16[32,2,128,512]{3,2,1,0:T(8,128)(2,1)}), bf16[32,2,128,512]{3,2,1,0:T(8,128)(2,1)}, u32[]{:S(2)}, u32[]{:S(2)}) async-start(bf16[32,2,128,512]{3,2,1,0:T(8,128)(2,1)} %bitcast.20), calls=%async_computation.1 | async-start | bytes 16777216 | tf_op jit(solution)/shard_map/all_to_all | solution.py:192
  261.5 253.7 %reduce-scatter.2.cloned.1.call-start = ((), (), s32[]{:S(2)}) async-start(), calls=%async_computation.3 | async-start | bytes 3538944 | tf_op jit(solution)/shard_map/reduce_scatter | solution.py:200
Sparse Core Ops, SparseCore 0:
  480.1 35.0 reduce-scatter.1

commit v7 on v3

--- a/solution.py
+++ b/solution.py
@@ -112,12 +112,17 @@
         cand = tiles[k][0]
         terms = jnp.dot(dscore, cand, preferred_element_type=jnp.float32)
         grad_unit = grad_unit + terms.astype(jnp.bfloat16).astype(jnp.float32)
-        pair_buf[k] = lax.dot_general(
-            dscore, unit_rows, (((0,), (0,)), ((), ())), preferred_element_type=jnp.float32
+        pair_t = lax.dot_general(
+            unit_rows, dscore, (((0,), (0,)), ((), ())), preferred_element_type=jnp.float32
         ).astype(jnp.bfloat16)
+        pair_buf[:, k] = pair_t.reshape(pair_buf.shape[0], D // pair_buf.shape[0], TILE)
     copies = []
     for k in range(K):
-        cp = pltpu.make_async_copy(pair_buf.at[k], pair_hbm.at[slot_ref[b * K + k]], pair_sem.at[k])
+        cp = pltpu.make_async_copy(
+            pair_buf.at[:, pl.ds(k, 1)],
+            pair_hbm.at[:, pl.ds(slot_ref[b * K + k], 1)],
+            pair_sem.at[k],
+        )
         cp.start()
         copies.append(cp)
     radial = jnp.sum(unit_exact * grad_unit, axis=1, keepdims=True)
@@ -126,7 +131,7 @@
         cp.wait()
 
 
-def block_step(slot_of, tile_count, emb_blocks, pos_cols, fetched):
+def block_step(slot_of, tile_count, emb_blocks, pos_cols, fetched, parts):
     blocks = emb_blocks.shape[0]
     pairs = fetched.shape[0]
 
@@ -147,7 +152,7 @@
             pl.BlockSpec(memory_space=pl.ANY),
         ],
         scratch_shapes=[
-            pltpu.VMEM((K, TILE, D), jnp.bfloat16),
+            pltpu.VMEM((parts, K, D // parts, TILE), jnp.bfloat16),
             pltpu.SemaphoreType.DMA((K,)),
         ],
     )
@@ -157,7 +162,7 @@
         out_shape=[
             jax.ShapeDtypeStruct((blocks, BR, 1), jnp.float32),
             jax.ShapeDtypeStruct((blocks, BR, D), jnp.bfloat16),
-            jax.ShapeDtypeStruct((pairs, TILE, D), jnp.bfloat16),
+            jax.ShapeDtypeStruct((parts, pairs, D // parts, TILE), jnp.bfloat16),
         ],
         compiler_params=pltpu.CompilerParams(vmem_limit_bytes=48 * 1024 * 1024),
     )(slot_of, tile_count, emb_blocks, pos_cols, *([fetched] * K))
@@ -185,19 +190,19 @@
     fetched = lax.all_to_all(outgoing, "cls", split_axis=0, concat_axis=0, tiled=True)
     fetched = fetched.reshape(pair_count, TILE, D)
     pos_cols = labels.reshape(blocks, BR, 1) - hard_tiles[:, 0:1, None] * TILE
+    parts = lax.axis_size("dp")
     loss, embed_grad, pair_grads = block_step(
-        slot_of, tile_count, embeddings.reshape(blocks, BR, D), pos_cols, fetched
-    )
-    pair_grads = pair_grads.reshape(groups, capacity, TILE, D)
-    returned = lax.all_to_all(pair_grads, "cls", split_axis=0, concat_axis=0, tiled=True)
-    got_ids = wanted.reshape(pair_count)
-    got_terms = returned.reshape(pair_count, TILE * D)
+        slot_of, tile_count, embeddings.reshape(blocks, BR, D), pos_cols, fetched, parts
+    )
+    pair_grads = pair_grads.reshape(parts * groups, capacity, D // parts, TILE)
+    returned = lax.all_to_all(pair_grads, ("dp", "cls"), split_axis=0, concat_axis=0, tiled=True)
+    got_ids = lax.all_gather(wanted, "dp").reshape(parts * pair_count)
+    got_terms = returned.reshape(parts * pair_count, D // parts, TILE)
     select_rows = (jnp.arange(tile_dev, dtype=jnp.int32)[:, None] == got_ids[None, :]).astype(
         jnp.bfloat16
     )
-    owned = jnp.dot(select_rows, got_terms, preferred_element_type=jnp.float32)
-    owned = owned.reshape(tile_dev * TILE, D)
-    proxy_share = lax.psum_scatter(owned, "dp", scatter_dimension=1, tiled=True)
+    owned = jnp.einsum("tp,pdc->tcd", select_rows, got_terms, preferred_element_type=jnp.float32)
+    proxy_share = owned.reshape(tile_dev * TILE, D // parts)
     return (loss.reshape(-1), embed_grad.reshape(-1, D), proxy_share)
 
 

time: 531 us -> 464 us (0.87)
  waiting for transfers between devices: 420 us -> 353 us
  blocking collectives: 0 us -> 17.6 us
  between operations: 14.2 us -> 0.77 us
  local copies, waits for them, and re-layouts: 33.8 us -> 25.1 us
  starting transfers between devices: 13.8 us -> 21.5 us
  matrix products: 7.28 us -> 1.19 us
    reduce_scatter x1 -> x0, waiting for transfers between devices: 42.2 us -> none  [per_device(): proxy_share = lax.psum_scatter(owned, 'dp', scatter_dimension=1, tiled=True)]
    all_to_all x1, waiting for transfers between devices: 189 us -> 168 us  [per_device(): lax.all_to_all(pair_grads, ('dp', 'cls'), split_axis=0, concat_axis=0, ti...]
    all_gather x0 -> x1, blocking collectives: none -> 17.6 us  [per_device(): got_ids = lax.all_gather(wanted, 'dp').reshape(parts * pair_count)]
    reshape x2 -> x0, local copies, waits for them, and re-layouts: 13.6 us -> none  [per_device(): owned = owned.reshape(tile_dev * TILE, D)]
    all_to_all x0 -> x1, local copies, waits for them, and re-layouts: none -> 12.3 us  [per_device(): lax.all_to_all(pair_grads, ('dp', 'cls'), split_axis=0, concat_axis=0, ti...]
    unnamed x17, local copies, waits for them, and re-layouts: 12.6 us -> 4.11 us
    all_to_all x1, starting transfers between devices: 6.17 us -> 14.3 us  [per_device(): lax.all_to_all(pair_grads, ('dp', 'cls'), split_axis=0, concat_axis=0, ti...]
    dot_general x1, matrix products: 7.28 us -> 1.19 us  [per_device(): jnp.einsum('tp,pdc->tcd', select_rows, got_terms, preferred_element_type=...]
  transfers between devices with their start and end apart: 3 -> 2, of which waited for: 3 -> 2; matrix products, arithmetic and copies ran while one was open for 0% -> 1% of each run, Pallas kernels for 0% -> 0%
where the time goes in v7:
time: 464 us
  waiting for transfers between devices  353 us (76%)
  Pallas kernels  37.7 us (8%)
  local copies, waits for them, and re-layouts  25.1 us (5%)
  starting transfers between devices  21.5 us (5%)
  blocking collectives  17.6 us (4%)
  other arithmetic  6.59 us (1%)
    all_to_all x1, waiting for transfers between devices, per_device(): lax.all_to_all(outgoing, 'cls', split_axis=0, concat_axis=0, tiled=True)  185 us
    all_to_all x1, waiting for transfers between devices, per_device(): lax.all_to_all(pair_grads, ('dp', 'cls'), split_axis=0, concat_axis=0, ti...  168 us
    pallas_call x1, Pallas kernels, block_step(): pl.pallas_call(_block_kernel, grid_spec=grid_spec, out_shape=[jax.ShapeDt...  23.2 us
    all_gather x1, blocking collectives, per_device(): got_ids = lax.all_gather(wanted, 'dp').reshape(parts * pair_count)  17.6 us
    pallas_call x1, Pallas kernels, cls_all_to_all(): pl.pallas_call(functools.partial(_a2a_kernel, n), out_shape=jax.ShapeDtyp...  14.4 us
    all_to_all x1, starting transfers between devices, per_device(): lax.all_to_all(pair_grads, ('dp', 'cls'), split_axis=0, concat_axis=0, ti...  14.3 us
    all_to_all x1, local copies, waits for them, and re-layouts, per_device(): lax.all_to_all(pair_grads, ('dp', 'cls'), split_axis=0, concat_axis=0, ti...  12.3 us
  transfers between devices with their start and end apart: 2, of which 2 were waited for; matrix products, arithmetic and copies ran while one was open for 1% of the time, Pallas kernels for 0%

profile of v7, /device:TPU:1, one launch (start us, length us, event | category | flops | bytes accessed | tf_op | source)
XLA Modules:
  0.0 463.5 jit_solution(4419951229710972399)
XLA Ops:
  0.6 0.8 sign_compare_fusion
  1.5 0.8 broadcast_remainder_fusion
  2.3 0.1 ne.51
  2.4 0.1 rem.30
  2.5 0.1 div.21
  2.6 0.2 select_reduce_fusion.1
  2.7 0.1 select_reduce_fusion
  2.9 0.8 gather_fusion
  3.7 0.7 reshape.152.src_ref
  4.4 14.4 %shard_map.76 = s32[32,2]{1,0:T(8,128)} custom-call(s32[32,2]{1,0:T(8,128)} %reshape.152.src_ref), custom_call_target="tpu_custom_call" | custom-call | tf_op jit(solution)/shard_map/pallas_call | solution.py:60
  18.8 0.7 compare_select_fusion
  19.6 0.1 reshape.169
  19.7 5.5 %gather_fusion.1 = bf16[64,128,512]{2,1,0:T(8,128)(2,1)} fusion(bf16[24,128,512]{2,1,0:T(8,128)(2,1)S(1)} %bitcast.25, s32[1024]{0:T(1024)S(1)} %pad_clamp_fusion), kind=kCustom, calls=%fused_computation.1 | custom fusion | bytes 16777472 | tf_op jit(solution)/shard_map/gather | solution.py:189
  25.2 7.2 %all-to-all-start = ((bf16[32,2,128,512]{3,2,1,0:T(8,128)(2,1)}), bf16[32,2,128,512]{3,2,1,0:T(8,128)(2,1)}, u32[]{:S(2)}, u32[]{:S(2)}) async-start(bf16[32,2,128,512]{3,2,1,0:T(8,128)(2,1)} %bitcast.28), calls=%async_computation | async-start | bytes 16777216 | tf_op jit(solution)/shard_map/all_to_all | solution.py:190
  32.4 1.0 copy.22
  33.5 0.1 multiply_reduce_fusion
  33.6 1.9 broadcast_subtract_fusion.pos_ref
  35.5 185.0 %all-to-all-done = bf16[32,2,128,512]{3,2,1,0:T(8,128)(2,1)} async-done(((bf16[32,2,128,512]{3,2,1,0:T(8,128)(2,1)}), bf16[32,2,128,512]{3,2,1,0:T(8,128)(2,1)}, u32[]{:S(2)}, u32[]{:S(2)}) %all-to-all-start) | async-done | bytes 8388640 | tf_op jit(solution)/shard_map/all_to_all | solution.py:190
  220.6 1.0 copy-done.1
  221.6 1.2 copy-done.2
  222.8 23.2 %shard_map.77 = (f32[8,128,1]{2,1,0:T(8,128)S(1)}, bf16[8,128,512]{2,1,0:T(8,128)(2,1)}, bf16[8,64,64,128]{3,2,1,0:T(8,128)(2,1)}) custom-call(s32[64]{0:T(128)S(1)} %multiply_add_fusion.slot_ref, s32[8]{0:T(128)S(1)} %copy-done.4, bf16[8,128,512]{2,1,0:T(8,128)(2,1)S(1)} %bitcast.26, s32[8,128,1]{2,1,0:T(8,128)S(1)} %copy-done.1, ...), custom_call_target="tpu_custom_call" | custom-call | tf_op jit(solution)/shard_map/pallas_call | solution.py:159
  246.1 0.8 copy-done.3
  246.9 14.3 %all-to-all-start.1 = ((bf16[256,2,64,128]{3,2,1,0:T(8,128)(2,1)}), bf16[256,2,64,128]{3,2,1,0:T(8,128)(2,1)}, u32[]{:S(2)}, u32[]{:S(2)}) async-start(bf16[256,2,64,128]{3,2,1,0:T(8,128)(2,1)} %bitcast.29), calls=%async_computation.1 | async-start | bytes 16777216 | tf_op jit(solution)/shard_map/all_to_all | solution.py:198
  261.2 0.1 copy.25
  261.3 17.6 %all-gather.1 = s32[8,32,2]{1,2,0:T(2,128)S(1)} all-gather(s32[1,32,2]{1,2,0:T(2,128)S(1)} %bitcast.34), channel_id=2, replica_groups=mesh['dp'=8,'cls'=32] {'dp'}, dimensions={0}, use_global_device_ids=true | all-gather | bytes 2304 | tf_op jit(solution)/shard_map/all_gather | solution.py:199
  278.8 0.1 copy.26
  279.0 0.1 eq.47
  279.1 1.8 reduce.1
  281.0 168.1 %all-to-all-done.1 = bf16[256,2,64,128]{3,2,1,0:T(8,128)(2,1)} async-done(((bf16[256,2,64,128]{3,2,1,0:T(8,128)(2,1)}), bf16[256,2,64,128]{3,2,1,0:T(8,128)(2,1)}, u32[]{:S(2)}, u32[]{:S(2)}) %all-to-all-start.1) | async-done | bytes 8388640 | tf_op jit(solution)/shard_map/all_to_all | solution.py:198
  449.0 12.3 %copy.24 = bf16[256,2,64,128]{3,1,0,2:T(2,128)(2,1)S(1)} copy(bf16[256,2,64,128]{3,2,1,0:T(8,128)(2,1)} %all-to-all-done.1) | data formatting | bytes 16777216 | tf_op jit(solution)/shard_map/all_to_all | solution.py:198
  461.3 1.2 fusion.1
  462.5 1.0 copy.29
  (18 shorter events, 0.1 us)
Async XLA Ops:
  0.6 19.1 %copy-start = (bf16[3072,512]{1,0:T(8,128)(2,1)S(1)}, bf16[3072,512]{1,0:T(8,128)(2,1)}, u32[]{:S(2)}) copy-start(bf16[3072,512]{1,0:T(8,128)(2,1)} %param.6) | copy-start | bytes 9437188
  25.2 7.2 %copy-start.7 = (s32[1024]{0:T(1024)S(1)}, s32[1024]{0:T(1024)}, u32[]{:S(2)}) copy-start(s32[1024]{0:T(1024)} %param.9) | copy-start | bytes 12292
  25.2 8.3 %copy-start.6 = (s32[8,8]{1,0:T(8,128)S(1)}, s32[8,8]{1,0:T(8,128)}, u32[]{:S(2)}) copy-start(s32[8,8]{1,0:T(8,128)} %param.7) | copy-start | bytes 772
  25.2 195.4 %copy-start.4 = (s32[8]{0:T(128)S(1)}, s32[8]{0:T(128)}, u32[]{:S(2)}) copy-start(s32[8]{0:T(128)} %count_ref.1) | copy-start | bytes 100
  25.2 195.4 %all-to-all-start = ((bf16[32,2,128,512]{3,2,1,0:T(8,128)(2,1)}), bf16[32,2,128,512]{3,2,1,0:T(8,128)(2,1)}, u32[]{:S(2)}, u32[]{:S(2)}) async-start(bf16[32,2,128,512]{3,2,1,0:T(8,128)(2,1)} %bitcast.28), calls=%async_computation | async-start | bytes 16777216 | tf_op jit(solution)/shard_map/all_to_all | solution.py:190
  220.6 1.0 copy-start.1
  221.6 1.2 copy-start.2
  246.1 0.8 copy-start.3
  246.9 14.3 %copy-start.5 = (s32[32,2]{1,0:T(8,128)S(1)}, s32[32,2]{1,0:T(8,128)}, u32[]{:S(2)}) copy-start(s32[32,2]{1,0:T(8,128)} %shard_map.76) | copy-start | bytes 772
  246.9 202.2 %all-to-all-start.1 = ((bf16[256,2,64,128]{3,2,1,0:T(8,128)(2,1)}), bf16[256,2,64,128]{3,2,1,0:T(8,128)(2,1)}, u32[]{:S(2)}, u32[]{:S(2)}) async-start(bf16[256,2,64,128]{3,2,1,0:T(8,128)(2,1)} %bitcast.29), calls=%async_computation.1 | async-start | bytes 16777216 | tf_op jit(solution)/shard_map/all_to_all | solution.py:198

commit v8 on v7

--- a/solution.py
+++ b/solution.py
@@ -83,38 +83,32 @@
     inverse_norm = lax.rsqrt(jnp.sum(emb * emb, axis=1, keepdims=True) + epsilon)
     unit_exact = emb * inverse_norm
     unit_rows = unit_exact.astype(jnp.bfloat16)
+    unit_t = unit_rows.T
     count = count_ref[b]
-    columns = lax.broadcasted_iota(jnp.int32, (BR, TILE), 1)
-    hit = columns == pos_ref[0]
+    classes = lax.broadcasted_iota(jnp.int32, (TILE, BR), 0)
+    hit = classes == pos_ref[0]
     logits = []
     for k in range(K):
-        cand = tiles[k][0]
-        lg = logit_scale * lax.dot_general(
-            unit_rows, cand, (((1,), (1,)), ((), ())), preferred_element_type=jnp.float32
-        )
-        logits.append(lg)
+        logits.append(logit_scale * jnp.dot(tiles[k][0], unit_t, preferred_element_type=jnp.float32))
     masked = [jnp.where(k < count, logits[k], -1e30) for k in range(K)]
-    peak = masked[0].max(axis=1, keepdims=True)
+    peak = masked[0].max(axis=0, keepdims=True)
     for k in range(1, K):
-        peak = jnp.maximum(peak, masked[k].max(axis=1, keepdims=True))
+        peak = jnp.maximum(peak, masked[k].max(axis=0, keepdims=True))
     total = jnp.zeros_like(peak)
     for k in range(K):
-        total = total + jnp.sum(jnp.exp(masked[k] - peak), axis=1, keepdims=True)
+        total = total + jnp.sum(jnp.exp(masked[k] - peak), axis=0, keepdims=True)
     log_total = peak + jnp.log(total)
-    positive = jnp.sum(jnp.where(hit, logits[0], 0.0), axis=1, keepdims=True)
+    positive = jnp.sum(jnp.where(hit, logits[0], 0.0), axis=0, keepdims=True)
     loss_ref[0] = log_total - positive
     grad_unit = jnp.zeros((BR, D), jnp.float32)
     for k in range(K):
         probabilities = jnp.exp(masked[k] - log_total)
         if k == 0:
             probabilities = probabilities - jnp.where(hit, 1.0, 0.0)
-        dscore = (logit_scale * probabilities).astype(jnp.bfloat16)
-        cand = tiles[k][0]
-        terms = jnp.dot(dscore, cand, preferred_element_type=jnp.float32)
+        dscore = (logit_scale * probabilities).astype(jnp.bfloat16).T
+        terms = jnp.dot(dscore, tiles[k][0], preferred_element_type=jnp.float32)
         grad_unit = grad_unit + terms.astype(jnp.bfloat16).astype(jnp.float32)
-        pair_t = lax.dot_general(
-            unit_rows, dscore, (((0,), (0,)), ((), ())), preferred_element_type=jnp.float32
-        ).astype(jnp.bfloat16)
+        pair_t = jnp.dot(unit_t, dscore, preferred_element_type=jnp.float32).astype(jnp.bfloat16)
         pair_buf[:, k] = pair_t.reshape(pair_buf.shape[0], D // pair_buf.shape[0], TILE)
     copies = []
     for k in range(K):
@@ -143,11 +137,11 @@
         grid=(blocks,),
         in_specs=[
             pl.BlockSpec((1, BR, D), lambda b, slot, cnt: (b, 0, 0)),
-            pl.BlockSpec((1, BR, 1), lambda b, slot, cnt: (b, 0, 0)),
+            pl.BlockSpec((1, 1, BR), lambda b, slot, cnt: (b, 0, 0)),
         ]
         + [tile_spec(k) for k in range(K)],
         out_specs=[
-            pl.BlockSpec((1, BR, 1), lambda b, slot, cnt: (b, 0, 0)),
+            pl.BlockSpec((1, 1, BR), lambda b, slot, cnt: (b, 0, 0)),
             pl.BlockSpec((1, BR, D), lambda b, slot, cnt: (b, 0, 0)),
             pl.BlockSpec(memory_space=pl.ANY),
         ],
@@ -160,12 +154,44 @@
         _block_kernel,
         grid_spec=grid_spec,
         out_shape=[
-            jax.ShapeDtypeStruct((blocks, BR, 1), jnp.float32),
+            jax.ShapeDtypeStruct((blocks, 1, BR), jnp.float32),
             jax.ShapeDtypeStruct((blocks, BR, D), jnp.bfloat16),
             jax.ShapeDtypeStruct((parts, pairs, D // parts, TILE), jnp.bfloat16),
         ],
         compiler_params=pltpu.CompilerParams(vmem_limit_bytes=48 * 1024 * 1024),
     )(slot_of, tile_count, emb_blocks, pos_cols, *([fetched] * K))
+
+
+def _column_sum_kernel(ids_ref, piece_ref, out_ref):
+    step = pl.program_id(0)
+    chunk = piece_ref.shape[0]
+
+    @pl.when(step == 0)
+    def _():
+        out_ref[...] = jnp.zeros_like(out_ref)
+
+    def body(j, carry):
+        start = pl.multiple_of(ids_ref[step * chunk + j] * TILE, TILE)
+        window = pl.ds(start, TILE)
+        out_ref[:, window] += piece_ref[j].astype(jnp.float32)
+        return carry
+
+    lax.fori_loop(0, chunk, body, 0, unroll=8)
+
+
+def column_sum(got_ids, pieces, tile_dev, chunk=64):
+    count, width, _ = pieces.shape
+    grid_spec = pltpu.PrefetchScalarGridSpec(
+        num_scalar_prefetch=1,
+        grid=(count // chunk,),
+        in_specs=[pl.BlockSpec((chunk, width, TILE), lambda s, ids: (s, 0, 0))],
+        out_specs=pl.BlockSpec((width, tile_dev * TILE), lambda s, ids: (0, 0)),
+    )
+    return pl.pallas_call(
+        _column_sum_kernel,
+        grid_spec=grid_spec,
+        out_shape=jax.ShapeDtypeStruct((width, tile_dev * TILE), jnp.float32),
+    )(got_ids, pieces)
 
 
 def per_device(embeddings, proxies, hard_tiles, tile_count, labels):
@@ -189,7 +215,7 @@
     outgoing = tile_table[wanted]
     fetched = lax.all_to_all(outgoing, "cls", split_axis=0, concat_axis=0, tiled=True)
     fetched = fetched.reshape(pair_count, TILE, D)
-    pos_cols = labels.reshape(blocks, BR, 1) - hard_tiles[:, 0:1, None] * TILE
+    pos_cols = labels.reshape(blocks, 1, BR) - hard_tiles[:, None, 0:1] * TILE
     parts = lax.axis_size("dp")
     loss, embed_grad, pair_grads = block_step(
         slot_of, tile_count, embeddings.reshape(blocks, BR, D), pos_cols, fetched, parts
@@ -198,11 +224,7 @@
     returned = lax.all_to_all(pair_grads, ("dp", "cls"), split_axis=0, concat_axis=0, tiled=True)
     got_ids = lax.all_gather(wanted, "dp").reshape(parts * pair_count)
     got_terms = returned.reshape(parts * pair_count, D // parts, TILE)
-    select_rows = (jnp.arange(tile_dev, dtype=jnp.int32)[:, None] == got_ids[None, :]).astype(
-        jnp.bfloat16
-    )
-    owned = jnp.einsum("tp,pdc->tcd", select_rows, got_terms, preferred_element_type=jnp.float32)
-    proxy_share = owned.reshape(tile_dev * TILE, D // parts)
+    proxy_share = column_sum(got_ids, got_terms, tile_dev).T
     return (loss.reshape(-1), embed_grad.reshape(-1, D), proxy_share)
 
 

time: 464 us -> 455 us (0.981)
  local copies, waits for them, and re-layouts: 25.1 us -> 9.52 us
  Pallas kernels: 37.7 us -> 46.4 us
  waiting for transfers between devices: 353 us -> 359 us
    all_to_all x1 -> x0, local copies, waits for them, and re-layouts: 12.3 us -> none  [per_device(): lax.all_to_all(pair_grads, ('dp', 'cls'), split_axis=0, concat_axis=0, ti...]
    pallas_call x0 -> x1, Pallas kernels: none -> 9.09 us  [column_sum(): pl.pallas_call(_column_sum_kernel, grid_spec=grid_spec, out_shape=jax.Sha...]
  transfers between devices with their start and end apart: 2 -> 2, of which waited for: 2 -> 2; matrix products, arithmetic and copies ran while one was open for 1% -> 0% of each run, Pallas kernels for 0% -> 0%
where the time goes in v8:
time: 455 us
  waiting for transfers between devices  359 us (79%)
  Pallas kernels  46.4 us (10%)
  starting transfers between devices  19.1 us (4%)
  blocking collectives  17.6 us (4%)
  local copies, waits for them, and re-layouts  9.52 us (2%)
    all_to_all x1, waiting for transfers between devices, per_device(): lax.all_to_all(outgoing, 'cls', split_axis=0, concat_axis=0, tiled=True)  189 us
    all_to_all x1, waiting for transfers between devices, per_device(): lax.all_to_all(pair_grads, ('dp', 'cls'), split_axis=0, concat_axis=0, ti...  169 us
    pallas_call x1, Pallas kernels, block_step(): pl.pallas_call(_block_kernel, grid_spec=grid_spec, out_shape=[jax.ShapeDt...  22.8 us
    all_gather x1, blocking collectives, per_device(): got_ids = lax.all_gather(wanted, 'dp').reshape(parts * pair_count)  17.6 us
    pallas_call x1, Pallas kernels, cls_all_to_all(): pl.pallas_call(functools.partial(_a2a_kernel, n), out_shape=jax.ShapeDtyp...  14.5 us
    all_to_all x1, starting transfers between devices, per_device(): lax.all_to_all(pair_grads, ('dp', 'cls'), split_axis=0, concat_axis=0, ti...  11.7 us
  transfers between devices with their start and end apart: 2, of which 2 were waited for; matrix products, arithmetic and copies ran while one was open for 0% of the time, Pallas kernels for 0%

profile of v8, /device:TPU:1, one launch (start us, length us, event | category | flops | bytes accessed | tf_op | source)
XLA Modules:
  0.0 454.8 jit_solution(10853640255244000901)
XLA Ops:
  0.6 0.0 copy-start
  0.6 0.8 sign_compare_fusion
  1.5 0.8 broadcast_remainder_fusion
  2.3 0.1 ne.51
  2.4 0.1 rem.30
  2.5 0.1 div.21
  2.6 0.2 select_reduce_fusion.1
  2.7 0.1 select_reduce_fusion
  2.9 0.8 gather_fusion
  3.7 0.7 reshape.149.src_ref
  4.4 14.5 %shard_map.76 = s32[32,2]{1,0:T(8,128)} custom-call(s32[32,2]{1,0:T(8,128)} %reshape.149.src_ref), custom_call_target="tpu_custom_call" | custom-call | tf_op jit(solution)/shard_map/pallas_call | solution.py:60
  18.8 0.7 compare_select_fusion
  19.6 0.1 reshape.166
  19.7 0.0 copy-done
  19.7 5.5 %gather_fusion.1 = bf16[64,128,512]{2,1,0:T(8,128)(2,1)} fusion(bf16[24,128,512]{2,1,0:T(8,128)(2,1)S(1)} %bitcast.15, s32[1024]{0:T(1024)S(1)} %pad_clamp_fusion), kind=kCustom, calls=%fused_computation.1 | custom fusion | bytes 16777472 | tf_op jit(solution)/shard_map/gather | solution.py:215
  25.2 7.3 %all-to-all-start = ((bf16[32,2,128,512]{3,2,1,0:T(8,128)(2,1)}), bf16[32,2,128,512]{3,2,1,0:T(8,128)(2,1)}, u32[]{:S(2)}, u32[]{:S(2)}) async-start(bf16[32,2,128,512]{3,2,1,0:T(8,128)(2,1)} %bitcast.17), calls=%async_computation | async-start | bytes 16777216 | tf_op jit(solution)/shard_map/all_to_all | solution.py:216
  32.6 0.0 copy-done.4
  32.6 0.1 multiply_reduce_fusion
  32.7 0.0 copy-done.5
  32.7 0.1 broadcast_subtract_fusion.pos_ref
  32.8 189.2 %all-to-all-done = bf16[32,2,128,512]{3,2,1,0:T(8,128)(2,1)} async-done(((bf16[32,2,128,512]{3,2,1,0:T(8,128)(2,1)}), bf16[32,2,128,512]{3,2,1,0:T(8,128)(2,1)}, u32[]{:S(2)}, u32[]{:S(2)}) %all-to-all-start) | async-done | bytes 8388640 | tf_op jit(solution)/shard_map/all_to_all | solution.py:216
  222.0 0.0 copy-done.2
  222.0 1.2 copy-done.1
  223.2 22.8 %shard_map.77 = (f32[8,1,128]{2,1,0:T(1,128)}, bf16[8,128,512]{2,1,0:T(8,128)(2,1)}, bf16[8,64,64,128]{3,2,1,0:T(8,128)(2,1)}) custom-call(s32[64]{0:T(128)S(1)} %multiply_add_fusion.slot_ref, s32[8]{0:T(128)S(1)} %copy-done.2, bf16[8,128,512]{2,1,0:T(8,128)(2,1)S(1)} %bitcast.16, s32[8,1,128]{2,1,0:T(1,128)S(1)} %broadcast_subtract_fusion.pos_ref, ...), custom_call_target="tpu_custom_call" | custom-call | tf_op jit(solution)/shard_map/pallas_call | solution.py:153
  246.1 0.0 copy-start.3
  246.1 11.7 %all-to-all-start.1 = ((bf16[256,2,64,128]{3,2,1,0:T(8,128)(2,1)}), bf16[256,2,64,128]{3,2,1,0:T(8,128)(2,1)}, u32[]{:S(2)}, u32[]{:S(2)}) async-start(bf16[256,2,64,128]{3,2,1,0:T(8,128)(2,1)} %bitcast.18), calls=%async_computation.1 | async-start | bytes 16777216 | tf_op jit(solution)/shard_map/all_to_all | solution.py:224
  257.8 0.1 copy.13
  257.9 17.6 %all-gather.1 = s32[8,32,2]{1,2,0:T(2,128)S(1)} all-gather(s32[1,32,2]{1,2,0:T(2,128)S(1)} %bitcast.20), channel_id=2, replica_groups=mesh['dp'=8,'cls'=32] {'dp'}, dimensions={0}, use_global_device_ids=true | all-gather | bytes 2304 | tf_op jit(solution)/shard_map/all_gather | solution.py:225
  275.5 0.1 copy.14
  275.6 0.7 reshape.153.ids_ref
  276.3 169.3 %all-to-all-done.1 = bf16[256,2,64,128]{3,2,1,0:T(8,128)(2,1)} async-done(((bf16[256,2,64,128]{3,2,1,0:T(8,128)(2,1)}), bf16[256,2,64,128]{3,2,1,0:T(8,128)(2,1)}, u32[]{:S(2)}, u32[]{:S(2)}) %all-to-all-start.1) | async-done | bytes 8388640 | tf_op jit(solution)/shard_map/all_to_all | solution.py:224
  445.7 9.1 %shard_map.78 = f32[64,3072]{1,0:T(8,128)} custom-call(s32[512]{0:T(512)} %reshape.153.ids_ref, bf16[512,64,128]{2,1,0:T(8,128)(2,1)} %bitcast.11.piece_ref), custom_call_target="tpu_custom_call" | custom-call | tf_op jit(solution)/shard_map/pallas_call | solution.py:190
  (10 shorter events, 0.0 us)
Async XLA Ops:
  0.6 19.1 %copy-start = (bf16[3072,512]{1,0:T(8,128)(2,1)S(1)}, bf16[3072,512]{1,0:T(8,128)(2,1)}, u32[]{:S(2)}) copy-start(bf16[3072,512]{1,0:T(8,128)(2,1)} %param.6) | copy-start | bytes 9437188
  25.2 7.4 %copy-start.4 = (s32[8,8]{1,0:T(8,128)S(1)}, s32[8,8]{1,0:T(8,128)}, u32[]{:S(2)}) copy-start(s32[8,8]{1,0:T(8,128)} %param.7) | copy-start | bytes 772
  25.2 7.5 %copy-start.5 = (s32[1024]{0:T(1024)S(1)}, s32[1024]{0:T(1024)}, u32[]{:S(2)}) copy-start(s32[1024]{0:T(1024)} %param.9) | copy-start | bytes 12292
  25.2 196.8 %copy-start.2 = (s32[8]{0:T(128)S(1)}, s32[8]{0:T(128)}, u32[]{:S(2)}) copy-start(s32[8]{0:T(128)} %count_ref.1) | copy-start | bytes 100
  25.2 196.8 %all-to-all-start = ((bf16[32,2,128,512]{3,2,1,0:T(8,128)(2,1)}), bf16[32,2,128,512]{3,2,1,0:T(8,128)(2,1)}, u32[]{:S(2)}, u32[]{:S(2)}) async-start(bf16[32,2,128,512]{3,2,1,0:T(8,128)(2,1)} %bitcast.17), calls=%async_computation | async-start | bytes 16777216 | tf_op jit(solution)/shard_map/all_to_all | solution.py:216
  222.0 1.2 copy-start.1
  246.1 11.8 %copy-start.3 = (s32[32,2]{1,0:T(8,128)S(1)}, s32[32,2]{1,0:T(8,128)}, u32[]{:S(2)}) copy-start(s32[32,2]{1,0:T(8,128)} %shard_map.76) | copy-start | bytes 772
  246.1 199.6 %all-to-all-start.1 = ((bf16[256,2,64,128]{3,2,1,0:T(8,128)(2,1)}), bf16[256,2,64,128]{3,2,1,0:T(8,128)(2,1)}, u32[]{:S(2)}, u32[]{:S(2)}) async-start(bf16[256,2,64,128]{3,2,1,0:T(8,128)(2,1)} %bitcast.18), calls=%async_computation.1 | async-start | bytes 16777216 | tf_op jit(solution)/shard_map/all_to_all | solution.py:224

commit v9 on v8

--- a/solution.py
+++ b/solution.py
@@ -75,15 +75,13 @@
 epsilon = 1e-06
 
 
-def _block_kernel(slot_ref, count_ref, emb_ref, pos_ref, *rest):
+def _score_kernel(slot_ref, count_ref, emb_ref, pos_ref, *rest):
     tiles = rest[:K]
-    loss_ref, grad_ref, pair_hbm, pair_buf, pair_sem = rest[K:]
+    loss_ref, score_ref, pair_hbm, pair_buf, pair_sem = rest[K:]
     b = pl.program_id(0)
     emb = emb_ref[0].astype(jnp.float32)
     inverse_norm = lax.rsqrt(jnp.sum(emb * emb, axis=1, keepdims=True) + epsilon)
-    unit_exact = emb * inverse_norm
-    unit_rows = unit_exact.astype(jnp.bfloat16)
-    unit_t = unit_rows.T
+    unit_t = (emb * inverse_norm).astype(jnp.bfloat16).T
     count = count_ref[b]
     classes = lax.broadcasted_iota(jnp.int32, (TILE, BR), 0)
     hit = classes == pos_ref[0]
@@ -100,14 +98,12 @@
     log_total = peak + jnp.log(total)
     positive = jnp.sum(jnp.where(hit, logits[0], 0.0), axis=0, keepdims=True)
     loss_ref[0] = log_total - positive
-    grad_unit = jnp.zeros((BR, D), jnp.float32)
     for k in range(K):
         probabilities = jnp.exp(masked[k] - log_total)
         if k == 0:
             probabilities = probabilities - jnp.where(hit, 1.0, 0.0)
         dscore = (logit_scale * probabilities).astype(jnp.bfloat16).T
-        terms = jnp.dot(dscore, tiles[k][0], preferred_element_type=jnp.float32)
-        grad_unit = grad_unit + terms.astype(jnp.bfloat16).astype(jnp.float32)
+        score_ref[0, k] = dscore
         pair_t = jnp.dot(unit_t, dscore, preferred_element_type=jnp.float32).astype(jnp.bfloat16)
         pair_buf[:, k] = pair_t.reshape(pair_buf.shape[0], D // pair_buf.shape[0], TILE)
     copies = []
@@ -119,19 +115,31 @@
         )
         cp.start()
         copies.append(cp)
+    for cp in copies:
+        cp.wait()
+
+
+def _embed_kernel(slot_ref, emb_ref, score_ref, *rest):
+    tiles = rest[:K]
+    (grad_ref,) = rest[K:]
+    emb = emb_ref[0].astype(jnp.float32)
+    inverse_norm = lax.rsqrt(jnp.sum(emb * emb, axis=1, keepdims=True) + epsilon)
+    unit_exact = emb * inverse_norm
+    grad_unit = jnp.zeros((BR, D), jnp.float32)
+    for k in range(K):
+        terms = jnp.dot(score_ref[0, k], tiles[k][0], preferred_element_type=jnp.float32)
+        grad_unit = grad_unit + terms.astype(jnp.bfloat16).astype(jnp.float32)
     radial = jnp.sum(unit_exact * grad_unit, axis=1, keepdims=True)
     grad_ref[0] = ((grad_unit - unit_exact * radial) * inverse_norm).astype(grad_ref.dtype)
-    for cp in copies:
-        cp.wait()
-
-
-def block_step(slot_of, tile_count, emb_blocks, pos_cols, fetched, parts):
+
+
+def _tile_spec(k):
+    return pl.BlockSpec((1, TILE, D), lambda b, slot, *_: (slot[b * K + k], 0, 0))
+
+
+def score_step(slot_of, tile_count, emb_blocks, pos_cols, fetched, parts):
     blocks = emb_blocks.shape[0]
     pairs = fetched.shape[0]
-
-    def tile_spec(k):
-        return pl.BlockSpec((1, TILE, D), lambda b, slot, cnt: (slot[b * K + k], 0, 0))
-
     grid_spec = pltpu.PrefetchScalarGridSpec(
         num_scalar_prefetch=2,
         grid=(blocks,),
@@ -139,10 +147,10 @@
             pl.BlockSpec((1, BR, D), lambda b, slot, cnt: (b, 0, 0)),
             pl.BlockSpec((1, 1, BR), lambda b, slot, cnt: (b, 0, 0)),
         ]
-        + [tile_spec(k) for k in range(K)],
+        + [_tile_spec(k) for k in range(K)],
         out_specs=[
             pl.BlockSpec((1, 1, BR), lambda b, slot, cnt: (b, 0, 0)),
-            pl.BlockSpec((1, BR, D), lambda b, slot, cnt: (b, 0, 0)),
+            pl.BlockSpec((1, K, BR, TILE), lambda b, slot, cnt: (b, 0, 0, 0)),
             pl.BlockSpec(memory_space=pl.ANY),
         ],
         scratch_shapes=[
@@ -151,15 +159,39 @@
         ],
     )
     return pl.pallas_call(
-        _block_kernel,
+        _score_kernel,
         grid_spec=grid_spec,
         out_shape=[
             jax.ShapeDtypeStruct((blocks, 1, BR), jnp.float32),
-            jax.ShapeDtypeStruct((blocks, BR, D), jnp.bfloat16),
+            jax.ShapeDtypeStruct((blocks, K, BR, TILE), jnp.bfloat16),
             jax.ShapeDtypeStruct((parts, pairs, D // parts, TILE), jnp.bfloat16),
         ],
         compiler_params=pltpu.CompilerParams(vmem_limit_bytes=48 * 1024 * 1024),
     )(slot_of, tile_count, emb_blocks, pos_cols, *([fetched] * K))
+
+
+def embed_step(slot_of, emb_blocks, scores, fetched):
+    blocks = emb_blocks.shape[0]
+    grid_spec = pltpu.PrefetchScalarGridSpec(
+        num_scalar_prefetch=1,
+        grid=(blocks,),
+        in_specs=[
+            pl.BlockSpec((1, BR, D), lambda b, slot: (b, 0, 0)),
+            pl.BlockSpec((1, K, BR, TILE), lambda b, slot: (b, 0, 0, 0)),
+        ]
+        + [_tile_spec(k) for k in range(K)],
+        out_specs=pl.BlockSpec((1, BR, D), lambda b, slot: (b, 0, 0)),
+    )
+    flops = blocks * K * 2 * BR * TILE * D
+    return pl.pallas_call(
+        _embed_kernel,
+        grid_spec=grid_spec,
+        out_shape=jax.ShapeDtypeStruct((blocks, BR, D), jnp.bfloat16),
+        compiler_params=pltpu.CompilerParams(vmem_limit_bytes=48 * 1024 * 1024),
+        cost_estimate=pl.CostEstimate(
+            flops=flops, transcendentals=0, bytes_accessed=blocks * (K + 3) * TILE * D * 2
+        ),
+    )(slot_of, emb_blocks, scores, *([fetched] * K))
 
 
 def _column_sum_kernel(ids_ref, piece_ref, out_ref):
@@ -217,9 +249,9 @@
     fetched = fetched.reshape(pair_count, TILE, D)
     pos_cols = labels.reshape(blocks, 1, BR) - hard_tiles[:, None, 0:1] * TILE
     parts = lax.axis_size("dp")
-    loss, embed_grad, pair_grads = block_step(
-        slot_of, tile_count, embeddings.reshape(blocks, BR, D), pos_cols, fetched, parts
-    )
+    emb_blocks = embeddings.reshape(blocks, BR, D)
+    loss, scores, pair_grads = score_step(slot_of, tile_count, emb_blocks, pos_cols, fetched, parts)
+    embed_grad = embed_step(slot_of, emb_blocks, scores, fetched)
     pair_grads = pair_grads.reshape(parts * groups, capacity, D // parts, TILE)
     returned = lax.all_to_all(pair_grads, ("dp", "cls"), split_axis=0, concat_axis=0, tiled=True)
     got_ids = lax.all_gather(wanted, "dp").reshape(parts * pair_count)

time: 455 us -> 455 us (level)
  waiting for transfers between devices: 359 us -> 345 us
  Pallas kernels: 46.4 us -> 53 us
    all_to_all x1, waiting for transfers between devices: 169 us -> 157 us  [per_device(): lax.all_to_all(pair_grads, ('dp', 'cls'), split_axis=0, concat_axis=0, ti...]
    pallas_call x1 -> x2, Pallas kernels: 22.8 us -> 29.4 us  [the longest x1 20.1 us: score_step(): pl.pallas_call(_score_kernel, grid_spec=grid_spec, out_shape=[jax.ShapeDt...]
  transfers between devices with their start and end apart: 2 -> 2, of which waited for: 2 -> 2; matrix products, arithmetic and copies ran while one was open for 0% -> 0% of each run, Pallas kernels for 0% -> 2%
where the time goes in v9:
time: 455 us; the launch traced here: 454 us
  waiting for transfers between devices  345 us (76%)
  Pallas kernels  53 us (12%)
  starting transfers between devices  21.5 us (5%)
  blocking collectives  17.6 us (4%)
  local copies, waits for them, and re-layouts  13.6 us (3%)
    all_to_all x1, waiting for transfers between devices, per_device(): lax.all_to_all(outgoing, 'cls', split_axis=0, concat_axis=0, tiled=True)  188 us
    all_to_all x1, waiting for transfers between devices, per_device(): lax.all_to_all(pair_grads, ('dp', 'cls'), split_axis=0, concat_axis=0, ti...  157 us
    pallas_call x1, Pallas kernels, score_step(): pl.pallas_call(_score_kernel, grid_spec=grid_spec, out_shape=[jax.ShapeDt...  20.1 us
    all_gather x1, blocking collectives, per_device(): got_ids = lax.all_gather(wanted, 'dp').reshape(parts * pair_count)  17.6 us
    pallas_call x1, Pallas kernels, cls_all_to_all(): pl.pallas_call(functools.partial(_a2a_kernel, n), out_shape=jax.ShapeDtyp...  14.5 us
    all_to_all x1, starting transfers between devices, per_device(): lax.all_to_all(pair_grads, ('dp', 'cls'), split_axis=0, concat_axis=0, ti...  14.3 us
    pallas_call x1, Pallas kernels, embed_step(): pl.pallas_call(_embed_kernel, grid_spec=grid_spec, out_shape=jax.ShapeDty...  9.31 us
  transfers between devices with their start and end apart: 2, of which 2 were waited for; matrix products, arithmetic and copies ran while one was open for 0% of the time, Pallas kernels for 2%

profile of v9, /device:TPU:1, one launch (start us, length us, event | category | flops | bytes accessed | tf_op | source)
XLA Modules:
  0.0 454.4 jit_solution(14437567917246232845)
XLA Ops:
  0.6 0.0 copy-start
  0.6 0.8 sign_compare_fusion
  1.5 0.8 broadcast_remainder_fusion
  2.3 0.1 ne.51
  2.4 0.1 rem.30
  2.5 0.1 div.21
  2.6 0.2 select_reduce_fusion.1
  2.7 0.1 select_reduce_fusion
  2.9 0.8 gather_fusion
  3.7 0.7 reshape.149.src_ref
  4.4 14.5 %shard_map.76 = s32[32,2]{1,0:T(8,128)} custom-call(s32[32,2]{1,0:T(8,128)} %reshape.149.src_ref), custom_call_target="tpu_custom_call" | custom-call | tf_op jit(solution)/shard_map/pallas_call | solution.py:60
  18.8 0.7 compare_select_fusion
  19.6 0.1 reshape.166
  19.7 5.5 %gather_fusion.1 = bf16[64,128,512]{2,1,0:T(8,128)(2,1)} fusion(bf16[24,128,512]{2,1,0:T(8,128)(2,1)S(1)} %bitcast.15, s32[1024]{0:T(1024)S(1)} %pad_clamp_fusion), kind=kCustom, calls=%fused_computation.1 | custom fusion | bytes 16777472 | tf_op jit(solution)/shard_map/gather | solution.py:247
  25.2 7.2 %all-to-all-start = ((bf16[32,2,128,512]{3,2,1,0:T(8,128)(2,1)}), bf16[32,2,128,512]{3,2,1,0:T(8,128)(2,1)}, u32[]{:S(2)}, u32[]{:S(2)}) async-start(bf16[32,2,128,512]{3,2,1,0:T(8,128)(2,1)} %bitcast.18), calls=%async_computation | async-start | bytes 16777216 | tf_op jit(solution)/shard_map/all_to_all | solution.py:248
  32.4 0.0 copy-done.7
  32.4 0.1 multiply_reduce_fusion
  32.5 0.1 broadcast_subtract_fusion.pos_ref
  32.6 187.8 %all-to-all-done = bf16[32,2,128,512]{3,2,1,0:T(8,128)(2,1)} async-done(((bf16[32,2,128,512]{3,2,1,0:T(8,128)(2,1)}), bf16[32,2,128,512]{3,2,1,0:T(8,128)(2,1)}, u32[]{:S(2)}, u32[]{:S(2)}) %all-to-all-start) | async-done | bytes 8388640 | tf_op jit(solution)/shard_map/all_to_all | solution.py:248
  220.5 1.2 copy-done.1
  221.7 20.1 %shard_map.77 = (f32[8,1,128]{2,1,0:T(1,128)}, bf16[8,8,128,128]{3,2,1,0:T(8,128)(2,1)S(1)}, bf16[8,64,64,128]{3,2,1,0:T(8,128)(2,1)}) custom-call(s32[64]{0:T(128)S(1)} %multiply_add_fusion.slot_ref, s32[8]{0:T(128)S(1)} %copy-done.5, bf16[8,128,512]{2,1,0:T(8,128)(2,1)S(1)} %bitcast.16, s32[8,1,128]{2,1,0:T(1,128)S(1)} %broadcast_subtract_fusion.pos_ref, ...), custom_call_target="tpu_custom_call" | custom-call | tf_op jit(solution)/shard_map/pallas_call | solution.py:161
  241.8 1.3 copy-done.3
  243.2 14.3 %all-to-all-start.1 = ((bf16[256,2,64,128]{3,2,1,0:T(8,128)(2,1)}), bf16[256,2,64,128]{3,2,1,0:T(8,128)(2,1)}, u32[]{:S(2)}, u32[]{:S(2)}) async-start(bf16[256,2,64,128]{3,2,1,0:T(8,128)(2,1)} %bitcast.19), calls=%async_computation.1 | async-start | bytes 16777216 | tf_op jit(solution)/shard_map/all_to_all | solution.py:256
  257.5 0.1 copy.13
  257.5 17.6 %all-gather.1 = s32[8,32,2]{1,2,0:T(2,128)S(1)} all-gather(s32[1,32,2]{1,2,0:T(2,128)S(1)} %bitcast.22), channel_id=2, replica_groups=mesh['dp'=8,'cls'=32] {'dp'}, dimensions={0}, use_global_device_ids=true | all-gather | bytes 2304 | tf_op jit(solution)/shard_map/all_gather | solution.py:257
  275.1 0.1 copy.14
  275.3 0.7 reshape.153.ids_ref
  275.9 1.2 copy-done.2
  277.1 1.6 copy-done.4
  278.7 9.3 %shard_map.78 = bf16[8,128,512]{2,1,0:T(8,128)(2,1)} custom-call(s32[64]{0:T(128)S(1)} %multiply_add_fusion.slot_ref, bf16[8,128,512]{2,1,0:T(8,128)(2,1)S(1)} %bitcast.17, bf16[8,8,128,128]{3,2,1,0:T(8,128)(2,1)S(1)} %copy-done.4, bf16[64,128,512]{2,1,0:T(8,128)(2,1)} %bitcast.6.rest_0_.rest_1_.rest_2_.rest_3_.rest_4_.rest_5_.rest_6_.rest_7_, ...), custom_call_target="tpu_custom_call" | custom-call | flops 1073741824 | bytes 11534336 | tf_op jit(solution)/shard_map/pallas_call | solution.py:186
  288.0 157.2 %all-to-all-done.1 = bf16[256,2,64,128]{3,2,1,0:T(8,128)(2,1)} async-done(((bf16[256,2,64,128]{3,2,1,0:T(8,128)(2,1)}), bf16[256,2,64,128]{3,2,1,0:T(8,128)(2,1)}, u32[]{:S(2)}, u32[]{:S(2)}) %all-to-all-start.1) | async-done | bytes 8388640 | tf_op jit(solution)/shard_map/all_to_all | solution.py:256
  445.3 9.1 %shard_map.79 = f32[64,3072]{1,0:T(8,128)} custom-call(s32[512]{0:T(512)} %reshape.153.ids_ref, bf16[512,64,128]{2,1,0:T(8,128)(2,1)} %bitcast.11.piece_ref), custom_call_target="tpu_custom_call" | custom-call | tf_op jit(solution)/shard_map/pallas_call | solution.py:222
  (17 shorter events, 0.1 us)
Async XLA Ops:
  0.6 19.1 %copy-start = (bf16[3072,512]{1,0:T(8,128)(2,1)S(1)}, bf16[3072,512]{1,0:T(8,128)(2,1)}, u32[]{:S(2)}) copy-start(bf16[3072,512]{1,0:T(8,128)(2,1)} %param.6) | copy-start | bytes 9437188
  25.2 7.2 %copy-start.7 = (s32[8,8]{1,0:T(8,128)S(1)}, s32[8,8]{1,0:T(8,128)}, u32[]{:S(2)}) copy-start(s32[8,8]{1,0:T(8,128)} %param.7) | copy-start | bytes 772
  25.2 7.3 %copy-start.8 = (s32[1024]{0:T(1024)S(1)}, s32[1024]{0:T(1024)}, u32[]{:S(2)}) copy-start(s32[1024]{0:T(1024)} %param.9) | copy-start | bytes 12292
  25.2 195.2 %copy-start.5 = (s32[8]{0:T(128)S(1)}, s32[8]{0:T(128)}, u32[]{:S(2)}) copy-start(s32[8]{0:T(128)} %count_ref.1) | copy-start | bytes 100
  25.2 195.2 %all-to-all-start = ((bf16[32,2,128,512]{3,2,1,0:T(8,128)(2,1)}), bf16[32,2,128,512]{3,2,1,0:T(8,128)(2,1)}, u32[]{:S(2)}, u32[]{:S(2)}) async-start(bf16[32,2,128,512]{3,2,1,0:T(8,128)(2,1)} %bitcast.18), calls=%async_computation | async-start | bytes 16777216 | tf_op jit(solution)/shard_map/all_to_all | solution.py:248
  220.5 1.2 copy-start.1
  241.8 1.4 copy-start.3
  243.2 14.3 %copy-start.6 = (s32[32,2]{1,0:T(8,128)S(1)}, s32[32,2]{1,0:T(8,128)}, u32[]{:S(2)}) copy-start(s32[32,2]{1,0:T(8,128)} %shard_map.76) | copy-start | bytes 772
  243.2 202.1 %all-to-all-start.1 = ((bf16[256,2,64,128]{3,2,1,0:T(8,128)(2,1)}), bf16[256,2,64,128]{3,2,1,0:T(8,128)(2,1)}, u32[]{:S(2)}, u32[]{:S(2)}) async-start(bf16[256,2,64,128]{3,2,1,0:T(8,128)(2,1)} %bitcast.19), calls=%async_computation.1 | async-start | bytes 16777216 | tf_op jit(solution)/shard_map/all_to_all | solution.py:256
  275.9 1.2 copy-start.2
  277.1 1.6 copy-start.4

commit v10 on v9

--- a/solution.py
+++ b/solution.py
@@ -79,6 +79,14 @@
     tiles = rest[:K]
     loss_ref, score_ref, pair_hbm, pair_buf, pair_sem = rest[K:]
     b = pl.program_id(0)
+    last = pl.num_programs(0) - 1
+
+    def pending(par, k, slot):
+        return pltpu.make_async_copy(
+            pair_buf.at[par, :, pl.ds(k, 1)],
+            pair_hbm.at[:, pl.ds(slot, 1)],
+            pair_sem.at[par, k],
+        )
     emb = emb_ref[0].astype(jnp.float32)
     inverse_norm = lax.rsqrt(jnp.sum(emb * emb, axis=1, keepdims=True) + epsilon)
     unit_t = (emb * inverse_norm).astype(jnp.bfloat16).T
@@ -92,31 +100,41 @@
     peak = masked[0].max(axis=0, keepdims=True)
     for k in range(1, K):
         peak = jnp.maximum(peak, masked[k].max(axis=0, keepdims=True))
+    shifted = [jnp.exp(masked[k] - peak) for k in range(K)]
     total = jnp.zeros_like(peak)
     for k in range(K):
-        total = total + jnp.sum(jnp.exp(masked[k] - peak), axis=0, keepdims=True)
+        total = total + jnp.sum(shifted[k], axis=0, keepdims=True)
     log_total = peak + jnp.log(total)
     positive = jnp.sum(jnp.where(hit, logits[0], 0.0), axis=0, keepdims=True)
     loss_ref[0] = log_total - positive
-    for k in range(K):
-        probabilities = jnp.exp(masked[k] - log_total)
+    inverse_total = 1.0 / total
+    parity = b % 2
+
+    @pl.when(b >= 2)
+    def _():
+        for k in range(K):
+            pending(parity, k, 0).wait()
+
+    for k in range(K):
+        probabilities = shifted[k] * inverse_total
         if k == 0:
             probabilities = probabilities - jnp.where(hit, 1.0, 0.0)
         dscore = (logit_scale * probabilities).astype(jnp.bfloat16).T
         score_ref[0, k] = dscore
         pair_t = jnp.dot(unit_t, dscore, preferred_element_type=jnp.float32).astype(jnp.bfloat16)
-        pair_buf[:, k] = pair_t.reshape(pair_buf.shape[0], D // pair_buf.shape[0], TILE)
-    copies = []
-    for k in range(K):
-        cp = pltpu.make_async_copy(
-            pair_buf.at[:, pl.ds(k, 1)],
-            pair_hbm.at[:, pl.ds(slot_ref[b * K + k], 1)],
-            pair_sem.at[k],
-        )
-        cp.start()
-        copies.append(cp)
-    for cp in copies:
-        cp.wait()
+        pair_buf[parity, :, k] = pair_t.reshape(pair_buf.shape[1], D // pair_buf.shape[1], TILE)
+    for k in range(K):
+        pending(parity, k, slot_ref[b * K + k]).start()
+
+    @pl.when(b == last)
+    def _():
+        for k in range(K):
+            pending(parity, k, 0).wait()
+
+    @pl.when((b == last) & (b >= 1))
+    def _():
+        for k in range(K):
+            pending(1 - parity, k, 0).wait()
 
 
 def _embed_kernel(slot_ref, emb_ref, score_ref, *rest):
@@ -154,8 +172,8 @@
             pl.BlockSpec(memory_space=pl.ANY),
         ],
         scratch_shapes=[
-            pltpu.VMEM((parts, K, D // parts, TILE), jnp.bfloat16),
-            pltpu.SemaphoreType.DMA((K,)),
+            pltpu.VMEM((2, parts, K, D // parts, TILE), jnp.bfloat16),
+            pltpu.SemaphoreType.DMA((2, K)),
         ],
     )
     return pl.pallas_call(

time: 455 us -> 450 us (0.989)
  Pallas kernels: 53 us -> 47.5 us
    pallas_call x1, Pallas kernels: 20.1 us -> 14.6 us  [score_step(): pl.pallas_call(_score_kernel, grid_spec=grid_spec, out_shape=[jax.ShapeDt...]
where the time goes in v10:
time: 450 us; the launch traced here: 449 us
  waiting for transfers between devices  345 us (77%)
  Pallas kernels  47.5 us (11%)
  starting transfers between devices  21.1 us (5%)
  blocking collectives  17.6 us (4%)
  local copies, waits for them, and re-layouts  13.6 us (3%)
    all_to_all x1, waiting for transfers between devices, per_device(): lax.all_to_all(outgoing, 'cls', split_axis=0, concat_axis=0, tiled=True)  188 us
    all_to_all x1, waiting for transfers between devices, per_device(): lax.all_to_all(pair_grads, ('dp', 'cls'), split_axis=0, concat_axis=0, ti...  157 us
    all_gather x1, blocking collectives, per_device(): got_ids = lax.all_gather(wanted, 'dp').reshape(parts * pair_count)  17.6 us
    pallas_call x1, Pallas kernels, score_step(): pl.pallas_call(_score_kernel, grid_spec=grid_spec, out_shape=[jax.ShapeDt...  14.6 us
    pallas_call x1, Pallas kernels, cls_all_to_all(): pl.pallas_call(functools.partial(_a2a_kernel, n), out_shape=jax.ShapeDtyp...  14.5 us
    all_to_all x1, starting transfers between devices, per_device(): lax.all_to_all(pair_grads, ('dp', 'cls'), split_axis=0, concat_axis=0, ti...  13.9 us
    pallas_call x1, Pallas kernels, embed_step(): pl.pallas_call(_embed_kernel, grid_spec=grid_spec, out_shape=jax.ShapeDty...  9.31 us
    pallas_call x1, Pallas kernels, column_sum(): pl.pallas_call(_column_sum_kernel, grid_spec=grid_spec, out_shape=jax.Sha...  9.09 us
  transfers between devices with their start and end apart: 2, of which 2 were waited for; matrix products, arithmetic and copies ran while one was open for 0% of the time, Pallas kernels for 2%

profile of v10, /device:TPU:1, one launch (start us, length us, event | category | flops | bytes accessed | tf_op | source)
XLA Modules:
  0.0 448.7 jit_solution(9404282294850154318)
XLA Ops:
  0.6 0.0 copy-start
  0.6 0.8 sign_compare_fusion
  1.5 0.8 broadcast_remainder_fusion
  2.3 0.1 ne.51
  2.4 0.1 rem.30
  2.5 0.1 div.21
  2.6 0.2 select_reduce_fusion.1
  2.7 0.1 select_reduce_fusion
  2.9 0.8 gather_fusion
  3.7 0.7 reshape.149.src_ref
  4.4 14.5 %shard_map.76 = s32[32,2]{1,0:T(8,128)} custom-call(s32[32,2]{1,0:T(8,128)} %reshape.149.src_ref), custom_call_target="tpu_custom_call" | custom-call | tf_op jit(solution)/shard_map/pallas_call | solution.py:60
  18.8 0.7 compare_select_fusion
  19.6 0.1 reshape.166
  19.7 5.5 %gather_fusion.1 = bf16[64,128,512]{2,1,0:T(8,128)(2,1)} fusion(bf16[24,128,512]{2,1,0:T(8,128)(2,1)S(1)} %bitcast.15, s32[1024]{0:T(1024)S(1)} %pad_clamp_fusion), kind=kCustom, calls=%fused_computation.1 | custom fusion | bytes 16777472 | tf_op jit(solution)/shard_map/gather | solution.py:265
  25.2 7.2 %all-to-all-start = ((bf16[32,2,128,512]{3,2,1,0:T(8,128)(2,1)}), bf16[32,2,128,512]{3,2,1,0:T(8,128)(2,1)}, u32[]{:S(2)}, u32[]{:S(2)}) async-start(bf16[32,2,128,512]{3,2,1,0:T(8,128)(2,1)} %bitcast.18), calls=%async_computation | async-start | bytes 16777216 | tf_op jit(solution)/shard_map/all_to_all | solution.py:266
  32.5 0.1 multiply_reduce_fusion
  32.6 0.1 broadcast_subtract_fusion.pos_ref
  32.7 188.0 %all-to-all-done = bf16[32,2,128,512]{3,2,1,0:T(8,128)(2,1)} async-done(((bf16[32,2,128,512]{3,2,1,0:T(8,128)(2,1)}), bf16[32,2,128,512]{3,2,1,0:T(8,128)(2,1)}, u32[]{:S(2)}, u32[]{:S(2)}) %all-to-all-start) | async-done | bytes 8388640 | tf_op jit(solution)/shard_map/all_to_all | solution.py:266
  220.7 1.2 copy-done.1
  221.9 14.6 %shard_map.77 = (f32[8,1,128]{2,1,0:T(1,128)}, bf16[8,8,128,128]{3,2,1,0:T(8,128)(2,1)S(1)}, bf16[8,64,64,128]{3,2,1,0:T(8,128)(2,1)}) custom-call(s32[64]{0:T(128)S(1)} %multiply_add_fusion.slot_ref, s32[8]{0:T(128)S(1)} %copy-done.5, bf16[8,128,512]{2,1,0:T(8,128)(2,1)S(1)} %bitcast.16, s32[8,1,128]{2,1,0:T(1,128)S(1)} %broadcast_subtract_fusion.pos_ref, ...), custom_call_target="tpu_custom_call" | custom-call | tf_op jit(solution)/shard_map/pallas_call | solution.py:179
  236.5 0.0 copy-start.3
  236.5 1.3 copy-done.3
  237.8 13.9 %all-to-all-start.1 = ((bf16[256,2,64,128]{3,2,1,0:T(8,128)(2,1)}), bf16[256,2,64,128]{3,2,1,0:T(8,128)(2,1)}, u32[]{:S(2)}, u32[]{:S(2)}) async-start(bf16[256,2,64,128]{3,2,1,0:T(8,128)(2,1)} %bitcast.19), calls=%async_computation.1 | async-start | bytes 16777216 | tf_op jit(solution)/shard_map/all_to_all | solution.py:274
  251.8 0.1 copy.13
  251.9 17.6 %all-gather.1 = s32[8,32,2]{1,2,0:T(2,128)S(1)} all-gather(s32[1,32,2]{1,2,0:T(2,128)S(1)} %bitcast.22), channel_id=2, replica_groups=mesh['dp'=8,'cls'=32] {'dp'}, dimensions={0}, use_global_device_ids=true | all-gather | bytes 2304 | tf_op jit(solution)/shard_map/all_gather | solution.py:275
  269.4 0.1 copy.14
  269.6 0.7 reshape.153.ids_ref
  270.2 1.2 copy-done.2
  271.5 1.6 copy-done.4
  273.1 9.3 %shard_map.78 = bf16[8,128,512]{2,1,0:T(8,128)(2,1)} custom-call(s32[64]{0:T(128)S(1)} %multiply_add_fusion.slot_ref, bf16[8,128,512]{2,1,0:T(8,128)(2,1)S(1)} %bitcast.17, bf16[8,8,128,128]{3,2,1,0:T(8,128)(2,1)S(1)} %copy-done.4, bf16[64,128,512]{2,1,0:T(8,128)(2,1)} %bitcast.6.rest_0_.rest_1_.rest_2_.rest_3_.rest_4_.rest_5_.rest_6_.rest_7_, ...), custom_call_target="tpu_custom_call" | custom-call | flops 1073741824 | bytes 11534336 | tf_op jit(solution)/shard_map/pallas_call | solution.py:204
  282.4 157.2 %all-to-all-done.1 = bf16[256,2,64,128]{3,2,1,0:T(8,128)(2,1)} async-done(((bf16[256,2,64,128]{3,2,1,0:T(8,128)(2,1)}), bf16[256,2,64,128]{3,2,1,0:T(8,128)(2,1)}, u32[]{:S(2)}, u32[]{:S(2)}) %all-to-all-start.1) | async-done | bytes 8388640 | tf_op jit(solution)/shard_map/all_to_all | solution.py:274
  439.6 9.1 %shard_map.79 = f32[64,3072]{1,0:T(8,128)} custom-call(s32[512]{0:T(512)} %reshape.153.ids_ref, bf16[512,64,128]{2,1,0:T(8,128)(2,1)} %bitcast.11.piece_ref), custom_call_target="tpu_custom_call" | custom-call | tf_op jit(solution)/shard_map/pallas_call | solution.py:240
  (17 shorter events, 0.1 us)
Async XLA Ops:
  0.6 19.1 %copy-start = (bf16[3072,512]{1,0:T(8,128)(2,1)S(1)}, bf16[3072,512]{1,0:T(8,128)(2,1)}, u32[]{:S(2)}) copy-start(bf16[3072,512]{1,0:T(8,128)(2,1)} %param.6) | copy-start | bytes 9437188
  25.2 7.2 %copy-start.7 = (s32[8,8]{1,0:T(8,128)S(1)}, s32[8,8]{1,0:T(8,128)}, u32[]{:S(2)}) copy-start(s32[8,8]{1,0:T(8,128)} %param.7) | copy-start | bytes 772
  25.2 7.4 %copy-start.8 = (s32[1024]{0:T(1024)S(1)}, s32[1024]{0:T(1024)}, u32[]{:S(2)}) copy-start(s32[1024]{0:T(1024)} %param.9) | copy-start | bytes 12292
  25.2 195.4 %copy-start.5 = (s32[8]{0:T(128)S(1)}, s32[8]{0:T(128)}, u32[]{:S(2)}) copy-start(s32[8]{0:T(128)} %count_ref.1) | copy-start | bytes 100
  25.2 195.4 %all-to-all-start = ((bf16[32,2,128,512]{3,2,1,0:T(8,128)(2,1)}), bf16[32,2,128,512]{3,2,1,0:T(8,128)(2,1)}, u32[]{:S(2)}, u32[]{:S(2)}) async-start(bf16[32,2,128,512]{3,2,1,0:T(8,128)(2,1)} %bitcast.18), calls=%async_computation | async-start | bytes 16777216 | tf_op jit(solution)/shard_map/all_to_all | solution.py:266
  220.6 1.2 copy-start.1
  236.5 1.4 copy-start.3
  237.8 13.9 %copy-start.6 = (s32[32,2]{1,0:T(8,128)S(1)}, s32[32,2]{1,0:T(8,128)}, u32[]{:S(2)}) copy-start(s32[32,2]{1,0:T(8,128)} %shard_map.76) | copy-start | bytes 772
  237.8 201.8 %all-to-all-start.1 = ((bf16[256,2,64,128]{3,2,1,0:T(8,128)(2,1)}), bf16[256,2,64,128]{3,2,1,0:T(8,128)(2,1)}, u32[]{:S(2)}, u32[]{:S(2)}) async-start(bf16[256,2,64,128]{3,2,1,0:T(8,128)(2,1)} %bitcast.19), calls=%async_computation.1 | async-start | bytes 16777216 | tf_op jit(solution)/shard_map/all_to_all | solution.py:274
  270.2 1.2 copy-start.2
  271.5 1.6 copy-start.4

commit v11 on v10

--- a/solution.py
+++ b/solution.py
@@ -263,7 +263,9 @@
     tile_table = proxies.reshape(tile_dev, TILE, D)
     wanted = cls_all_to_all(request_ids, 0)
     outgoing = tile_table[wanted]
+    got_ids = lax.all_gather(wanted, "dp").reshape(-1)
     fetched = lax.all_to_all(outgoing, "cls", split_axis=0, concat_axis=0, tiled=True)
+    fetched, got_ids = lax.optimization_barrier((fetched, got_ids))
     fetched = fetched.reshape(pair_count, TILE, D)
     pos_cols = labels.reshape(blocks, 1, BR) - hard_tiles[:, None, 0:1] * TILE
     parts = lax.axis_size("dp")
@@ -272,7 +274,6 @@
     embed_grad = embed_step(slot_of, emb_blocks, scores, fetched)
     pair_grads = pair_grads.reshape(parts * groups, capacity, D // parts, TILE)
     returned = lax.all_to_all(pair_grads, ("dp", "cls"), split_axis=0, concat_axis=0, tiled=True)
-    got_ids = lax.all_gather(wanted, "dp").reshape(parts * pair_count)
     got_terms = returned.reshape(parts * pair_count, D // parts, TILE)
     proxy_share = column_sum(got_ids, got_terms, tile_dev).T
     return (loss.reshape(-1), embed_grad.reshape(-1, D), proxy_share)

time: 450 us -> 449 us (level)
  waiting for transfers between devices: 345 us -> 351 us
  blocking collectives: 17.6 us -> 12.6 us
    all_to_all x1, waiting for transfers between devices: 157 us -> 176 us  [per_device(): lax.all_to_all(pair_grads, ('dp', 'cls'), split_axis=0, concat_axis=0, ti...]
    all_to_all x1, waiting for transfers between devices: 188 us -> 176 us  [per_device(): lax.all_to_all(outgoing, 'cls', split_axis=0, concat_axis=0, tiled=True)]
    all_gather x1, blocking collectives: 17.6 us -> 12.6 us  [per_device(): got_ids = lax.all_gather(wanted, 'dp').reshape(-1)]
where the time goes in v11:
time: 449 us; the launch traced here: 448 us
  waiting for transfers between devices  351 us (78%)
  Pallas kernels  47.4 us (11%)
  starting transfers between devices  19.2 us (4%)
  local copies, waits for them, and re-layouts  13.7 us (3%)
  blocking collectives  12.6 us (3%)
    all_to_all x1, waiting for transfers between devices, per_device(): lax.all_to_all(pair_grads, ('dp', 'cls'), split_axis=0, concat_axis=0, ti...  176 us
    all_to_all x1, waiting for transfers between devices, per_device(): lax.all_to_all(outgoing, 'cls', split_axis=0, concat_axis=0, tiled=True)  176 us
    pallas_call x1, Pallas kernels, score_step(): pl.pallas_call(_score_kernel, grid_spec=grid_spec, out_shape=[jax.ShapeDt...  14.6 us
    pallas_call x1, Pallas kernels, cls_all_to_all(): pl.pallas_call(functools.partial(_a2a_kernel, n), out_shape=jax.ShapeDtyp...  14.5 us
    all_gather x1, blocking collectives, per_device(): got_ids = lax.all_gather(wanted, 'dp').reshape(-1)  12.6 us
    all_to_all x1, starting transfers between devices, per_device(): lax.all_to_all(pair_grads, ('dp', 'cls'), split_axis=0, concat_axis=0, ti...  11.9 us
    pallas_call x1, Pallas kernels, embed_step(): pl.pallas_call(_embed_kernel, grid_spec=grid_spec, out_shape=jax.ShapeDty...  9.31 us
    pallas_call x1, Pallas kernels, column_sum(): pl.pallas_call(_column_sum_kernel, grid_spec=grid_spec, out_shape=jax.Sha...  9.09 us
  transfers between devices with their start and end apart: 2, of which 2 were waited for; matrix products, arithmetic and copies ran while one was open for 0% of the time, Pallas kernels for 2%

profile of v11, /device:TPU:1, one launch (start us, length us, event | category | flops | bytes accessed | tf_op | source)
XLA Modules:
  0.0 447.9 jit_solution(15279362388527795597)
XLA Ops:
  0.6 0.0 copy-start
  0.6 0.8 sign_compare_fusion
  1.5 0.8 broadcast_remainder_fusion
  2.3 0.1 ne.51
  2.4 0.1 rem.30
  2.5 0.1 div.21
  2.6 0.2 select_reduce_fusion.1
  2.7 0.1 select_reduce_fusion
  2.9 0.8 gather_fusion
  3.7 0.7 reshape.149.src_ref
  4.4 14.5 %shard_map.76 = s32[32,2]{1,0:T(8,128)} custom-call(s32[32,2]{1,0:T(8,128)} %reshape.149.src_ref), custom_call_target="tpu_custom_call" | custom-call | tf_op jit(solution)/shard_map/pallas_call | solution.py:60
  18.8 0.7 compare_select_fusion
  19.6 0.1 reshape.166
  19.7 5.5 %gather_fusion.1 = bf16[64,128,512]{2,1,0:T(8,128)(2,1)} fusion(bf16[24,128,512]{2,1,0:T(8,128)(2,1)S(1)} %bitcast.15, s32[1024]{0:T(1024)S(1)} %pad_clamp_fusion), kind=kCustom, calls=%fused_computation.1 | custom fusion | bytes 16777472 | tf_op jit(solution)/shard_map/gather | solution.py:265
  25.2 7.3 %all-to-all-start = ((bf16[32,2,128,512]{3,2,1,0:T(8,128)(2,1)}), bf16[32,2,128,512]{3,2,1,0:T(8,128)(2,1)}, u32[]{:S(2)}, u32[]{:S(2)}) async-start(bf16[32,2,128,512]{3,2,1,0:T(8,128)(2,1)} %bitcast.18), calls=%async_computation | async-start | bytes 16777216 | tf_op jit(solution)/shard_map/all_to_all | solution.py:267
  32.6 0.1 copy.13
  32.7 12.6 %all-gather.1 = s32[8,32,2]{1,2,0:T(2,128)S(1)} all-gather(s32[1,32,2]{1,2,0:T(2,128)S(1)} %bitcast.22), channel_id=2, replica_groups=mesh['dp'=8,'cls'=32] {'dp'}, dimensions={0}, use_global_device_ids=true | all-gather | bytes 2304 | tf_op jit(solution)/shard_map/all_gather | solution.py:266
  45.3 0.1 copy.14
  45.4 0.7 reshape.150.ids_ref
  46.1 0.1 multiply_reduce_fusion
  46.2 0.1 broadcast_subtract_fusion.pos_ref
  46.3 175.6 %all-to-all-done = bf16[32,2,128,512]{3,2,1,0:T(8,128)(2,1)} async-done(((bf16[32,2,128,512]{3,2,1,0:T(8,128)(2,1)}), bf16[32,2,128,512]{3,2,1,0:T(8,128)(2,1)}, u32[]{:S(2)}, u32[]{:S(2)}) %all-to-all-start) | async-done | bytes 8388640 | tf_op jit(solution)/shard_map/all_to_all | solution.py:267
  221.9 1.2 copy-done.1
  223.1 14.6 %shard_map.77 = (f32[8,1,128]{2,1,0:T(1,128)}, bf16[8,8,128,128]{3,2,1,0:T(8,128)(2,1)S(1)}, bf16[8,64,64,128]{3,2,1,0:T(8,128)(2,1)}) custom-call(s32[64]{0:T(128)S(1)} %multiply_add_fusion.slot_ref, s32[8]{0:T(128)S(1)} %copy-done.5, bf16[8,128,512]{2,1,0:T(8,128)(2,1)S(1)} %bitcast.16, s32[8,1,128]{2,1,0:T(1,128)S(1)} %broadcast_subtract_fusion.pos_ref, ...), custom_call_target="tpu_custom_call" | custom-call | tf_op jit(solution)/shard_map/pallas_call | solution.py:179
  237.7 1.3 copy-done.3
  239.1 11.9 %all-to-all-start.1 = ((bf16[256,2,64,128]{3,2,1,0:T(8,128)(2,1)}), bf16[256,2,64,128]{3,2,1,0:T(8,128)(2,1)}, u32[]{:S(2)}, u32[]{:S(2)}) async-start(bf16[256,2,64,128]{3,2,1,0:T(8,128)(2,1)} %bitcast.19), calls=%async_computation.1 | async-start | bytes 16777216 | tf_op jit(solution)/shard_map/all_to_all | solution.py:276
  251.0 0.0 copy-start.2
  251.0 1.2 copy-done.2
  252.2 1.6 copy-done.4
  253.8 9.3 %shard_map.78 = bf16[8,128,512]{2,1,0:T(8,128)(2,1)} custom-call(s32[64]{0:T(128)S(1)} %multiply_add_fusion.slot_ref, bf16[8,128,512]{2,1,0:T(8,128)(2,1)S(1)} %bitcast.17, bf16[8,8,128,128]{3,2,1,0:T(8,128)(2,1)S(1)} %copy-done.4, bf16[64,128,512]{2,1,0:T(8,128)(2,1)} %bitcast.7.rest_0_.rest_1_.rest_2_.rest_3_.rest_4_.rest_5_.rest_6_.rest_7_, ...), custom_call_target="tpu_custom_call" | custom-call | flops 1073741824 | bytes 11534336 | tf_op jit(solution)/shard_map/pallas_call | solution.py:204
  263.1 175.7 %all-to-all-done.1 = bf16[256,2,64,128]{3,2,1,0:T(8,128)(2,1)} async-done(((bf16[256,2,64,128]{3,2,1,0:T(8,128)(2,1)}), bf16[256,2,64,128]{3,2,1,0:T(8,128)(2,1)}, u32[]{:S(2)}, u32[]{:S(2)}) %all-to-all-start.1) | async-done | bytes 8388640 | tf_op jit(solution)/shard_map/all_to_all | solution.py:276
  438.8 9.1 %shard_map.79 = f32[64,3072]{1,0:T(8,128)} custom-call(s32[512]{0:T(512)} %reshape.150.ids_ref, bf16[512,64,128]{2,1,0:T(8,128)(2,1)} %bitcast.11.piece_ref), custom_call_target="tpu_custom_call" | custom-call | tf_op jit(solution)/shard_map/pallas_call | solution.py:240
  (17 shorter events, 0.1 us)
Async XLA Ops:
  0.6 19.1 %copy-start = (bf16[3072,512]{1,0:T(8,128)(2,1)S(1)}, bf16[3072,512]{1,0:T(8,128)(2,1)}, u32[]{:S(2)}) copy-start(bf16[3072,512]{1,0:T(8,128)(2,1)} %param.6) | copy-start | bytes 9437188
  25.2 7.4 %copy-start.6 = (s32[32,2]{1,0:T(8,128)S(1)}, s32[32,2]{1,0:T(8,128)}, u32[]{:S(2)}) copy-start(s32[32,2]{1,0:T(8,128)} %shard_map.76) | copy-start | bytes 772
  25.2 20.8 %copy-start.7 = (s32[8,8]{1,0:T(8,128)S(1)}, s32[8,8]{1,0:T(8,128)}, u32[]{:S(2)}) copy-start(s32[8,8]{1,0:T(8,128)} %param.7) | copy-start | bytes 772
  25.2 20.9 %copy-start.8 = (s32[1024]{0:T(1024)S(1)}, s32[1024]{0:T(1024)}, u32[]{:S(2)}) copy-start(s32[1024]{0:T(1024)} %param.9) | copy-start | bytes 12292
  25.2 196.7 %copy-start.5 = (s32[8]{0:T(128)S(1)}, s32[8]{0:T(128)}, u32[]{:S(2)}) copy-start(s32[8]{0:T(128)} %count_ref.1) | copy-start | bytes 100
  25.2 196.6 %all-to-all-start = ((bf16[32,2,128,512]{3,2,1,0:T(8,128)(2,1)}), bf16[32,2,128,512]{3,2,1,0:T(8,128)(2,1)}, u32[]{:S(2)}, u32[]{:S(2)}) async-start(bf16[32,2,128,512]{3,2,1,0:T(8,128)(2,1)} %bitcast.18), calls=%async_computation | async-start | bytes 16777216 | tf_op jit(solution)/shard_map/all_to_all | solution.py:267
  221.9 1.2 copy-start.1
  237.7 1.4 copy-start.3
  239.1 199.8 %all-to-all-start.1 = ((bf16[256,2,64,128]{3,2,1,0:T(8,128)(2,1)}), bf16[256,2,64,128]{3,2,1,0:T(8,128)(2,1)}, u32[]{:S(2)}, u32[]{:S(2)}) async-start(bf16[256,2,64,128]{3,2,1,0:T(8,128)(2,1)} %bitcast.19), calls=%async_computation.1 | async-start | bytes 16777216 | tf_op jit(solution)/shard_map/all_to_all | solution.py:276
  251.0 1.2 copy-start.2
  252.2 1.6 copy-start.4

commit v12 on v10

--- a/solution.py
+++ b/solution.py
@@ -19,15 +19,6 @@
 def _a2a_kernel(n, src_ref, out_ref, send_sem, recv_sem, local_sem):
     me = lax.axis_index("cls")
     row = lax.axis_index("dp")
-    barrier = pltpu.get_barrier_semaphore()
-
-    def greet(j, carry):
-        peer = lax.rem(me + j, n)
-        pl.semaphore_signal(barrier, inc=1, device_id=(row, peer), device_id_type=MESH)
-        return carry
-
-    lax.fori_loop(1, n, greet, 0)
-    pl.semaphore_wait(barrier, n - 1)
     local = pltpu.make_async_copy(src_ref.at[me], out_ref.at[me], local_sem)
     local.start()
 
@@ -55,7 +46,7 @@
     local.wait()
 
 
-def cls_all_to_all(x, cid):
+def cls_all_to_all(x):
     n = x.shape[0]
     return pl.pallas_call(
         functools.partial(_a2a_kernel, n),
@@ -67,7 +58,7 @@
             pltpu.SemaphoreType.DMA((n,)),
             pltpu.SemaphoreType.DMA,
         ],
-        compiler_params=pltpu.CompilerParams(collective_id=cid, has_side_effects=True),
+        compiler_params=pltpu.CompilerParams(has_side_effects=True),
     )(x)
 
 
@@ -261,7 +252,7 @@
     holder = jnp.sum(jnp.where(slot_of[None, :] == counter[:, None], counter[None, :], 0), axis=1)
     request_ids = local_ids[holder].reshape(groups, capacity)
     tile_table = proxies.reshape(tile_dev, TILE, D)
-    wanted = cls_all_to_all(request_ids, 0)
+    wanted = cls_all_to_all(request_ids)
     outgoing = tile_table[wanted]
     fetched = lax.all_to_all(outgoing, "cls", split_axis=0, concat_axis=0, tiled=True)
     fetched = fetched.reshape(pair_count, TILE, D)

time: 450 us -> 459 us (1.020)
  Pallas kernels: 47.5 us -> 57.3 us
    pallas_call x1, Pallas kernels: 14.5 us -> 24.4 us  [cls_all_to_all(): pl.pallas_call(functools.partial(_a2a_kernel, n), out_shape=jax.ShapeDtyp...]
where the time goes in v12:
time: 459 us; the launch traced here: 457 us
  waiting for transfers between devices  345 us (75%)
  Pallas kernels  57.3 us (12%)
  starting transfers between devices  20.7 us (5%)
  blocking collectives  17.6 us (4%)
  local copies, waits for them, and re-layouts  13.6 us (3%)
    all_to_all x1, waiting for transfers between devices, per_device(): lax.all_to_all(outgoing, 'cls', split_axis=0, concat_axis=0, tiled=True)  187 us
    all_to_all x1, waiting for transfers between devices, per_device(): lax.all_to_all(pair_grads, ('dp', 'cls'), split_axis=0, concat_axis=0, ti...  157 us
    pallas_call x1, Pallas kernels, cls_all_to_all(): pl.pallas_call(functools.partial(_a2a_kernel, n), out_shape=jax.ShapeDtyp...  24.4 us
    all_gather x1, blocking collectives, per_device(): got_ids = lax.all_gather(wanted, 'dp').reshape(parts * pair_count)  17.6 us
    all_to_all x1, starting transfers between devices, per_device(): lax.all_to_all(pair_grads, ('dp', 'cls'), split_axis=0, concat_axis=0, ti...  15.6 us
    pallas_call x1, Pallas kernels, score_step(): pl.pallas_call(_score_kernel, grid_spec=grid_spec, out_shape=[jax.ShapeDt...  14.6 us
    pallas_call x1, Pallas kernels, embed_step(): pl.pallas_call(_embed_kernel, grid_spec=grid_spec, out_shape=jax.ShapeDty...  9.31 us
  transfers between devices with their start and end apart: 2, of which 2 were waited for; matrix products, arithmetic and copies ran while one was open for 0% of the time, Pallas kernels for 2%

profile of v12, /device:TPU:1, one launch (start us, length us, event | category | flops | bytes accessed | tf_op | source)
XLA Modules:
  0.0 457.5 jit_solution(17990332234098433108)
XLA Ops:
  0.6 0.0 copy-start
  0.6 0.8 sign_compare_fusion
  1.5 0.8 broadcast_remainder_fusion
  2.3 0.1 ne.51
  2.4 0.1 rem.30
  2.5 0.1 div.21
  2.6 0.2 select_reduce_fusion.1
  2.7 0.1 select_reduce_fusion
  2.9 0.8 gather_fusion
  3.7 0.7 reshape.149.src_ref
  4.4 24.4 %shard_map.76 = s32[32,2]{1,0:T(8,128)} custom-call(s32[32,2]{1,0:T(8,128)} %reshape.149.src_ref), custom_call_target="tpu_custom_call" | custom-call | tf_op jit(solution)/shard_map/pallas_call | solution.py:51
  28.8 0.7 compare_select_fusion
  29.5 0.1 reshape.166
  29.6 5.5 %gather_fusion.1 = bf16[64,128,512]{2,1,0:T(8,128)(2,1)} fusion(bf16[24,128,512]{2,1,0:T(8,128)(2,1)S(1)} %bitcast.15, s32[1024]{0:T(1024)S(1)} %pad_clamp_fusion), kind=kCustom, calls=%fused_computation.1 | custom fusion | bytes 16777472 | tf_op jit(solution)/shard_map/gather | solution.py:256
  35.1 5.1 %all-to-all-start = ((bf16[32,2,128,512]{3,2,1,0:T(8,128)(2,1)}), bf16[32,2,128,512]{3,2,1,0:T(8,128)(2,1)}, u32[]{:S(2)}, u32[]{:S(2)}) async-start(bf16[32,2,128,512]{3,2,1,0:T(8,128)(2,1)} %bitcast.18), calls=%async_computation | async-start | bytes 16777216 | tf_op jit(solution)/shard_map/all_to_all | solution.py:257
  40.2 0.1 multiply_reduce_fusion
  40.4 0.1 broadcast_subtract_fusion.pos_ref
  40.4 187.3 %all-to-all-done = bf16[32,2,128,512]{3,2,1,0:T(8,128)(2,1)} async-done(((bf16[32,2,128,512]{3,2,1,0:T(8,128)(2,1)}), bf16[32,2,128,512]{3,2,1,0:T(8,128)(2,1)}, u32[]{:S(2)}, u32[]{:S(2)}) %all-to-all-start) | async-done | bytes 8388640 | tf_op jit(solution)/shard_map/all_to_all | solution.py:257
  227.8 0.0 copy-done.5
  227.8 1.2 copy-done.1
  229.0 14.6 %shard_map.77 = (f32[8,1,128]{2,1,0:T(1,128)}, bf16[8,8,128,128]{3,2,1,0:T(8,128)(2,1)S(1)}, bf16[8,64,64,128]{3,2,1,0:T(8,128)(2,1)}) custom-call(s32[64]{0:T(128)S(1)} %multiply_add_fusion.slot_ref, s32[8]{0:T(128)S(1)} %copy-done.5, bf16[8,128,512]{2,1,0:T(8,128)(2,1)S(1)} %bitcast.16, s32[8,1,128]{2,1,0:T(1,128)S(1)} %broadcast_subtract_fusion.pos_ref, ...), custom_call_target="tpu_custom_call" | custom-call | tf_op jit(solution)/shard_map/pallas_call | solution.py:170
  243.6 1.3 copy-done.3
  244.9 15.6 %all-to-all-start.1 = ((bf16[256,2,64,128]{3,2,1,0:T(8,128)(2,1)}), bf16[256,2,64,128]{3,2,1,0:T(8,128)(2,1)}, u32[]{:S(2)}, u32[]{:S(2)}) async-start(bf16[256,2,64,128]{3,2,1,0:T(8,128)(2,1)} %bitcast.19), calls=%async_computation.1 | async-start | bytes 16777216 | tf_op jit(solution)/shard_map/all_to_all | solution.py:265
  260.6 0.1 copy.13
  260.6 17.6 %all-gather.1 = s32[8,32,2]{1,2,0:T(2,128)S(1)} all-gather(s32[1,32,2]{1,2,0:T(2,128)S(1)} %bitcast.22), channel_id=2, replica_groups=mesh['dp'=8,'cls'=32] {'dp'}, dimensions={0}, use_global_device_ids=true | all-gather | bytes 2304 | tf_op jit(solution)/shard_map/all_gather | solution.py:266
  278.2 0.1 copy.14
  278.4 0.7 reshape.153.ids_ref
  279.0 1.2 copy-done.2
  280.2 1.6 copy-done.4
  281.8 9.3 %shard_map.78 = bf16[8,128,512]{2,1,0:T(8,128)(2,1)} custom-call(s32[64]{0:T(128)S(1)} %multiply_add_fusion.slot_ref, bf16[8,128,512]{2,1,0:T(8,128)(2,1)S(1)} %bitcast.17, bf16[8,8,128,128]{3,2,1,0:T(8,128)(2,1)S(1)} %copy-done.4, bf16[64,128,512]{2,1,0:T(8,128)(2,1)} %bitcast.6.rest_0_.rest_1_.rest_2_.rest_3_.rest_4_.rest_5_.rest_6_.rest_7_, ...), custom_call_target="tpu_custom_call" | custom-call | flops 1073741824 | bytes 11534336 | tf_op jit(solution)/shard_map/pallas_call | solution.py:195
  291.1 157.2 %all-to-all-done.1 = bf16[256,2,64,128]{3,2,1,0:T(8,128)(2,1)} async-done(((bf16[256,2,64,128]{3,2,1,0:T(8,128)(2,1)}), bf16[256,2,64,128]{3,2,1,0:T(8,128)(2,1)}, u32[]{:S(2)}, u32[]{:S(2)}) %all-to-all-start.1) | async-done | bytes 8388640 | tf_op jit(solution)/shard_map/all_to_all | solution.py:265
  448.4 9.1 %shard_map.79 = f32[64,3072]{1,0:T(8,128)} custom-call(s32[512]{0:T(512)} %reshape.153.ids_ref, bf16[512,64,128]{2,1,0:T(8,128)(2,1)} %bitcast.11.piece_ref), custom_call_target="tpu_custom_call" | custom-call | tf_op jit(solution)/shard_map/pallas_call | solution.py:231
  (17 shorter events, 0.1 us)
Async XLA Ops:
  0.6 29.0 %copy-start = (bf16[3072,512]{1,0:T(8,128)(2,1)S(1)}, bf16[3072,512]{1,0:T(8,128)(2,1)}, u32[]{:S(2)}) copy-start(bf16[3072,512]{1,0:T(8,128)(2,1)} %param.6) | copy-start | bytes 9437188
  35.1 5.1 %copy-start.7 = (s32[8,8]{1,0:T(8,128)S(1)}, s32[8,8]{1,0:T(8,128)}, u32[]{:S(2)}) copy-start(s32[8,8]{1,0:T(8,128)} %param.7) | copy-start | bytes 772
  35.1 5.2 %copy-start.8 = (s32[1024]{0:T(1024)S(1)}, s32[1024]{0:T(1024)}, u32[]{:S(2)}) copy-start(s32[1024]{0:T(1024)} %param.9) | copy-start | bytes 12292
  35.1 192.6 %copy-start.5 = (s32[8]{0:T(128)S(1)}, s32[8]{0:T(128)}, u32[]{:S(2)}) copy-start(s32[8]{0:T(128)} %count_ref.1) | copy-start | bytes 100
  35.1 192.6 %all-to-all-start = ((bf16[32,2,128,512]{3,2,1,0:T(8,128)(2,1)}), bf16[32,2,128,512]{3,2,1,0:T(8,128)(2,1)}, u32[]{:S(2)}, u32[]{:S(2)}) async-start(bf16[32,2,128,512]{3,2,1,0:T(8,128)(2,1)} %bitcast.18), calls=%async_computation | async-start | bytes 16777216 | tf_op jit(solution)/shard_map/all_to_all | solution.py:257
  227.8 1.2 copy-start.1
  243.6 1.4 copy-start.3
  244.9 15.6 %copy-start.6 = (s32[32,2]{1,0:T(8,128)S(1)}, s32[32,2]{1,0:T(8,128)}, u32[]{:S(2)}) copy-start(s32[32,2]{1,0:T(8,128)} %shard_map.76) | copy-start | bytes 772
  244.9 203.5 %all-to-all-start.1 = ((bf16[256,2,64,128]{3,2,1,0:T(8,128)(2,1)}), bf16[256,2,64,128]{3,2,1,0:T(8,128)(2,1)}, u32[]{:S(2)}, u32[]{:S(2)}) async-start(bf16[256,2,64,128]{3,2,1,0:T(8,128)(2,1)} %bitcast.19), calls=%async_computation.1 | async-start | bytes 16777216 | tf_op jit(solution)/shard_map/all_to_all | solution.py:265
  279.0 1.2 copy-start.2
  280.2 1.6 copy-start.4

commit v13 on v10

--- a/solution.py
+++ b/solution.py
@@ -75,22 +75,11 @@
 epsilon = 1e-06
 
 
-def _score_kernel(slot_ref, count_ref, emb_ref, pos_ref, *rest):
-    tiles = rest[:K]
-    loss_ref, score_ref, pair_hbm, pair_buf, pair_sem = rest[K:]
-    b = pl.program_id(0)
-    last = pl.num_programs(0) - 1
-
-    def pending(par, k, slot):
-        return pltpu.make_async_copy(
-            pair_buf.at[par, :, pl.ds(k, 1)],
-            pair_hbm.at[:, pl.ds(slot, 1)],
-            pair_sem.at[par, k],
-        )
+def _block_scores(emb_ref, pos_ref, count, tiles):
     emb = emb_ref[0].astype(jnp.float32)
     inverse_norm = lax.rsqrt(jnp.sum(emb * emb, axis=1, keepdims=True) + epsilon)
-    unit_t = (emb * inverse_norm).astype(jnp.bfloat16).T
-    count = count_ref[b]
+    unit_exact = emb * inverse_norm
+    unit_t = unit_exact.astype(jnp.bfloat16).T
     classes = lax.broadcasted_iota(jnp.int32, (TILE, BR), 0)
     hit = classes == pos_ref[0]
     logits = []
@@ -106,46 +95,63 @@
         total = total + jnp.sum(shifted[k], axis=0, keepdims=True)
     log_total = peak + jnp.log(total)
     positive = jnp.sum(jnp.where(hit, logits[0], 0.0), axis=0, keepdims=True)
-    loss_ref[0] = log_total - positive
     inverse_total = 1.0 / total
-    parity = b % 2
-
-    @pl.when(b >= 2)
-    def _():
-        for k in range(K):
-            pending(parity, k, 0).wait()
-
+    scores = []
     for k in range(K):
         probabilities = shifted[k] * inverse_total
         if k == 0:
             probabilities = probabilities - jnp.where(hit, 1.0, 0.0)
-        dscore = (logit_scale * probabilities).astype(jnp.bfloat16).T
-        score_ref[0, k] = dscore
-        pair_t = jnp.dot(unit_t, dscore, preferred_element_type=jnp.float32).astype(jnp.bfloat16)
-        pair_buf[parity, :, k] = pair_t.reshape(pair_buf.shape[1], D // pair_buf.shape[1], TILE)
-    for k in range(K):
-        pending(parity, k, slot_ref[b * K + k]).start()
-
-    @pl.when(b == last)
+        scores.append((logit_scale * probabilities).astype(jnp.bfloat16).T)
+    return unit_exact, inverse_norm, unit_t, log_total - positive, scores
+
+
+def _score_kernel(slot_ref, count_ref, emb_ref, pos_ref, *rest):
+    tiles = rest[:K]
+    loss_ref, pair_hbm, pair_buf, pair_sem = rest[K:]
+    b = pl.program_id(0)
+    last = pl.num_programs(0) - 1
+
+    def pending(par, k, slot):
+        return pltpu.make_async_copy(
+            pair_buf.at[par, :, pl.ds(k, 1)],
+            pair_hbm.at[:, pl.ds(slot, 1)],
+            pair_sem.at[par, k],
+        )
+
+    _, _, unit_t, loss, scores = _block_scores(emb_ref, pos_ref, count_ref[b], tiles)
+    loss_ref[0] = loss
+    parity = b % 2
+
+    @pl.when(b >= 2)
     def _():
         for k in range(K):
             pending(parity, k, 0).wait()
 
+    for k in range(K):
+        pair_t = jnp.dot(unit_t, scores[k], preferred_element_type=jnp.float32).astype(jnp.bfloat16)
+        pair_buf[parity, :, k] = pair_t.reshape(pair_buf.shape[1], D // pair_buf.shape[1], TILE)
+    for k in range(K):
+        pending(parity, k, slot_ref[b * K + k]).start()
+
+    @pl.when(b == last)
+    def _():
+        for k in range(K):
+            pending(parity, k, 0).wait()
+
     @pl.when((b == last) & (b >= 1))
     def _():
         for k in range(K):
             pending(1 - parity, k, 0).wait()
 
 
-def _embed_kernel(slot_ref, emb_ref, score_ref, *rest):
+def _embed_kernel(slot_ref, count_ref, emb_ref, pos_ref, *rest):
     tiles = rest[:K]
     (grad_ref,) = rest[K:]
-    emb = emb_ref[0].astype(jnp.float32)
-    inverse_norm = lax.rsqrt(jnp.sum(emb * emb, axis=1, keepdims=True) + epsilon)
-    unit_exact = emb * inverse_norm
+    b = pl.program_id(0)
+    unit_exact, inverse_norm, _, _, scores = _block_scores(emb_ref, pos_ref, count_ref[b], tiles)
     grad_unit = jnp.zeros((BR, D), jnp.float32)
     for k in range(K):
-        terms = jnp.dot(score_ref[0, k], tiles[k][0], preferred_element_type=jnp.float32)
+        terms = jnp.dot(scores[k], tiles[k][0], preferred_element_type=jnp.float32)
         grad_unit = grad_unit + terms.astype(jnp.bfloat16).astype(jnp.float32)
     radial = jnp.sum(unit_exact * grad_unit, axis=1, keepdims=True)
     grad_ref[0] = ((grad_unit - unit_exact * radial) * inverse_norm).astype(grad_ref.dtype)
@@ -168,7 +174,6 @@
         + [_tile_spec(k) for k in range(K)],
         out_specs=[
             pl.BlockSpec((1, 1, BR), lambda b, slot, cnt: (b, 0, 0)),
-            pl.BlockSpec((1, K, BR, TILE), lambda b, slot, cnt: (b, 0, 0, 0)),
             pl.BlockSpec(memory_space=pl.ANY),
         ],
         scratch_shapes=[
@@ -181,35 +186,34 @@
         grid_spec=grid_spec,
         out_shape=[
             jax.ShapeDtypeStruct((blocks, 1, BR), jnp.float32),
-            jax.ShapeDtypeStruct((blocks, K, BR, TILE), jnp.bfloat16),
             jax.ShapeDtypeStruct((parts, pairs, D // parts, TILE), jnp.bfloat16),
         ],
         compiler_params=pltpu.CompilerParams(vmem_limit_bytes=48 * 1024 * 1024),
     )(slot_of, tile_count, emb_blocks, pos_cols, *([fetched] * K))
 
 
-def embed_step(slot_of, emb_blocks, scores, fetched):
+def embed_step(slot_of, tile_count, emb_blocks, pos_cols, fetched):
     blocks = emb_blocks.shape[0]
     grid_spec = pltpu.PrefetchScalarGridSpec(
-        num_scalar_prefetch=1,
+        num_scalar_prefetch=2,
         grid=(blocks,),
         in_specs=[
-            pl.BlockSpec((1, BR, D), lambda b, slot: (b, 0, 0)),
-            pl.BlockSpec((1, K, BR, TILE), lambda b, slot: (b, 0, 0, 0)),
+            pl.BlockSpec((1, BR, D), lambda b, slot, cnt: (b, 0, 0)),
+            pl.BlockSpec((1, 1, BR), lambda b, slot, cnt: (b, 0, 0)),
         ]
         + [_tile_spec(k) for k in range(K)],
-        out_specs=pl.BlockSpec((1, BR, D), lambda b, slot: (b, 0, 0)),
-    )
-    flops = blocks * K * 2 * BR * TILE * D
+        out_specs=pl.BlockSpec((1, BR, D), lambda b, slot, cnt: (b, 0, 0)),
+    )
+    flops = blocks * K * 4 * BR * TILE * D
     return pl.pallas_call(
         _embed_kernel,
         grid_spec=grid_spec,
         out_shape=jax.ShapeDtypeStruct((blocks, BR, D), jnp.bfloat16),
         compiler_params=pltpu.CompilerParams(vmem_limit_bytes=48 * 1024 * 1024),
         cost_estimate=pl.CostEstimate(
-            flops=flops, transcendentals=0, bytes_accessed=blocks * (K + 3) * TILE * D * 2
+            flops=flops, transcendentals=blocks * K * BR * TILE, bytes_accessed=blocks * (K + 2) * TILE * D * 2
         ),
-    )(slot_of, emb_blocks, scores, *([fetched] * K))
+    )(slot_of, tile_count, emb_blocks, pos_cols, *([fetched] * K))
 
 
 def _column_sum_kernel(ids_ref, piece_ref, out_ref):
@@ -268,8 +272,8 @@
     pos_cols = labels.reshape(blocks, 1, BR) - hard_tiles[:, None, 0:1] * TILE
     parts = lax.axis_size("dp")
     emb_blocks = embeddings.reshape(blocks, BR, D)
-    loss, scores, pair_grads = score_step(slot_of, tile_count, emb_blocks, pos_cols, fetched, parts)
-    embed_grad = embed_step(slot_of, emb_blocks, scores, fetched)
+    loss, pair_grads = score_step(slot_of, tile_count, emb_blocks, pos_cols, fetched, parts)
+    embed_grad = embed_step(slot_of, tile_count, emb_blocks, pos_cols, fetched)
     pair_grads = pair_grads.reshape(parts * groups, capacity, D // parts, TILE)
     returned = lax.all_to_all(pair_grads, ("dp", "cls"), split_axis=0, concat_axis=0, tiled=True)
     got_ids = lax.all_gather(wanted, "dp").reshape(parts * pair_count)

time: 450 us -> 448 us (level)
  transfers between devices with their start and end apart: 2 -> 2, of which waited for: 2 -> 2; matrix products, arithmetic and copies ran while one was open for 0% -> 0% of each run, Pallas kernels for 2% -> 3%
where the time goes in v13:
time: 448 us; the launch traced here: 447 us
  waiting for transfers between devices  343 us (77%)
  Pallas kernels  51 us (11%)
  starting transfers between devices  21.5 us (5%)
  blocking collectives  17.6 us (4%)
  local copies, waits for them, and re-layouts  10.8 us (2%)
    all_to_all x1, waiting for transfers between devices, per_device(): lax.all_to_all(outgoing, 'cls', split_axis=0, concat_axis=0, tiled=True)  188 us
    all_to_all x1, waiting for transfers between devices, per_device(): lax.all_to_all(pair_grads, ('dp', 'cls'), split_axis=0, concat_axis=0, ti...  155 us
    all_gather x1, blocking collectives, per_device(): got_ids = lax.all_gather(wanted, 'dp').reshape(parts * pair_count)  17.6 us
    pallas_call x1, Pallas kernels, score_step(): pl.pallas_call(_score_kernel, grid_spec=grid_spec, out_shape=[jax.ShapeDt...  14.6 us
    pallas_call x1, Pallas kernels, cls_all_to_all(): pl.pallas_call(functools.partial(_a2a_kernel, n), out_shape=jax.ShapeDtyp...  14.3 us
    all_to_all x1, starting transfers between devices, per_device(): lax.all_to_all(pair_grads, ('dp', 'cls'), split_axis=0, concat_axis=0, ti...  14.1 us
    pallas_call x1, Pallas kernels, embed_step(): pl.pallas_call(_embed_kernel, grid_spec=grid_spec, out_shape=jax.ShapeDty...  13 us
    pallas_call x1, Pallas kernels, column_sum(): pl.pallas_call(_column_sum_kernel, grid_spec=grid_spec, out_shape=jax.Sha...  9.09 us
  transfers between devices with their start and end apart: 2, of which 2 were waited for; matrix products, arithmetic and copies ran while one was open for 0% of the time, Pallas kernels for 3%

profile of v13, /device:TPU:1, one launch (start us, length us, event | category | flops | bytes accessed | tf_op | source)
XLA Modules:
  0.0 447.5 jit_solution(15652017147849001543)
XLA Ops:
  0.6 0.0 copy-start
  0.6 0.8 sign_compare_fusion
  1.5 0.8 broadcast_remainder_fusion
  2.3 0.1 ne.51
  2.4 0.1 rem.30
  2.5 0.1 div.21
  2.6 0.2 select_reduce_fusion.1
  2.7 0.1 select_reduce_fusion
  2.9 0.8 gather_fusion
  3.7 0.7 reshape.149.src_ref
  4.4 14.3 %shard_map.76 = s32[32,2]{1,0:T(8,128)} custom-call(s32[32,2]{1,0:T(8,128)} %reshape.149.src_ref), custom_call_target="tpu_custom_call" | custom-call | tf_op jit(solution)/shard_map/pallas_call | solution.py:60
  18.7 0.7 compare_select_fusion
  19.4 0.1 reshape.166
  19.5 0.0 copy-done
  19.5 5.5 %gather_fusion.1 = bf16[64,128,512]{2,1,0:T(8,128)(2,1)} fusion(bf16[24,128,512]{2,1,0:T(8,128)(2,1)S(1)} %bitcast.15, s32[1024]{0:T(1024)S(1)} %pad_clamp_fusion), kind=kCustom, calls=%fused_computation.1 | custom fusion | bytes 16777472 | tf_op jit(solution)/shard_map/gather | solution.py:269
  25.1 7.3 %all-to-all-start = ((bf16[32,2,128,512]{3,2,1,0:T(8,128)(2,1)}), bf16[32,2,128,512]{3,2,1,0:T(8,128)(2,1)}, u32[]{:S(2)}, u32[]{:S(2)}) async-start(bf16[32,2,128,512]{3,2,1,0:T(8,128)(2,1)} %bitcast.18), calls=%async_computation | async-start | bytes 16777216 | tf_op jit(solution)/shard_map/all_to_all | solution.py:270
  32.4 0.0 copy-done.5
  32.4 0.1 multiply_reduce_fusion
  32.5 0.1 broadcast_subtract_fusion.pos_ref
  32.6 187.9 %all-to-all-done = bf16[32,2,128,512]{3,2,1,0:T(8,128)(2,1)} async-done(((bf16[32,2,128,512]{3,2,1,0:T(8,128)(2,1)}), bf16[32,2,128,512]{3,2,1,0:T(8,128)(2,1)}, u32[]{:S(2)}, u32[]{:S(2)}) %all-to-all-start) | async-done | bytes 8388640 | tf_op jit(solution)/shard_map/all_to_all | solution.py:270
  220.5 1.2 copy-done.1
  221.8 14.6 %shard_map.77 = (f32[8,1,128]{2,1,0:T(1,128)}, bf16[8,64,64,128]{3,2,1,0:T(8,128)(2,1)}) custom-call(s32[64]{0:T(128)S(1)} %multiply_add_fusion.slot_ref, s32[8]{0:T(128)S(1)} %copy-done.3, bf16[8,128,512]{2,1,0:T(8,128)(2,1)S(1)} %bitcast.16, s32[8,1,128]{2,1,0:T(1,128)S(1)} %broadcast_subtract_fusion.pos_ref, ...), custom_call_target="tpu_custom_call" | custom-call | tf_op jit(solution)/shard_map/pallas_call | solution.py:184
  236.4 0.0 copy-start.4
  236.4 14.1 %all-to-all-start.1 = ((bf16[256,2,64,128]{3,2,1,0:T(8,128)(2,1)}), bf16[256,2,64,128]{3,2,1,0:T(8,128)(2,1)}, u32[]{:S(2)}, u32[]{:S(2)}) async-start(bf16[256,2,64,128]{3,2,1,0:T(8,128)(2,1)} %bitcast.19), calls=%async_computation.1 | async-start | bytes 16777216 | tf_op jit(solution)/shard_map/all_to_all | solution.py:278
  250.5 0.1 copy.13
  250.6 17.6 %all-gather.1 = s32[8,32,2]{1,2,0:T(2,128)S(1)} all-gather(s32[1,32,2]{1,2,0:T(2,128)S(1)} %bitcast.22), channel_id=2, replica_groups=mesh['dp'=8,'cls'=32] {'dp'}, dimensions={0}, use_global_device_ids=true | all-gather | bytes 2304 | tf_op jit(solution)/shard_map/all_gather | solution.py:279
  268.2 0.1 copy.14
  268.3 0.7 reshape.153.ids_ref
  269.1 1.2 copy-done.2
  270.3 13.0 %shard_map.78 = bf16[8,128,512]{2,1,0:T(8,128)(2,1)} custom-call(s32[64]{0:T(128)S(1)} %multiply_add_fusion.slot_ref, s32[8]{0:T(128)S(1)} %copy-done.3, bf16[8,128,512]{2,1,0:T(8,128)(2,1)S(1)} %bitcast.17, s32[8,1,128]{2,1,0:T(1,128)S(1)} %broadcast_subtract_fusion.pos_ref, ...), custom_call_target="tpu_custom_call" | custom-call | flops 2147483648 | bytes 10485760 | tf_op jit(solution)/shard_map/pallas_call | solution.py:208
  283.3 155.1 %all-to-all-done.1 = bf16[256,2,64,128]{3,2,1,0:T(8,128)(2,1)} async-done(((bf16[256,2,64,128]{3,2,1,0:T(8,128)(2,1)}), bf16[256,2,64,128]{3,2,1,0:T(8,128)(2,1)}, u32[]{:S(2)}, u32[]{:S(2)}) %all-to-all-start.1) | async-done | bytes 8388640 | tf_op jit(solution)/shard_map/all_to_all | solution.py:278
  438.4 9.1 %shard_map.79 = f32[64,3072]{1,0:T(8,128)} custom-call(s32[512]{0:T(512)} %reshape.153.ids_ref, bf16[512,64,128]{2,1,0:T(8,128)(2,1)} %bitcast.11.piece_ref), custom_call_target="tpu_custom_call" | custom-call | tf_op jit(solution)/shard_map/pallas_call | solution.py:244
  (13 shorter events, 0.0 us)
Async XLA Ops:
  0.6 18.9 %copy-start = (bf16[3072,512]{1,0:T(8,128)(2,1)S(1)}, bf16[3072,512]{1,0:T(8,128)(2,1)}, u32[]{:S(2)}) copy-start(bf16[3072,512]{1,0:T(8,128)(2,1)} %param.6) | copy-start | bytes 9437188
  25.1 7.4 %copy-start.5 = (s32[8,8]{1,0:T(8,128)S(1)}, s32[8,8]{1,0:T(8,128)}, u32[]{:S(2)}) copy-start(s32[8,8]{1,0:T(8,128)} %param.7) | copy-start | bytes 772
  25.1 7.5 %copy-start.6 = (s32[1024]{0:T(1024)S(1)}, s32[1024]{0:T(1024)}, u32[]{:S(2)}) copy-start(s32[1024]{0:T(1024)} %param.9) | copy-start | bytes 12292
  25.1 195.5 %copy-start.3 = (s32[8]{0:T(128)S(1)}, s32[8]{0:T(128)}, u32[]{:S(2)}) copy-start(s32[8]{0:T(128)} %count_ref.3) | copy-start | bytes 100
  25.1 195.5 %all-to-all-start = ((bf16[32,2,128,512]{3,2,1,0:T(8,128)(2,1)}), bf16[32,2,128,512]{3,2,1,0:T(8,128)(2,1)}, u32[]{:S(2)}, u32[]{:S(2)}) async-start(bf16[32,2,128,512]{3,2,1,0:T(8,128)(2,1)} %bitcast.18), calls=%async_computation | async-start | bytes 16777216 | tf_op jit(solution)/shard_map/all_to_all | solution.py:270
  220.5 1.2 copy-start.1
  236.4 14.1 %copy-start.4 = (s32[32,2]{1,0:T(8,128)S(1)}, s32[32,2]{1,0:T(8,128)}, u32[]{:S(2)}) copy-start(s32[32,2]{1,0:T(8,128)} %shard_map.76) | copy-start | bytes 772
  236.4 202.0 %all-to-all-start.1 = ((bf16[256,2,64,128]{3,2,1,0:T(8,128)(2,1)}), bf16[256,2,64,128]{3,2,1,0:T(8,128)(2,1)}, u32[]{:S(2)}, u32[]{:S(2)}) async-start(bf16[256,2,64,128]{3,2,1,0:T(8,128)(2,1)} %bitcast.19), calls=%async_computation.1 | async-start | bytes 16777216 | tf_op jit(solution)/shard_map/all_to_all | solution.py:278
  269.1 1.2 copy-start.2

commit v14 on v13

--- a/solution.py
+++ b/solution.py
@@ -106,42 +106,49 @@
 
 
 def _score_kernel(slot_ref, count_ref, emb_ref, pos_ref, *rest):
-    tiles = rest[:K]
-    loss_ref, pair_hbm, pair_buf, pair_sem = rest[K:]
-    b = pl.program_id(0)
+    per_step = emb_ref.shape[0]
+    tiles = rest[: per_step * K]
+    loss_ref, pair_hbm, pair_buf, pair_sem = rest[per_step * K:]
+    g = pl.program_id(0)
     last = pl.num_programs(0) - 1
-
-    def pending(par, k, slot):
+    width = per_step * K
+
+    def pending(par, i, slot):
         return pltpu.make_async_copy(
-            pair_buf.at[par, :, pl.ds(k, 1)],
+            pair_buf.at[par, :, pl.ds(i, 1)],
             pair_hbm.at[:, pl.ds(slot, 1)],
-            pair_sem.at[par, k],
+            pair_sem.at[par, i],
         )
 
-    _, _, unit_t, loss, scores = _block_scores(emb_ref, pos_ref, count_ref[b], tiles)
-    loss_ref[0] = loss
-    parity = b % 2
-
-    @pl.when(b >= 2)
+    parity = g % 2
+
+    @pl.when(g >= 2)
     def _():
+        for i in range(width):
+            pending(parity, i, 0).wait()
+
+    for j in range(per_step):
+        b = g * per_step + j
+        block_tiles = tiles[j * K:(j + 1) * K]
+        _, _, unit_t, loss, scores = _block_scores(
+            emb_ref.at[pl.ds(j, 1)], pos_ref.at[pl.ds(j, 1)], count_ref[b], block_tiles
+        )
+        loss_ref[j] = loss
         for k in range(K):
-            pending(parity, k, 0).wait()
-
-    for k in range(K):
-        pair_t = jnp.dot(unit_t, scores[k], preferred_element_type=jnp.float32).astype(jnp.bfloat16)
-        pair_buf[parity, :, k] = pair_t.reshape(pair_buf.shape[1], D // pair_buf.shape[1], TILE)
-    for k in range(K):
-        pending(parity, k, slot_ref[b * K + k]).start()
-
-    @pl.when(b == last)
+            pair_t = jnp.dot(unit_t, scores[k], preferred_element_type=jnp.float32).astype(jnp.bfloat16)
+            pair_buf[parity, :, j * K + k] = pair_t.reshape(pair_buf.shape[1], D // pair_buf.shape[1], TILE)
+        for k in range(K):
+            pending(parity, j * K + k, slot_ref[b * K + k]).start()
+
+    @pl.when(g == last)
     def _():
-        for k in range(K):
-            pending(parity, k, 0).wait()
-
-    @pl.when((b == last) & (b >= 1))
+        for i in range(width):
+            pending(parity, i, 0).wait()
+
+    @pl.when((g == last) & (g >= 1))
     def _():
-        for k in range(K):
-            pending(1 - parity, k, 0).wait()
+        for i in range(width):
+            pending(1 - parity, i, 0).wait()
 
 
 def _embed_kernel(slot_ref, count_ref, emb_ref, pos_ref, *rest):
@@ -161,24 +168,31 @@
     return pl.BlockSpec((1, TILE, D), lambda b, slot, *_: (slot[b * K + k], 0, 0))
 
 
-def score_step(slot_of, tile_count, emb_blocks, pos_cols, fetched, parts):
+def score_step(slot_of, tile_count, emb_blocks, pos_cols, fetched, parts, per_step=2):
     blocks = emb_blocks.shape[0]
     pairs = fetched.shape[0]
+
+    def step_tile_spec(i):
+        j, k = divmod(i, K)
+        return pl.BlockSpec(
+            (1, TILE, D), lambda g, slot, cnt: (slot[(g * per_step + j) * K + k], 0, 0)
+        )
+
     grid_spec = pltpu.PrefetchScalarGridSpec(
         num_scalar_prefetch=2,
-        grid=(blocks,),
+        grid=(blocks // per_step,),
         in_specs=[
-            pl.BlockSpec((1, BR, D), lambda b, slot, cnt: (b, 0, 0)),
-            pl.BlockSpec((1, 1, BR), lambda b, slot, cnt: (b, 0, 0)),
+            pl.BlockSpec((per_step, BR, D), lambda g, slot, cnt: (g, 0, 0)),
+            pl.BlockSpec((per_step, 1, BR), lambda g, slot, cnt: (g, 0, 0)),
         ]
-        + [_tile_spec(k) for k in range(K)],
+        + [step_tile_spec(i) for i in range(per_step * K)],
         out_specs=[
-            pl.BlockSpec((1, 1, BR), lambda b, slot, cnt: (b, 0, 0)),
+            pl.BlockSpec((per_step, 1, BR), lambda g, slot, cnt: (g, 0, 0)),
             pl.BlockSpec(memory_space=pl.ANY),
         ],
         scratch_shapes=[
-            pltpu.VMEM((2, parts, K, D // parts, TILE), jnp.bfloat16),
-            pltpu.SemaphoreType.DMA((2, K)),
+            pltpu.VMEM((2, parts, per_step * K, D // parts, TILE), jnp.bfloat16),
+            pltpu.SemaphoreType.DMA((2, per_step * K)),
         ],
     )
     return pl.pallas_call(
@@ -189,7 +203,7 @@
             jax.ShapeDtypeStruct((parts, pairs, D // parts, TILE), jnp.bfloat16),
         ],
         compiler_params=pltpu.CompilerParams(vmem_limit_bytes=48 * 1024 * 1024),
-    )(slot_of, tile_count, emb_blocks, pos_cols, *([fetched] * K))
+    )(slot_of, tile_count, emb_blocks, pos_cols, *([fetched] * (per_step * K)))
 
 
 def embed_step(slot_of, tile_count, emb_blocks, pos_cols, fetched):

time: 448 us -> 447 us (level)
  no operation moved by 1% of the time
where the time goes in v14:
time: 447 us; the launch traced here: 446 us
  waiting for transfers between devices  343 us (77%)
  Pallas kernels  49.6 us (11%)
  starting transfers between devices  21.6 us (5%)
  blocking collectives  17.6 us (4%)
  local copies, waits for them, and re-layouts  10.8 us (2%)
    all_to_all x1, waiting for transfers between devices, per_device(): lax.all_to_all(outgoing, 'cls', split_axis=0, concat_axis=0, tiled=True)  188 us
    all_to_all x1, waiting for transfers between devices, per_device(): lax.all_to_all(pair_grads, ('dp', 'cls'), split_axis=0, concat_axis=0, ti...  155 us
    all_gather x1, blocking collectives, per_device(): got_ids = lax.all_gather(wanted, 'dp').reshape(parts * pair_count)  17.6 us
    pallas_call x1, Pallas kernels, cls_all_to_all(): pl.pallas_call(functools.partial(_a2a_kernel, n), out_shape=jax.ShapeDtyp...  14.3 us
    all_to_all x1, starting transfers between devices, per_device(): lax.all_to_all(pair_grads, ('dp', 'cls'), split_axis=0, concat_axis=0, ti...  14.3 us
    pallas_call x1, Pallas kernels, score_step(): pl.pallas_call(_score_kernel, grid_spec=grid_spec, out_shape=[jax.ShapeDt...  13.2 us
    pallas_call x1, Pallas kernels, embed_step(): pl.pallas_call(_embed_kernel, grid_spec=grid_spec, out_shape=jax.ShapeDty...  13 us
    pallas_call x1, Pallas kernels, column_sum(): pl.pallas_call(_column_sum_kernel, grid_spec=grid_spec, out_shape=jax.Sha...  9.1 us
  transfers between devices with their start and end apart: 2, of which 2 were waited for; matrix products, arithmetic and copies ran while one was open for 0% of the time, Pallas kernels for 3%

profile of v14, /device:TPU:1, one launch (start us, length us, event | category | flops | bytes accessed | tf_op | source)
XLA Modules:
  0.0 446.1 jit_solution(3057938032303656796)
XLA Ops:
  0.6 0.0 copy-start
  0.6 0.8 sign_compare_fusion
  1.5 0.8 broadcast_remainder_fusion
  2.3 0.1 ne.51
  2.4 0.1 rem.30
  2.5 0.1 div.21
  2.6 0.2 select_reduce_fusion.1
  2.7 0.1 select_reduce_fusion
  2.9 0.8 gather_fusion
  3.7 0.7 reshape.149.src_ref
  4.4 14.3 %shard_map.76 = s32[32,2]{1,0:T(8,128)} custom-call(s32[32,2]{1,0:T(8,128)} %reshape.149.src_ref), custom_call_target="tpu_custom_call" | custom-call | tf_op jit(solution)/shard_map/pallas_call | solution.py:60
  18.7 0.7 compare_select_fusion
  19.4 0.1 reshape.166
  19.5 5.5 %gather_fusion.1 = bf16[64,128,512]{2,1,0:T(8,128)(2,1)} fusion(bf16[24,128,512]{2,1,0:T(8,128)(2,1)S(1)} %bitcast.15, s32[1024]{0:T(1024)S(1)} %pad_clamp_fusion), kind=kCustom, calls=%fused_computation.1 | custom fusion | bytes 16777472 | tf_op jit(solution)/shard_map/gather | solution.py:283
  25.1 7.3 %all-to-all-start = ((bf16[32,2,128,512]{3,2,1,0:T(8,128)(2,1)}), bf16[32,2,128,512]{3,2,1,0:T(8,128)(2,1)}, u32[]{:S(2)}, u32[]{:S(2)}) async-start(bf16[32,2,128,512]{3,2,1,0:T(8,128)(2,1)} %bitcast.18), calls=%async_computation | async-start | bytes 16777216 | tf_op jit(solution)/shard_map/all_to_all | solution.py:284
  32.4 0.0 copy-done.5
  32.4 0.1 multiply_reduce_fusion
  32.6 0.0 copy-done.6
  32.6 0.1 broadcast_subtract_fusion.pos_ref
  32.6 187.8 %all-to-all-done = bf16[32,2,128,512]{3,2,1,0:T(8,128)(2,1)} async-done(((bf16[32,2,128,512]{3,2,1,0:T(8,128)(2,1)}), bf16[32,2,128,512]{3,2,1,0:T(8,128)(2,1)}, u32[]{:S(2)}, u32[]{:S(2)}) %all-to-all-start) | async-done | bytes 8388640 | tf_op jit(solution)/shard_map/all_to_all | solution.py:284
  220.5 0.0 copy-done.3
  220.5 1.2 copy-done.1
  221.7 13.2 %shard_map.77 = (f32[8,1,128]{2,1,0:T(1,128)}, bf16[8,64,64,128]{3,2,1,0:T(8,128)(2,1)}) custom-call(s32[64]{0:T(128)S(1)} %multiply_add_fusion.slot_ref, s32[8]{0:T(128)S(1)} %copy-done.3, bf16[8,128,512]{2,1,0:T(8,128)(2,1)S(1)} %bitcast.16, s32[8,1,128]{2,1,0:T(1,128)S(1)} %broadcast_subtract_fusion.pos_ref, ...), custom_call_target="tpu_custom_call" | custom-call | tf_op jit(solution)/shard_map/pallas_call | solution.py:198
  234.9 14.3 %all-to-all-start.1 = ((bf16[256,2,64,128]{3,2,1,0:T(8,128)(2,1)}), bf16[256,2,64,128]{3,2,1,0:T(8,128)(2,1)}, u32[]{:S(2)}, u32[]{:S(2)}) async-start(bf16[256,2,64,128]{3,2,1,0:T(8,128)(2,1)} %bitcast.19), calls=%async_computation.1 | async-start | bytes 16777216 | tf_op jit(solution)/shard_map/all_to_all | solution.py:292
  249.2 0.1 copy.13
  249.2 17.6 %all-gather.1 = s32[8,32,2]{1,2,0:T(2,128)S(1)} all-gather(s32[1,32,2]{1,2,0:T(2,128)S(1)} %bitcast.22), channel_id=2, replica_groups=mesh['dp'=8,'cls'=32] {'dp'}, dimensions={0}, use_global_device_ids=true | all-gather | bytes 2304 | tf_op jit(solution)/shard_map/all_gather | solution.py:293
  266.8 0.1 copy.14
  267.0 0.7 reshape.153.ids_ref
  267.7 1.2 copy-done.2
  268.9 13.0 %shard_map.78 = bf16[8,128,512]{2,1,0:T(8,128)(2,1)} custom-call(s32[64]{0:T(128)S(1)} %multiply_add_fusion.slot_ref, s32[8]{0:T(128)S(1)} %copy-done.3, bf16[8,128,512]{2,1,0:T(8,128)(2,1)S(1)} %bitcast.17, s32[8,1,128]{2,1,0:T(1,128)S(1)} %broadcast_subtract_fusion.pos_ref, ...), custom_call_target="tpu_custom_call" | custom-call | flops 2147483648 | bytes 10485760 | tf_op jit(solution)/shard_map/pallas_call | solution.py:222
  282.0 155.0 %all-to-all-done.1 = bf16[256,2,64,128]{3,2,1,0:T(8,128)(2,1)} async-done(((bf16[256,2,64,128]{3,2,1,0:T(8,128)(2,1)}), bf16[256,2,64,128]{3,2,1,0:T(8,128)(2,1)}, u32[]{:S(2)}, u32[]{:S(2)}) %all-to-all-start.1) | async-done | bytes 8388640 | tf_op jit(solution)/shard_map/all_to_all | solution.py:292
  437.0 9.1 %shard_map.79 = f32[64,3072]{1,0:T(8,128)} custom-call(s32[512]{0:T(512)} %reshape.153.ids_ref, bf16[512,64,128]{2,1,0:T(8,128)(2,1)} %bitcast.11.piece_ref), custom_call_target="tpu_custom_call" | custom-call | tf_op jit(solution)/shard_map/pallas_call | solution.py:258
  (13 shorter events, 0.0 us)
Async XLA Ops:
  0.6 18.9 %copy-start = (bf16[3072,512]{1,0:T(8,128)(2,1)S(1)}, bf16[3072,512]{1,0:T(8,128)(2,1)}, u32[]{:S(2)}) copy-start(bf16[3072,512]{1,0:T(8,128)(2,1)} %param.6) | copy-start | bytes 9437188
  25.1 7.4 %copy-start.5 = (s32[8,8]{1,0:T(8,128)S(1)}, s32[8,8]{1,0:T(8,128)}, u32[]{:S(2)}) copy-start(s32[8,8]{1,0:T(8,128)} %param.7) | copy-start | bytes 772
  25.1 7.5 %copy-start.6 = (s32[1024]{0:T(1024)S(1)}, s32[1024]{0:T(1024)}, u32[]{:S(2)}) copy-start(s32[1024]{0:T(1024)} %param.9) | copy-start | bytes 12292
  25.1 195.4 %copy-start.3 = (s32[8]{0:T(128)S(1)}, s32[8]{0:T(128)}, u32[]{:S(2)}) copy-start(s32[8]{0:T(128)} %count_ref.3) | copy-start | bytes 100
  25.1 195.4 %all-to-all-start = ((bf16[32,2,128,512]{3,2,1,0:T(8,128)(2,1)}), bf16[32,2,128,512]{3,2,1,0:T(8,128)(2,1)}, u32[]{:S(2)}, u32[]{:S(2)}) async-start(bf16[32,2,128,512]{3,2,1,0:T(8,128)(2,1)} %bitcast.18), calls=%async_computation | async-start | bytes 16777216 | tf_op jit(solution)/shard_map/all_to_all | solution.py:284
  220.5 1.2 copy-start.1
  234.9 14.3 %copy-start.4 = (s32[32,2]{1,0:T(8,128)S(1)}, s32[32,2]{1,0:T(8,128)}, u32[]{:S(2)}) copy-start(s32[32,2]{1,0:T(8,128)} %shard_map.76) | copy-start | bytes 772
  234.9 202.1 %all-to-all-start.1 = ((bf16[256,2,64,128]{3,2,1,0:T(8,128)(2,1)}), bf16[256,2,64,128]{3,2,1,0:T(8,128)(2,1)}, u32[]{:S(2)}, u32[]{:S(2)}) async-start(bf16[256,2,64,128]{3,2,1,0:T(8,128)(2,1)} %bitcast.19), calls=%async_computation.1 | async-start | bytes 16777216 | tf_op jit(solution)/shard_map/all_to_all | solution.py:292
  267.7 1.2 copy-start.2

commit v15 on v14

--- a/solution.py
+++ b/solution.py
@@ -168,7 +168,7 @@
     return pl.BlockSpec((1, TILE, D), lambda b, slot, *_: (slot[b * K + k], 0, 0))
 
 
-def score_step(slot_of, tile_count, emb_blocks, pos_cols, fetched, parts, per_step=2):
+def score_step(slot_of, tile_count, emb_blocks, pos_cols, fetched, parts, per_step=4):
     blocks = emb_blocks.shape[0]
     pairs = fetched.shape[0]
 

time: 447 us -> 447 us (level)
  no operation moved by 1% of the time
where the time goes in v15:
time: 447 us; the launch traced here: 446 us
  waiting for transfers between devices  343 us (77%)
  Pallas kernels  49.7 us (11%)
  starting transfers between devices  21.3 us (5%)
  blocking collectives  17.6 us (4%)
  local copies, waits for them, and re-layouts  10.8 us (2%)
    all_to_all x1, waiting for transfers between devices, per_device(): lax.all_to_all(outgoing, 'cls', split_axis=0, concat_axis=0, tiled=True)  188 us
    all_to_all x1, waiting for transfers between devices, per_device(): lax.all_to_all(pair_grads, ('dp', 'cls'), split_axis=0, concat_axis=0, ti...  155 us
    all_gather x1, blocking collectives, per_device(): got_ids = lax.all_gather(wanted, 'dp').reshape(parts * pair_count)  17.6 us
    pallas_call x1, Pallas kernels, cls_all_to_all(): pl.pallas_call(functools.partial(_a2a_kernel, n), out_shape=jax.ShapeDtyp...  14.3 us
    all_to_all x1, starting transfers between devices, per_device(): lax.all_to_all(pair_grads, ('dp', 'cls'), split_axis=0, concat_axis=0, ti...  13.9 us
    pallas_call x1, Pallas kernels, score_step(): pl.pallas_call(_score_kernel, grid_spec=grid_spec, out_shape=[jax.ShapeDt...  13.2 us
    pallas_call x1, Pallas kernels, embed_step(): pl.pallas_call(_embed_kernel, grid_spec=grid_spec, out_shape=jax.ShapeDty...  13 us
    pallas_call x1, Pallas kernels, column_sum(): pl.pallas_call(_column_sum_kernel, grid_spec=grid_spec, out_shape=jax.Sha...  9.09 us
  transfers between devices with their start and end apart: 2, of which 2 were waited for; matrix products, arithmetic and copies ran while one was open for 0% of the time, Pallas kernels for 3%

profile of v15, /device:TPU:1, one launch (start us, length us, event | category | flops | bytes accessed | tf_op | source)
XLA Modules:
  0.0 446.0 jit_solution(2465031624512025812)
XLA Ops:
  0.6 0.0 copy-start
  0.6 0.8 sign_compare_fusion
  1.5 0.8 broadcast_remainder_fusion
  2.3 0.1 ne.51
  2.4 0.1 rem.30
  2.5 0.1 div.21
  2.6 0.2 select_reduce_fusion.1
  2.7 0.1 select_reduce_fusion
  2.9 0.8 gather_fusion
  3.7 0.7 reshape.149.src_ref
  4.4 14.3 %shard_map.76 = s32[32,2]{1,0:T(8,128)} custom-call(s32[32,2]{1,0:T(8,128)} %reshape.149.src_ref), custom_call_target="tpu_custom_call" | custom-call | tf_op jit(solution)/shard_map/pallas_call | solution.py:60
  18.7 0.7 compare_select_fusion
  19.4 0.1 reshape.166
  19.5 0.0 copy-done
  19.5 5.5 %gather_fusion.1 = bf16[64,128,512]{2,1,0:T(8,128)(2,1)} fusion(bf16[24,128,512]{2,1,0:T(8,128)(2,1)S(1)} %bitcast.15, s32[1024]{0:T(1024)S(1)} %pad_clamp_fusion), kind=kCustom, calls=%fused_computation.1 | custom fusion | bytes 16777472 | tf_op jit(solution)/shard_map/gather | solution.py:283
  25.1 7.4 %all-to-all-start = ((bf16[32,2,128,512]{3,2,1,0:T(8,128)(2,1)}), bf16[32,2,128,512]{3,2,1,0:T(8,128)(2,1)}, u32[]{:S(2)}, u32[]{:S(2)}) async-start(bf16[32,2,128,512]{3,2,1,0:T(8,128)(2,1)} %bitcast.18), calls=%async_computation | async-start | bytes 16777216 | tf_op jit(solution)/shard_map/all_to_all | solution.py:284
  32.5 0.1 multiply_reduce_fusion
  32.6 0.1 broadcast_subtract_fusion.pos_ref
  32.6 188.0 %all-to-all-done = bf16[32,2,128,512]{3,2,1,0:T(8,128)(2,1)} async-done(((bf16[32,2,128,512]{3,2,1,0:T(8,128)(2,1)}), bf16[32,2,128,512]{3,2,1,0:T(8,128)(2,1)}, u32[]{:S(2)}, u32[]{:S(2)}) %all-to-all-start) | async-done | bytes 8388640 | tf_op jit(solution)/shard_map/all_to_all | solution.py:284
  220.6 0.0 copy-done.3
  220.6 1.2 copy-done.1
  221.9 13.2 %shard_map.77 = (f32[8,1,128]{2,1,0:T(1,128)}, bf16[8,64,64,128]{3,2,1,0:T(8,128)(2,1)}) custom-call(s32[64]{0:T(128)S(1)} %multiply_add_fusion.slot_ref, s32[8]{0:T(128)S(1)} %copy-done.3, bf16[8,128,512]{2,1,0:T(8,128)(2,1)S(1)} %bitcast.16, s32[8,1,128]{2,1,0:T(1,128)S(1)} %broadcast_subtract_fusion.pos_ref, ...), custom_call_target="tpu_custom_call" | custom-call | tf_op jit(solution)/shard_map/pallas_call | solution.py:198
  235.1 13.9 %all-to-all-start.1 = ((bf16[256,2,64,128]{3,2,1,0:T(8,128)(2,1)}), bf16[256,2,64,128]{3,2,1,0:T(8,128)(2,1)}, u32[]{:S(2)}, u32[]{:S(2)}) async-start(bf16[256,2,64,128]{3,2,1,0:T(8,128)(2,1)} %bitcast.19), calls=%async_computation.1 | async-start | bytes 16777216 | tf_op jit(solution)/shard_map/all_to_all | solution.py:292
  249.1 0.0 copy-done.4
  249.1 0.1 copy.13
  249.1 17.6 %all-gather.1 = s32[8,32,2]{1,2,0:T(2,128)S(1)} all-gather(s32[1,32,2]{1,2,0:T(2,128)S(1)} %bitcast.22), channel_id=2, replica_groups=mesh['dp'=8,'cls'=32] {'dp'}, dimensions={0}, use_global_device_ids=true | all-gather | bytes 2304 | tf_op jit(solution)/shard_map/all_gather | solution.py:293
  266.7 0.1 copy.14
  266.9 0.7 reshape.153.ids_ref
  267.6 1.2 copy-done.2
  268.8 13.0 %shard_map.78 = bf16[8,128,512]{2,1,0:T(8,128)(2,1)} custom-call(s32[64]{0:T(128)S(1)} %multiply_add_fusion.slot_ref, s32[8]{0:T(128)S(1)} %copy-done.3, bf16[8,128,512]{2,1,0:T(8,128)(2,1)S(1)} %bitcast.17, s32[8,1,128]{2,1,0:T(1,128)S(1)} %broadcast_subtract_fusion.pos_ref, ...), custom_call_target="tpu_custom_call" | custom-call | flops 2147483648 | bytes 10485760 | tf_op jit(solution)/shard_map/pallas_call | solution.py:222
  281.8 155.0 %all-to-all-done.1 = bf16[256,2,64,128]{3,2,1,0:T(8,128)(2,1)} async-done(((bf16[256,2,64,128]{3,2,1,0:T(8,128)(2,1)}), bf16[256,2,64,128]{3,2,1,0:T(8,128)(2,1)}, u32[]{:S(2)}, u32[]{:S(2)}) %all-to-all-start.1) | async-done | bytes 8388640 | tf_op jit(solution)/shard_map/all_to_all | solution.py:292
  436.9 9.1 %shard_map.79 = f32[64,3072]{1,0:T(8,128)} custom-call(s32[512]{0:T(512)} %reshape.153.ids_ref, bf16[512,64,128]{2,1,0:T(8,128)(2,1)} %bitcast.11.piece_ref), custom_call_target="tpu_custom_call" | custom-call | tf_op jit(solution)/shard_map/pallas_call | solution.py:258
  (13 shorter events, 0.0 us)
Async XLA Ops:
  0.6 18.9 %copy-start = (bf16[3072,512]{1,0:T(8,128)(2,1)S(1)}, bf16[3072,512]{1,0:T(8,128)(2,1)}, u32[]{:S(2)}) copy-start(bf16[3072,512]{1,0:T(8,128)(2,1)} %param.6) | copy-start | bytes 9437188
  25.1 7.4 %copy-start.5 = (s32[8,8]{1,0:T(8,128)S(1)}, s32[8,8]{1,0:T(8,128)}, u32[]{:S(2)}) copy-start(s32[8,8]{1,0:T(8,128)} %param.7) | copy-start | bytes 772
  25.1 7.5 %copy-start.6 = (s32[1024]{0:T(1024)S(1)}, s32[1024]{0:T(1024)}, u32[]{:S(2)}) copy-start(s32[1024]{0:T(1024)} %param.9) | copy-start | bytes 12292
  25.1 195.6 %copy-start.3 = (s32[8]{0:T(128)S(1)}, s32[8]{0:T(128)}, u32[]{:S(2)}) copy-start(s32[8]{0:T(128)} %count_ref.3) | copy-start | bytes 100
  25.1 195.6 %all-to-all-start = ((bf16[32,2,128,512]{3,2,1,0:T(8,128)(2,1)}), bf16[32,2,128,512]{3,2,1,0:T(8,128)(2,1)}, u32[]{:S(2)}, u32[]{:S(2)}) async-start(bf16[32,2,128,512]{3,2,1,0:T(8,128)(2,1)} %bitcast.18), calls=%async_computation | async-start | bytes 16777216 | tf_op jit(solution)/shard_map/all_to_all | solution.py:284
  220.6 1.2 copy-start.1
  235.1 13.9 %copy-start.4 = (s32[32,2]{1,0:T(8,128)S(1)}, s32[32,2]{1,0:T(8,128)}, u32[]{:S(2)}) copy-start(s32[32,2]{1,0:T(8,128)} %shard_map.76) | copy-start | bytes 772
  235.1 201.8 %all-to-all-start.1 = ((bf16[256,2,64,128]{3,2,1,0:T(8,128)(2,1)}), bf16[256,2,64,128]{3,2,1,0:T(8,128)(2,1)}, u32[]{:S(2)}, u32[]{:S(2)}) async-start(bf16[256,2,64,128]{3,2,1,0:T(8,128)(2,1)} %bitcast.19), calls=%async_computation.1 | async-start | bytes 16777216 | tf_op jit(solution)/shard_map/all_to_all | solution.py:292
  267.6 1.2 copy-start.2

commit v16 on v15

--- a/solution.py
+++ b/solution.py
@@ -247,7 +247,7 @@
     lax.fori_loop(0, chunk, body, 0, unroll=8)
 
 
-def column_sum(got_ids, pieces, tile_dev, chunk=64):
+def column_sum(got_ids, pieces, tile_dev, chunk=128):
     count, width, _ = pieces.shape
     grid_spec = pltpu.PrefetchScalarGridSpec(
         num_scalar_prefetch=1,

time: 447 us -> 445 us (level)
  no operation moved by 1% of the time
where the time goes in v16:
time: 445 us
  waiting for transfers between devices  343 us (77%)
  Pallas kernels  48.3 us (11%)
  starting transfers between devices  21.6 us (5%)
  blocking collectives  17.6 us (4%)
  local copies, waits for them, and re-layouts  10.8 us (2%)
    all_to_all x1, waiting for transfers between devices, per_device(): lax.all_to_all(outgoing, 'cls', split_axis=0, concat_axis=0, tiled=True)  188 us
    all_to_all x1, waiting for transfers between devices, per_device(): lax.all_to_all(pair_grads, ('dp', 'cls'), split_axis=0, concat_axis=0, ti...  155 us
    all_gather x1, blocking collectives, per_device(): got_ids = lax.all_gather(wanted, 'dp').reshape(parts * pair_count)  17.6 us
    pallas_call x1, Pallas kernels, cls_all_to_all(): pl.pallas_call(functools.partial(_a2a_kernel, n), out_shape=jax.ShapeDtyp...  14.3 us
    all_to_all x1, starting transfers between devices, per_device(): lax.all_to_all(pair_grads, ('dp', 'cls'), split_axis=0, concat_axis=0, ti...  14.2 us
    pallas_call x1, Pallas kernels, score_step(): pl.pallas_call(_score_kernel, grid_spec=grid_spec, out_shape=[jax.ShapeDt...  13.2 us
    pallas_call x1, Pallas kernels, embed_step(): pl.pallas_call(_embed_kernel, grid_spec=grid_spec, out_shape=jax.ShapeDty...  13 us
  transfers between devices with their start and end apart: 2, of which 2 were waited for; matrix products, arithmetic and copies ran while one was open for 0% of the time, Pallas kernels for 3%

profile of v16, /device:TPU:1, one launch (start us, length us, event | category | flops | bytes accessed | tf_op | source)
XLA Modules:
  0.0 444.6 jit_solution(2200700058760340113)
XLA Ops:
  0.6 0.0 copy-start
  0.6 0.8 sign_compare_fusion
  1.5 0.8 broadcast_remainder_fusion
  2.3 0.1 ne.51
  2.4 0.1 rem.30
  2.5 0.1 div.21
  2.6 0.2 select_reduce_fusion.1
  2.7 0.1 select_reduce_fusion
  2.9 0.8 gather_fusion
  3.7 0.7 reshape.149.src_ref
  4.4 14.3 %shard_map.76 = s32[32,2]{1,0:T(8,128)} custom-call(s32[32,2]{1,0:T(8,128)} %reshape.149.src_ref), custom_call_target="tpu_custom_call" | custom-call | tf_op jit(solution)/shard_map/pallas_call | solution.py:60
  18.7 0.7 compare_select_fusion
  19.4 0.1 reshape.166
  19.5 0.0 copy-done
  19.5 5.5 %gather_fusion.1 = bf16[64,128,512]{2,1,0:T(8,128)(2,1)} fusion(bf16[24,128,512]{2,1,0:T(8,128)(2,1)S(1)} %bitcast.15, s32[1024]{0:T(1024)S(1)} %pad_clamp_fusion), kind=kCustom, calls=%fused_computation.1 | custom fusion | bytes 16777472 | tf_op jit(solution)/shard_map/gather | solution.py:283
  25.1 7.3 %all-to-all-start = ((bf16[32,2,128,512]{3,2,1,0:T(8,128)(2,1)}), bf16[32,2,128,512]{3,2,1,0:T(8,128)(2,1)}, u32[]{:S(2)}, u32[]{:S(2)}) async-start(bf16[32,2,128,512]{3,2,1,0:T(8,128)(2,1)} %bitcast.18), calls=%async_computation | async-start | bytes 16777216 | tf_op jit(solution)/shard_map/all_to_all | solution.py:284
  32.4 0.1 multiply_reduce_fusion
  32.5 0.1 broadcast_subtract_fusion.pos_ref
  32.6 187.8 %all-to-all-done = bf16[32,2,128,512]{3,2,1,0:T(8,128)(2,1)} async-done(((bf16[32,2,128,512]{3,2,1,0:T(8,128)(2,1)}), bf16[32,2,128,512]{3,2,1,0:T(8,128)(2,1)}, u32[]{:S(2)}, u32[]{:S(2)}) %all-to-all-start) | async-done | bytes 8388640 | tf_op jit(solution)/shard_map/all_to_all | solution.py:284
  220.4 0.0 copy-done.3
  220.4 1.2 copy-done.1
  221.6 13.2 %shard_map.77 = (f32[8,1,128]{2,1,0:T(1,128)}, bf16[8,64,64,128]{3,2,1,0:T(8,128)(2,1)}) custom-call(s32[64]{0:T(128)S(1)} %multiply_add_fusion.slot_ref, s32[8]{0:T(128)S(1)} %copy-done.3, bf16[8,128,512]{2,1,0:T(8,128)(2,1)S(1)} %bitcast.16, s32[8,1,128]{2,1,0:T(1,128)S(1)} %broadcast_subtract_fusion.pos_ref, ...), custom_call_target="tpu_custom_call" | custom-call | tf_op jit(solution)/shard_map/pallas_call | solution.py:198
  234.8 14.2 %all-to-all-start.1 = ((bf16[256,2,64,128]{3,2,1,0:T(8,128)(2,1)}), bf16[256,2,64,128]{3,2,1,0:T(8,128)(2,1)}, u32[]{:S(2)}, u32[]{:S(2)}) async-start(bf16[256,2,64,128]{3,2,1,0:T(8,128)(2,1)} %bitcast.19), calls=%async_computation.1 | async-start | bytes 16777216 | tf_op jit(solution)/shard_map/all_to_all | solution.py:292
  249.0 0.0 copy-done.4
  249.0 0.1 copy.13
  249.1 17.6 %all-gather.1 = s32[8,32,2]{1,2,0:T(2,128)S(1)} all-gather(s32[1,32,2]{1,2,0:T(2,128)S(1)} %bitcast.22), channel_id=2, replica_groups=mesh['dp'=8,'cls'=32] {'dp'}, dimensions={0}, use_global_device_ids=true | all-gather | bytes 2304 | tf_op jit(solution)/shard_map/all_gather | solution.py:293
  266.7 0.1 copy.14
  266.8 0.7 reshape.153.ids_ref
  267.6 1.2 copy-done.2
  268.8 13.0 %shard_map.78 = bf16[8,128,512]{2,1,0:T(8,128)(2,1)} custom-call(s32[64]{0:T(128)S(1)} %multiply_add_fusion.slot_ref, s32[8]{0:T(128)S(1)} %copy-done.3, bf16[8,128,512]{2,1,0:T(8,128)(2,1)S(1)} %bitcast.17, s32[8,1,128]{2,1,0:T(1,128)S(1)} %broadcast_subtract_fusion.pos_ref, ...), custom_call_target="tpu_custom_call" | custom-call | flops 2147483648 | bytes 10485760 | tf_op jit(solution)/shard_map/pallas_call | solution.py:222
  281.8 155.0 %all-to-all-done.1 = bf16[256,2,64,128]{3,2,1,0:T(8,128)(2,1)} async-done(((bf16[256,2,64,128]{3,2,1,0:T(8,128)(2,1)}), bf16[256,2,64,128]{3,2,1,0:T(8,128)(2,1)}, u32[]{:S(2)}, u32[]{:S(2)}) %all-to-all-start.1) | async-done | bytes 8388640 | tf_op jit(solution)/shard_map/all_to_all | solution.py:292
  436.9 7.8 %shard_map.79 = f32[64,3072]{1,0:T(8,128)} custom-call(s32[512]{0:T(512)} %reshape.153.ids_ref, bf16[512,64,128]{2,1,0:T(8,128)(2,1)} %bitcast.11.piece_ref), custom_call_target="tpu_custom_call" | custom-call | tf_op jit(solution)/shard_map/pallas_call | solution.py:258
  (13 shorter events, 0.0 us)
Async XLA Ops:
  0.6 18.9 %copy-start = (bf16[3072,512]{1,0:T(8,128)(2,1)S(1)}, bf16[3072,512]{1,0:T(8,128)(2,1)}, u32[]{:S(2)}) copy-start(bf16[3072,512]{1,0:T(8,128)(2,1)} %param.6) | copy-start | bytes 9437188
  25.1 7.3 %copy-start.5 = (s32[8,8]{1,0:T(8,128)S(1)}, s32[8,8]{1,0:T(8,128)}, u32[]{:S(2)}) copy-start(s32[8,8]{1,0:T(8,128)} %param.7) | copy-start | bytes 772
  25.1 7.5 %copy-start.6 = (s32[1024]{0:T(1024)S(1)}, s32[1024]{0:T(1024)}, u32[]{:S(2)}) copy-start(s32[1024]{0:T(1024)} %param.9) | copy-start | bytes 12292
  25.1 195.3 %copy-start.3 = (s32[8]{0:T(128)S(1)}, s32[8]{0:T(128)}, u32[]{:S(2)}) copy-start(s32[8]{0:T(128)} %count_ref.3) | copy-start | bytes 100
  25.1 195.3 %all-to-all-start = ((bf16[32,2,128,512]{3,2,1,0:T(8,128)(2,1)}), bf16[32,2,128,512]{3,2,1,0:T(8,128)(2,1)}, u32[]{:S(2)}, u32[]{:S(2)}) async-start(bf16[32,2,128,512]{3,2,1,0:T(8,128)(2,1)} %bitcast.18), calls=%async_computation | async-start | bytes 16777216 | tf_op jit(solution)/shard_map/all_to_all | solution.py:284
  220.4 1.2 copy-start.1
  234.8 14.2 %copy-start.4 = (s32[32,2]{1,0:T(8,128)S(1)}, s32[32,2]{1,0:T(8,128)}, u32[]{:S(2)}) copy-start(s32[32,2]{1,0:T(8,128)} %shard_map.76) | copy-start | bytes 772
  234.8 202.1 %all-to-all-start.1 = ((bf16[256,2,64,128]{3,2,1,0:T(8,128)(2,1)}), bf16[256,2,64,128]{3,2,1,0:T(8,128)(2,1)}, u32[]{:S(2)}, u32[]{:S(2)}) async-start(bf16[256,2,64,128]{3,2,1,0:T(8,128)(2,1)} %bitcast.19), calls=%async_computation.1 | async-start | bytes 16777216 | tf_op jit(solution)/shard_map/all_to_all | solution.py:292
  267.6 1.2 copy-start.2

commit v17 on v16

--- a/solution.py
+++ b/solution.py
@@ -244,7 +244,7 @@
         out_ref[:, window] += piece_ref[j].astype(jnp.float32)
         return carry
 
-    lax.fori_loop(0, chunk, body, 0, unroll=8)
+    lax.fori_loop(0, chunk, body, 0, unroll=16)
 
 
 def column_sum(got_ids, pieces, tile_dev, chunk=128):

time: 445 us -> 445 us (level)
  no operation moved by 1% of the time
where the time goes in v17:
time: 445 us
  waiting for transfers between devices  343 us (77%)
  Pallas kernels  48.6 us (11%)
  starting transfers between devices  21.4 us (5%)
  blocking collectives  17.6 us (4%)
  local copies, waits for them, and re-layouts  10.8 us (2%)
    all_to_all x1, waiting for transfers between devices, per_device(): lax.all_to_all(outgoing, 'cls', split_axis=0, concat_axis=0, tiled=True)  188 us
    all_to_all x1, waiting for transfers between devices, per_device(): lax.all_to_all(pair_grads, ('dp', 'cls'), split_axis=0, concat_axis=0, ti...  155 us
    all_gather x1, blocking collectives, per_device(): got_ids = lax.all_gather(wanted, 'dp').reshape(parts * pair_count)  17.6 us
    pallas_call x1, Pallas kernels, cls_all_to_all(): pl.pallas_call(functools.partial(_a2a_kernel, n), out_shape=jax.ShapeDtyp...  14.3 us
    all_to_all x1, starting transfers between devices, per_device(): lax.all_to_all(pair_grads, ('dp', 'cls'), split_axis=0, concat_axis=0, ti...  14.1 us
    pallas_call x1, Pallas kernels, score_step(): pl.pallas_call(_score_kernel, grid_spec=grid_spec, out_shape=[jax.ShapeDt...  13.2 us
    pallas_call x1, Pallas kernels, embed_step(): pl.pallas_call(_embed_kernel, grid_spec=grid_spec, out_shape=jax.ShapeDty...  13.1 us
  transfers between devices with their start and end apart: 2, of which 2 were waited for; matrix products, arithmetic and copies ran while one was open for 0% of the time, Pallas kernels for 3%

profile of v17, /device:TPU:1, one launch (start us, length us, event | category | flops | bytes accessed | tf_op | source)
XLA Modules:
  0.0 444.8 jit_solution(6292999189932712487)
XLA Ops:
  0.6 0.0 copy-start
  0.6 0.8 sign_compare_fusion
  1.5 0.8 broadcast_remainder_fusion
  2.3 0.1 ne.51
  2.4 0.1 rem.30
  2.5 0.1 div.21
  2.6 0.2 select_reduce_fusion.1
  2.7 0.1 select_reduce_fusion
  2.9 0.8 gather_fusion
  3.7 0.7 reshape.149.src_ref
  4.4 14.3 %shard_map.76 = s32[32,2]{1,0:T(8,128)} custom-call(s32[32,2]{1,0:T(8,128)} %reshape.149.src_ref), custom_call_target="tpu_custom_call" | custom-call | tf_op jit(solution)/shard_map/pallas_call | solution.py:60
  18.7 0.7 compare_select_fusion
  19.4 0.1 reshape.166
  19.5 0.0 copy-done
  19.5 5.5 %gather_fusion.1 = bf16[64,128,512]{2,1,0:T(8,128)(2,1)} fusion(bf16[24,128,512]{2,1,0:T(8,128)(2,1)S(1)} %bitcast.15, s32[1024]{0:T(1024)S(1)} %pad_clamp_fusion), kind=kCustom, calls=%fused_computation.1 | custom fusion | bytes 16777472 | tf_op jit(solution)/shard_map/gather | solution.py:283
  25.1 7.3 %all-to-all-start = ((bf16[32,2,128,512]{3,2,1,0:T(8,128)(2,1)}), bf16[32,2,128,512]{3,2,1,0:T(8,128)(2,1)}, u32[]{:S(2)}, u32[]{:S(2)}) async-start(bf16[32,2,128,512]{3,2,1,0:T(8,128)(2,1)} %bitcast.18), calls=%async_computation | async-start | bytes 16777216 | tf_op jit(solution)/shard_map/all_to_all | solution.py:284
  32.4 0.0 copy-done.5
  32.4 0.1 multiply_reduce_fusion
  32.6 0.1 broadcast_subtract_fusion.pos_ref
  32.6 187.9 %all-to-all-done = bf16[32,2,128,512]{3,2,1,0:T(8,128)(2,1)} async-done(((bf16[32,2,128,512]{3,2,1,0:T(8,128)(2,1)}), bf16[32,2,128,512]{3,2,1,0:T(8,128)(2,1)}, u32[]{:S(2)}, u32[]{:S(2)}) %all-to-all-start) | async-done | bytes 8388640 | tf_op jit(solution)/shard_map/all_to_all | solution.py:284
  220.5 0.0 copy-done.3
  220.5 1.2 copy-done.1
  221.7 13.2 %shard_map.77 = (f32[8,1,128]{2,1,0:T(1,128)}, bf16[8,64,64,128]{3,2,1,0:T(8,128)(2,1)}) custom-call(s32[64]{0:T(128)S(1)} %multiply_add_fusion.slot_ref, s32[8]{0:T(128)S(1)} %copy-done.3, bf16[8,128,512]{2,1,0:T(8,128)(2,1)S(1)} %bitcast.16, s32[8,1,128]{2,1,0:T(1,128)S(1)} %broadcast_subtract_fusion.pos_ref, ...), custom_call_target="tpu_custom_call" | custom-call | tf_op jit(solution)/shard_map/pallas_call | solution.py:198
  234.9 14.1 %all-to-all-start.1 = ((bf16[256,2,64,128]{3,2,1,0:T(8,128)(2,1)}), bf16[256,2,64,128]{3,2,1,0:T(8,128)(2,1)}, u32[]{:S(2)}, u32[]{:S(2)}) async-start(bf16[256,2,64,128]{3,2,1,0:T(8,128)(2,1)} %bitcast.19), calls=%async_computation.1 | async-start | bytes 16777216 | tf_op jit(solution)/shard_map/all_to_all | solution.py:292
  249.0 0.1 copy.13
  249.1 17.6 %all-gather.1 = s32[8,32,2]{1,2,0:T(2,128)S(1)} all-gather(s32[1,32,2]{1,2,0:T(2,128)S(1)} %bitcast.22), channel_id=2, replica_groups=mesh['dp'=8,'cls'=32] {'dp'}, dimensions={0}, use_global_device_ids=true | all-gather | bytes 2304 | tf_op jit(solution)/shard_map/all_gather | solution.py:293
  266.7 0.1 copy.14
  266.8 0.7 reshape.153.ids_ref
  267.5 1.2 copy-done.2
  268.8 13.1 %shard_map.78 = bf16[8,128,512]{2,1,0:T(8,128)(2,1)} custom-call(s32[64]{0:T(128)S(1)} %multiply_add_fusion.slot_ref, s32[8]{0:T(128)S(1)} %copy-done.3, bf16[8,128,512]{2,1,0:T(8,128)(2,1)S(1)} %bitcast.17, s32[8,1,128]{2,1,0:T(1,128)S(1)} %broadcast_subtract_fusion.pos_ref, ...), custom_call_target="tpu_custom_call" | custom-call | flops 2147483648 | bytes 10485760 | tf_op jit(solution)/shard_map/pallas_call | solution.py:222
  281.9 155.0 %all-to-all-done.1 = bf16[256,2,64,128]{3,2,1,0:T(8,128)(2,1)} async-done(((bf16[256,2,64,128]{3,2,1,0:T(8,128)(2,1)}), bf16[256,2,64,128]{3,2,1,0:T(8,128)(2,1)}, u32[]{:S(2)}, u32[]{:S(2)}) %all-to-all-start.1) | async-done | bytes 8388640 | tf_op jit(solution)/shard_map/all_to_all | solution.py:292
  436.8 8.0 %shard_map.79 = f32[64,3072]{1,0:T(8,128)} custom-call(s32[512]{0:T(512)} %reshape.153.ids_ref, bf16[512,64,128]{2,1,0:T(8,128)(2,1)} %bitcast.11.piece_ref), custom_call_target="tpu_custom_call" | custom-call | tf_op jit(solution)/shard_map/pallas_call | solution.py:258
  (13 shorter events, 0.0 us)
Async XLA Ops:
  0.6 18.9 %copy-start = (bf16[3072,512]{1,0:T(8,128)(2,1)S(1)}, bf16[3072,512]{1,0:T(8,128)(2,1)}, u32[]{:S(2)}) copy-start(bf16[3072,512]{1,0:T(8,128)(2,1)} %param.6) | copy-start | bytes 9437188
  25.1 7.4 %copy-start.5 = (s32[8,8]{1,0:T(8,128)S(1)}, s32[8,8]{1,0:T(8,128)}, u32[]{:S(2)}) copy-start(s32[8,8]{1,0:T(8,128)} %param.7) | copy-start | bytes 772
  25.1 7.5 %copy-start.6 = (s32[1024]{0:T(1024)S(1)}, s32[1024]{0:T(1024)}, u32[]{:S(2)}) copy-start(s32[1024]{0:T(1024)} %param.9) | copy-start | bytes 12292
  25.1 195.4 %copy-start.3 = (s32[8]{0:T(128)S(1)}, s32[8]{0:T(128)}, u32[]{:S(2)}) copy-start(s32[8]{0:T(128)} %count_ref.3) | copy-start | bytes 100
  25.1 195.4 %all-to-all-start = ((bf16[32,2,128,512]{3,2,1,0:T(8,128)(2,1)}), bf16[32,2,128,512]{3,2,1,0:T(8,128)(2,1)}, u32[]{:S(2)}, u32[]{:S(2)}) async-start(bf16[32,2,128,512]{3,2,1,0:T(8,128)(2,1)} %bitcast.18), calls=%async_computation | async-start | bytes 16777216 | tf_op jit(solution)/shard_map/all_to_all | solution.py:284
  220.5 1.2 copy-start.1
  234.9 14.1 %copy-start.4 = (s32[32,2]{1,0:T(8,128)S(1)}, s32[32,2]{1,0:T(8,128)}, u32[]{:S(2)}) copy-start(s32[32,2]{1,0:T(8,128)} %shard_map.76) | copy-start | bytes 772
  234.9 201.9 %all-to-all-start.1 = ((bf16[256,2,64,128]{3,2,1,0:T(8,128)(2,1)}), bf16[256,2,64,128]{3,2,1,0:T(8,128)(2,1)}, u32[]{:S(2)}, u32[]{:S(2)}) async-start(bf16[256,2,64,128]{3,2,1,0:T(8,128)(2,1)} %bitcast.19), calls=%async_computation.1 | async-start | bytes 16777216 | tf_op jit(solution)/shard_map/all_to_all | solution.py:292
  267.5 1.2 copy-start.2

commit v18 on v17

--- a/solution.py
+++ b/solution.py
@@ -247,7 +247,7 @@
     lax.fori_loop(0, chunk, body, 0, unroll=16)
 
 
-def column_sum(got_ids, pieces, tile_dev, chunk=128):
+def column_sum(got_ids, pieces, tile_dev, chunk=256):
     count, width, _ = pieces.shape
     grid_spec = pltpu.PrefetchScalarGridSpec(
         num_scalar_prefetch=1,

time: 445 us -> 445 us (level)
  no operation moved by 1% of the time
where the time goes in v18:
time: 445 us
  waiting for transfers between devices  343 us (77%)
  Pallas kernels  48.3 us (11%)
  starting transfers between devices  21.5 us (5%)
  blocking collectives  17.6 us (4%)
  local copies, waits for them, and re-layouts  10.8 us (2%)
    all_to_all x1, waiting for transfers between devices, per_device(): lax.all_to_all(outgoing, 'cls', split_axis=0, concat_axis=0, tiled=True)  188 us
    all_to_all x1, waiting for transfers between devices, per_device(): lax.all_to_all(pair_grads, ('dp', 'cls'), split_axis=0, concat_axis=0, ti...  155 us
    all_gather x1, blocking collectives, per_device(): got_ids = lax.all_gather(wanted, 'dp').reshape(parts * pair_count)  17.6 us
    pallas_call x1, Pallas kernels, cls_all_to_all(): pl.pallas_call(functools.partial(_a2a_kernel, n), out_shape=jax.ShapeDtyp...  14.3 us
    all_to_all x1, starting transfers between devices, per_device(): lax.all_to_all(pair_grads, ('dp', 'cls'), split_axis=0, concat_axis=0, ti...  14.1 us
    pallas_call x1, Pallas kernels, score_step(): pl.pallas_call(_score_kernel, grid_spec=grid_spec, out_shape=[jax.ShapeDt...  13.1 us
    pallas_call x1, Pallas kernels, embed_step(): pl.pallas_call(_embed_kernel, grid_spec=grid_spec, out_shape=jax.ShapeDty...  13.1 us
  transfers between devices with their start and end apart: 2, of which 2 were waited for; matrix products, arithmetic and copies ran while one was open for 0% of the time, Pallas kernels for 3%

profile of v18, /device:TPU:1, one launch (start us, length us, event | category | flops | bytes accessed | tf_op | source)
XLA Modules:
  0.0 444.8 jit_solution(5860652950402509901)
XLA Ops:
  0.6 0.0 copy-start
  0.6 0.8 sign_compare_fusion
  1.5 0.8 broadcast_remainder_fusion
  2.3 0.1 ne.51
  2.4 0.1 rem.30
  2.5 0.1 div.21
  2.6 0.2 select_reduce_fusion.1
  2.7 0.1 select_reduce_fusion
  2.9 0.8 gather_fusion
  3.7 0.7 reshape.149.src_ref
  4.4 14.3 %shard_map.76 = s32[32,2]{1,0:T(8,128)} custom-call(s32[32,2]{1,0:T(8,128)} %reshape.149.src_ref), custom_call_target="tpu_custom_call" | custom-call | tf_op jit(solution)/shard_map/pallas_call | solution.py:60
  18.7 0.7 compare_select_fusion
  19.4 0.1 reshape.166
  19.5 0.0 copy-done
  19.5 5.5 %gather_fusion.1 = bf16[64,128,512]{2,1,0:T(8,128)(2,1)} fusion(bf16[24,128,512]{2,1,0:T(8,128)(2,1)S(1)} %bitcast.15, s32[1024]{0:T(1024)S(1)} %pad_clamp_fusion), kind=kCustom, calls=%fused_computation.1 | custom fusion | bytes 16777472 | tf_op jit(solution)/shard_map/gather | solution.py:283
  25.1 7.4 %all-to-all-start = ((bf16[32,2,128,512]{3,2,1,0:T(8,128)(2,1)}), bf16[32,2,128,512]{3,2,1,0:T(8,128)(2,1)}, u32[]{:S(2)}, u32[]{:S(2)}) async-start(bf16[32,2,128,512]{3,2,1,0:T(8,128)(2,1)} %bitcast.18), calls=%async_computation | async-start | bytes 16777216 | tf_op jit(solution)/shard_map/all_to_all | solution.py:284
  32.4 0.0 copy-done.5
  32.5 0.1 multiply_reduce_fusion
  32.6 0.0 copy-done.6
  32.6 0.1 broadcast_subtract_fusion.pos_ref
  32.6 188.0 %all-to-all-done = bf16[32,2,128,512]{3,2,1,0:T(8,128)(2,1)} async-done(((bf16[32,2,128,512]{3,2,1,0:T(8,128)(2,1)}), bf16[32,2,128,512]{3,2,1,0:T(8,128)(2,1)}, u32[]{:S(2)}, u32[]{:S(2)}) %all-to-all-start) | async-done | bytes 8388640 | tf_op jit(solution)/shard_map/all_to_all | solution.py:284
  220.6 1.2 copy-done.1
  221.8 13.1 %shard_map.77 = (f32[8,1,128]{2,1,0:T(1,128)}, bf16[8,64,64,128]{3,2,1,0:T(8,128)(2,1)}) custom-call(s32[64]{0:T(128)S(1)} %multiply_add_fusion.slot_ref, s32[8]{0:T(128)S(1)} %copy-done.3, bf16[8,128,512]{2,1,0:T(8,128)(2,1)S(1)} %bitcast.16, s32[8,1,128]{2,1,0:T(1,128)S(1)} %broadcast_subtract_fusion.pos_ref, ...), custom_call_target="tpu_custom_call" | custom-call | tf_op jit(solution)/shard_map/pallas_call | solution.py:198
  235.0 14.1 %all-to-all-start.1 = ((bf16[256,2,64,128]{3,2,1,0:T(8,128)(2,1)}), bf16[256,2,64,128]{3,2,1,0:T(8,128)(2,1)}, u32[]{:S(2)}, u32[]{:S(2)}) async-start(bf16[256,2,64,128]{3,2,1,0:T(8,128)(2,1)} %bitcast.19), calls=%async_computation.1 | async-start | bytes 16777216 | tf_op jit(solution)/shard_map/all_to_all | solution.py:292
  249.2 0.1 copy.13
  249.2 17.6 %all-gather.1 = s32[8,32,2]{1,2,0:T(2,128)S(1)} all-gather(s32[1,32,2]{1,2,0:T(2,128)S(1)} %bitcast.22), channel_id=2, replica_groups=mesh['dp'=8,'cls'=32] {'dp'}, dimensions={0}, use_global_device_ids=true | all-gather | bytes 2304 | tf_op jit(solution)/shard_map/all_gather | solution.py:293
  266.8 0.1 copy.14
  266.9 0.7 reshape.153.ids_ref
  267.7 1.2 copy-done.2
  268.9 13.1 %shard_map.78 = bf16[8,128,512]{2,1,0:T(8,128)(2,1)} custom-call(s32[64]{0:T(128)S(1)} %multiply_add_fusion.slot_ref, s32[8]{0:T(128)S(1)} %copy-done.3, bf16[8,128,512]{2,1,0:T(8,128)(2,1)S(1)} %bitcast.17, s32[8,1,128]{2,1,0:T(1,128)S(1)} %broadcast_subtract_fusion.pos_ref, ...), custom_call_target="tpu_custom_call" | custom-call | flops 2147483648 | bytes 10485760 | tf_op jit(solution)/shard_map/pallas_call | solution.py:222
  282.0 155.0 %all-to-all-done.1 = bf16[256,2,64,128]{3,2,1,0:T(8,128)(2,1)} async-done(((bf16[256,2,64,128]{3,2,1,0:T(8,128)(2,1)}), bf16[256,2,64,128]{3,2,1,0:T(8,128)(2,1)}, u32[]{:S(2)}, u32[]{:S(2)}) %all-to-all-start.1) | async-done | bytes 8388640 | tf_op jit(solution)/shard_map/all_to_all | solution.py:292
  437.0 7.8 %shard_map.79 = f32[64,3072]{1,0:T(8,128)} custom-call(s32[512]{0:T(512)} %reshape.153.ids_ref, bf16[512,64,128]{2,1,0:T(8,128)(2,1)} %bitcast.11.piece_ref), custom_call_target="tpu_custom_call" | custom-call | tf_op jit(solution)/shard_map/pallas_call | solution.py:258
  (13 shorter events, 0.0 us)
Async XLA Ops:
  0.6 18.9 %copy-start = (bf16[3072,512]{1,0:T(8,128)(2,1)S(1)}, bf16[3072,512]{1,0:T(8,128)(2,1)}, u32[]{:S(2)}) copy-start(bf16[3072,512]{1,0:T(8,128)(2,1)} %param.6) | copy-start | bytes 9437188
  25.1 7.4 %copy-start.5 = (s32[8,8]{1,0:T(8,128)S(1)}, s32[8,8]{1,0:T(8,128)}, u32[]{:S(2)}) copy-start(s32[8,8]{1,0:T(8,128)} %param.7) | copy-start | bytes 772
  25.1 7.5 %copy-start.6 = (s32[1024]{0:T(1024)S(1)}, s32[1024]{0:T(1024)}, u32[]{:S(2)}) copy-start(s32[1024]{0:T(1024)} %param.9) | copy-start | bytes 12292
  25.1 195.5 %copy-start.3 = (s32[8]{0:T(128)S(1)}, s32[8]{0:T(128)}, u32[]{:S(2)}) copy-start(s32[8]{0:T(128)} %count_ref.3) | copy-start | bytes 100
  25.1 195.5 %all-to-all-start = ((bf16[32,2,128,512]{3,2,1,0:T(8,128)(2,1)}), bf16[32,2,128,512]{3,2,1,0:T(8,128)(2,1)}, u32[]{:S(2)}, u32[]{:S(2)}) async-start(bf16[32,2,128,512]{3,2,1,0:T(8,128)(2,1)} %bitcast.18), calls=%async_computation | async-start | bytes 16777216 | tf_op jit(solution)/shard_map/all_to_all | solution.py:284
  220.6 1.2 copy-start.1
  235.0 14.2 %copy-start.4 = (s32[32,2]{1,0:T(8,128)S(1)}, s32[32,2]{1,0:T(8,128)}, u32[]{:S(2)}) copy-start(s32[32,2]{1,0:T(8,128)} %shard_map.76) | copy-start | bytes 772
  235.0 202.0 %all-to-all-start.1 = ((bf16[256,2,64,128]{3,2,1,0:T(8,128)(2,1)}), bf16[256,2,64,128]{3,2,1,0:T(8,128)(2,1)}, u32[]{:S(2)}, u32[]{:S(2)}) async-start(bf16[256,2,64,128]{3,2,1,0:T(8,128)(2,1)} %bitcast.19), calls=%async_computation.1 | async-start | bytes 16777216 | tf_op jit(solution)/shard_map/all_to_all | solution.py:292
  267.7 1.2 copy-start.2
